TPU v7x, 128 devices: a whole 4x4x4 slice. The times are simulated.
128 devices in a mesh: box: 128 (over z, y, x, core).
Axes of the slice: x: 4, y: 4, z: 4, core: 2. Of those that a mesh axis runs over, the one named last changes fastest.
Arguments:
- rhs_fine: float32 [512, 512, 512], P('box'), may hold values from -6 to 6
- coef_zero: float32 [512, 512, 512], P('box'), may hold values from 0.5 to 4
- coef_one: float32 [256, 256, 256], P('box'), may hold values from 0.5 to 4
- coef_two: float32 [128, 128, 128], P('box'), may hold values from 0.5 to 4
- coef_three: float32 [64, 64, 64], replicated, may hold values from 0.5 to 4
Outputs:
- smooth_zero: float32 [512, 512, 512], P('box')
- smooth_one: float32 [256, 256, 256], P('box')
- smooth_two: float32 [128, 128, 128], P('box')
- coarse_solution: float32 [64, 64, 64], replicated
All inputs are finite; a program needn't handle non-finite values.
Results may differ from a plain program's by a relative error of at most 0.00002.
Values sent between devices are 32-bit elements; how exact they have to be, the bound alone decides.
No kernel may reach another device: no remote copies, remote signals or barrier semaphores. Data moves between devices by JAX's collectives and lax.ppermute only.
A program may use at most 192 MiB of HBM per device.

v0:
```python
import jax
import jax.numpy as jnp
from jax import lax
from jax.sharding import PartitionSpec as P

CHEB = 16


OMEGA = 0.8
CENTER_VALUE = 1.04
HALF_WIDTH = 0.96
OFFSETS = ((1, 0, 0), (-1, 0, 0), (0, 1, 0), (0, -1, 0), (0, 0, 1), (0, 0, -1))


def with_halo(shard, sides, width):
    for axis, dim in sides:
        size, length = (lax.axis_size(axis), shard.shape[dim])
        up = [(i, (i + 1) % size) for i in range(size - 1)]
        down = [(j, i) for i, j in up]
        last = lax.slice_in_dim(shard, length - width, length, axis=dim)
        initial = lax.slice_in_dim(shard, 0, width, axis=dim)
        before = lax.ppermute(last, axis, up)
        after = lax.ppermute(initial, axis, down)
        shard = jnp.concatenate([before, shard, after], axis=dim)
    return shard


def passed_along(block, axis, distance):
    devices = range(lax.axis_size(axis))
    route = [(i - distance, i) for i in devices if i - distance in devices]
    return lax.ppermute(block, axis, route)


def pad_sides(field):
    return jnp.pad(field, ((0, 0), (1, 1), (1, 1)))


def pad_first(field):
    return jnp.pad(field, ((1, 1), (0, 0), (0, 0)))


def shifted(field, delta_x, delta_y, delta_z):
    return field[
        1 + delta_x : field.shape[0] - 1 + delta_x,
        1 + delta_y : field.shape[1] - 1 + delta_y,
        1 + delta_z : field.shape[2] - 1 + delta_z,
    ]


def face_sum(coef_ext):
    padded = pad_sides(coef_ext)
    centre_coef = shifted(padded, 0, 0, 0)
    total = jnp.zeros_like(centre_coef)
    for offset in OFFSETS:
        total = total + 0.5 * (centre_coef + shifted(padded, *offset))
    return total


def apply_operator(field_ext, coef_ext, diagonal):
    padded_coef = pad_sides(coef_ext)
    padded_field = pad_sides(field_ext)
    centre_coef = shifted(padded_coef, 0, 0, 0)
    beside = jnp.zeros_like(centre_coef)
    for offset in OFFSETS:
        beside = beside + 0.5 * (centre_coef + shifted(padded_coef, *offset)) * shifted(
            padded_field, *offset
        )
    return diagonal * shifted(padded_field, 0, 0, 0) - beside


def restrict_axis(padded, axis, count):
    return (
        0.25 * lax.slice_in_dim(padded, 0, count, 2, axis)
        + 0.5 * lax.slice_in_dim(padded, 1, count + 1, 2, axis)
        + 0.25 * lax.slice_in_dim(padded, 2, count + 1, 2, axis)
    )


def restrict_sides(field):
    for axis in (1, 2):
        count = field.shape[axis]
        front = [(0, 0), (0, 0), (0, 0)]
        front[axis] = (1, 0)
        field = restrict_axis(jnp.pad(field, tuple(front)), axis, count)
    return field


def chebyshev(rhs_coarse, coef_coarse, iterations):
    coef_ext = pad_first(coef_coarse)
    diagonal = face_sum(coef_ext)
    sigma = CENTER_VALUE / HALF_WIDTH
    step_field = rhs_coarse / (CENTER_VALUE * diagonal)
    iterate = step_field
    remains = rhs_coarse - apply_operator(pad_first(step_field), coef_ext, diagonal)
    rho_start = jnp.float32(1.0 / sigma)

    def advance(index, carry):
        iterate, remains, step_field, rho_now = carry
        rho_new = 1.0 / (2.0 * sigma - rho_now)
        step_field = (
            rho_new * rho_now * step_field + 2.0 * rho_new / HALF_WIDTH * remains / diagonal
        )
        iterate = iterate + step_field
        remains = remains - apply_operator(pad_first(step_field), coef_ext, diagonal)
        return (iterate, remains, step_field, rho_new)

    result = lax.fori_loop(0, iterations - 1, advance, (iterate, remains, step_field, rho_start))
    return result[0]


def coef_halo(coef_level):
    return with_halo(coef_level, (("box", 0),), 1)


def face_halo(field):
    return with_halo(field, (("box", 0),), 1)


def smooth_level(rhs_level, coef_ext):
    diagonal = face_sum(coef_ext)
    first_iter = OMEGA * rhs_level / diagonal
    smoothed = (
        first_iter
        + OMEGA * (rhs_level - apply_operator(face_halo(first_iter), coef_ext, diagonal)) / diagonal
    )
    return (smoothed, diagonal)


def upper_level(rhs_level, coef_level):
    planes = rhs_level.shape[0]
    coef_ext = coef_halo(coef_level)
    smoothed, diagonal = smooth_level(rhs_level, coef_ext)
    residual = rhs_level - apply_operator(face_halo(smoothed), coef_ext, diagonal)
    rim_plane = passed_along(residual[planes - 1 :], "box", 1)
    with_rim = jnp.concatenate([rim_plane, residual], axis=0)
    coarse_rhs = 4.0 * restrict_sides(restrict_axis(with_rim, 0, planes))
    return (smoothed, coarse_rhs)


def local(rhs_fine, coef_zero, coef_one, coef_two, coef_three):
    smooth_zero, rhs_next = upper_level(rhs_fine, coef_zero)
    smooth_one, rhs_third = upper_level(rhs_next, coef_one)
    coef_ext = coef_halo(coef_two)
    smooth_two, diagonal = smooth_level(rhs_third, coef_ext)
    residual = rhs_third - apply_operator(face_halo(smooth_two), coef_ext, diagonal)
    in_plane = restrict_sides(residual)
    gathered = lax.all_gather(in_plane, "box", axis=0, tiled=True)
    count = gathered.shape[0]
    rhs_coarse = 4.0 * restrict_axis(jnp.pad(gathered, ((1, 0), (0, 0), (0, 0))), 0, count)
    coarse_solution = chebyshev(rhs_coarse, coef_three, CHEB)
    return (smooth_zero, smooth_one, smooth_two, coarse_solution)


def solution(mesh):
    placed = (
        P("box", None, None),
        P("box", None, None),
        P("box", None, None),
        P("box", None, None),
        P(),
    )
    return jax.shard_map(
        local,
        mesh=mesh,
        in_specs=placed,
        out_specs=(P("box", None, None), P("box", None, None), P("box", None, None), P()),
        check_vma=False,
    )
```

profile of v0, /device:TPU:1, one launch (start us, length us, event | category | flops | bytes accessed | tf_op | source)
XLA Modules:
  0.0 656.2 jit_solution(9558285076958443031)
XLA Ops:
  15.5 10.5 %collective-permute-done = f32[1,512,512]{2,1,0:T(8,128)S(1)} collective-permute-done((f32[1,512,512]{2,1,0:T(8,128)S(1)}, f32[1,512,512]{2,1,0:T(8,128)S(1)}, u32[]{:S(2)}, u32[]{:S(2)}) %collective-permute-start) | collective-permute-done | bytes 1048608 | tf_op jit(solution)/shard_map/ppermute | solution.py:23
  31.6 7.8 %fusion.50 = f32[4,512,512]{2,1,0:T(8,128)} fusion(f32[4,512,512]{2,1,0:T(8,128)} %param.7, f32[4,512,512]{2,1,0:T(8,128)S(1)} %copy-done.8, f32[1,512,512]{2,1,0:T(8,128)S(1)} %collective-permute-done, f32[1,512,512]{2,1,0:T(8,128)S(1)} %collective-permute-done.1, f32[6,514,514]{2,1,0:T(8,128)S(1)} %select_maximum_fusion.4), kind=kLoop, calls=%fused_computation.89 | loop fusion | flops 22020096 | bytes 31457280 | tf_op jit(solution)/shard_map/div | solution.py:121
  47.7 10.5 %collective-permute-done.2 = f32[1,512,512]{2,1,0:T(8,128)S(1)} collective-permute-done((f32[1,512,512]{2,1,0:T(8,128)S(1)}, f32[1,512,512]{2,1,0:T(8,128)S(1)}, u32[]{:S(2)}, u32[]{:S(2)}) %collective-permute-start.2) | collective-permute-done | bytes 1048608 | tf_op jit(solution)/shard_map/ppermute | solution.py:23
  65.2 16.8 %fusion.35 = f32[4,512,512]{2,1,0:T(8,128)} fusion(f32[4,512,512]{2,1,0:T(8,128)} %fusion.50, f32[4,512,512]{2,1,0:T(8,128)} %param.7, f32[6,514,514]{2,1,0:T(8,128)} %select_maximum_fusion.2, f32[1,512,512]{2,1,0:T(8,128)S(1)} %collective-permute-done.3, f32[1,512,512]{2,1,0:T(8,128)S(1)} %collective-permute-done.2, f32[4,512,512]{2,1,0:T(8,128)S(1)} %copy-done.8, ...), kind=kLoop, calls=%fused_computation.62 | loop fusion | flops 39845888 | bytes 54525952 | tf_op jit(solution)/shard_map/add | solution.py:123
  90.8 10.1 %collective-permute-done.4 = f32[1,512,512]{2,1,0:T(8,128)S(1)} collective-permute-done((f32[1,512,512]{2,1,0:T(8,128)S(1)}, f32[1,512,512]{2,1,0:T(8,128)S(1)}, u32[]{:S(2)}, u32[]{:S(2)}) %collective-permute-start.4) | collective-permute-done | bytes 1048608 | tf_op jit(solution)/shard_map/ppermute | solution.py:23
  107.9 16.6 %fusion.23 = f32[4,512,512]{2,1,0:T(8,128)} fusion(f32[4,512,512]{2,1,0:T(8,128)} %param.7, f32[6,514,514]{2,1,0:T(8,128)} %select_maximum_fusion, f32[4,512,512]{2,1,0:T(8,128)} %fusion.35, f32[1,512,512]{2,1,0:T(8,128)S(1)} %collective-permute-done.5, f32[1,512,512]{2,1,0:T(8,128)S(1)} %collective-permute-done.4, f32[4,512,512]{2,1,0:T(8,128)S(1)} %copy-done.8, ...), kind=kLoop, calls=%fused_computation.44 | loop fusion | flops 36700160 | bytes 54525952 | tf_op jit(solution)/shard_map/sub | solution.py:133
  138.2 6.8 %collective-permute-done.8 = f32[1,256,256]{2,1,0:T(8,128)S(1)} collective-permute-done((f32[1,256,256]{2,1,0:T(8,128)S(1)}, f32[1,256,256]{2,1,0:T(8,128)S(1)}, u32[]{:S(2)}, u32[]{:S(2)}) %collective-permute-start.8) | collective-permute-done | bytes 262176 | tf_op jit(solution)/shard_map/ppermute | solution.py:22
  154.5 6.4 slice.522
  160.9 6.5 slice.523
  169.7 23.8 %slice.524 = f32[2,256,256]{2,1,0:T(8,128)} slice(f32[2,256,513]{2,1,0:T(8,128)S(1)} %pad.101), slice={[0:2:1], [0:256:1], [0:512:2]} | slice | bytes 1048576 | tf_op jit(solution)/shard_map/slice | solution.py:73
  193.5 23.8 %slice.525 = f32[2,256,256]{2,1,0:T(8,128)} slice(f32[2,256,513]{2,1,0:T(8,128)S(1)} %pad.101), slice={[0:2:1], [0:256:1], [1:513:2]} | slice | bytes 1048576 | tf_op jit(solution)/shard_map/slice | solution.py:74
  217.3 23.8 %slice.526 = f32[2,256,256]{2,1,0:T(8,128)} slice(f32[2,256,513]{2,1,0:T(8,128)S(1)} %pad.101), slice={[0:2:1], [0:256:1], [2:513:2]} | slice | bytes 1048576 | tf_op jit(solution)/shard_map/slice | solution.py:75
  306.9 114.4 %all-gather.2.cloned.1.call-done = f32[128,64,64]{2,1,0:T(8,128)} async-done(((f32[1,64,64]{2,1,0:T(8,128)}), f32[128,64,64]{2,1,0:T(8,128)}) %all-gather.2.cloned.1.call-update) | async-done | bytes 2097168 | tf_op jit(solution)/shard_map/all_gather | solution.py:147
  421.3 10.0 %slice_add_fusion.4 = (f32[64,64,64]{2,1,0:T(8,128)}, f32[64,64,64]{2,1,0:T(8,128)}, f32[64,64,64]{2,1,0:T(8,128)S(1)}, f32[64,64,64]{2,1,0:T(8,128)S(1)}) fusion(f32[64,64,64]{2,1,0:T(8,128)} %param.11, f32[66,64,64]{2,1,0:T(8,128)S(1)} %pad.113, f32[128,64,64]{2,1,0:T(8,128)} %all-gather.2.cloned.1.call-done), kind=kLoop, calls=%fused_computation.131 | loop fusion | flops 7077888 | bytes 8421376 | tf_op jit(solution)/shard_map/add | solution.py:55
  435.1 7.4 %fusion.65 = f32[64,64,64]{2,1,0:T(8,128)} fusion(f32[66,64,64]{2,1,0:T(8,128)S(1)} %pad.115, f32[64,64,64]{2,1,0:T(8,128)S(1)} %get-tuple-element.212, f32[64,64,64]{2,1,0:T(8,128)S(1)} %copy-done.14, f32[66,64,64]{2,1,0:T(8,128)S(1)} %copy-done.1, f32[128,64,64]{2,1,0:T(8,128)} %all-gather.2.cloned.1.call-done), kind=kLoop, calls=%fused_computation.119 | loop fusion | flops 8912896 | bytes 15859712 | tf_op jit(solution)/shard_map/sub | solution.py:94
  442.5 206.4 %while.18 = (s32[]{:T(128)}, f32[64,64,64]{2,1,0:T(8,128)}, f32[64,64,64]{2,1,0:T(8,128)}, f32[64,64,64]{2,1,0:T(8,128)S(1)}, f32[]{:T(128)}, /*index=5*/f32[64,...) while((s32[]{:T(128)}, f32[64,64,64]{2,1,0:T(8,128)}, ...), condition=%wide.region_1.2_spmd, body=%wide.region_0.1_spmd.sunk | while | flops 7602182 | bytes 55869808 | solution.py:107
  442.6 6.1 fusion.142
  456.3 6.1 fusion.142
  470.1 6.1 fusion.142
  483.8 6.1 fusion.142
  511.4 6.1 fusion.142
  525.1 6.1 fusion.142
  538.9 6.1 fusion.142
  566.4 6.1 fusion.142
  (343 shorter events, 295.2 us)
Async XLA Ops:
  7.2 414.2 %all-gather.2.cloned.1.call-start = ((), (), s32[]{:S(2)}) async-start(), calls=%async_computation | async-start | bytes 4227072 | tf_op jit(solution)/shard_map/all_gather | solution.py:147
  9.1 17.0 %collective-permute-start = (f32[1,512,512]{2,1,0:T(8,128)S(1)}, f32[1,512,512]{2,1,0:T(8,128)S(1)}, u32[]{:S(2)}, u32[]{:S(2)}) collective-permute-start(f32[1,512,512]{2,1,0:T(8,128)S(1)} %get-tuple-element.137), channel_id=1, source_target_pairs={{1,0},{2,1},{3,2},{4,3},{5,4},{6,5},{7,6},{8,7},{9,8},{10,9},{11,1... | collective-permute-start | bytes 3145736 | tf_op jit(solution)/shard_map/ppermute | solution.py:23
  12.4 14.8 %collective-permute-start.1 = (f32[1,512,512]{2,1,0:T(8,128)S(1)}, f32[1,512,512]{2,1,0:T(8,128)S(1)}, u32[]{:S(2)}, u32[]{:S(2)}) collective-permute-start(f32[1,512,512]{2,1,0:T(8,128)S(1)} %get-tuple-element.136), channel_id=1, source_target_pairs={{0,1},{1,2},{2,3},{3,4},{4,5},{5,6},{6,7},{7,8},{8,9},{9,10},{10,1... | collective-permute-start | bytes 3145736 | tf_op jit(solution)/shard_map/ppermute | solution.py:22
  41.3 17.0 %collective-permute-start.2 = (f32[1,512,512]{2,1,0:T(8,128)S(1)}, f32[1,512,512]{2,1,0:T(8,128)S(1)}, u32[]{:S(2)}, u32[]{:S(2)}) collective-permute-start(f32[1,512,512]{2,1,0:T(8,128)S(1)} %get-tuple-element.135), channel_id=1, source_target_pairs={{1,0},{2,1},{3,2},{4,3},{5,4},{6,5},{7,6},{8,7},{9,8},{10,9},{11,1... | collective-permute-start | bytes 3145736 | tf_op jit(solution)/shard_map/ppermute | solution.py:23
  43.3 16.1 %collective-permute-start.3 = (f32[1,512,512]{2,1,0:T(8,128)S(1)}, f32[1,512,512]{2,1,0:T(8,128)S(1)}, u32[]{:S(2)}, u32[]{:S(2)}) collective-permute-start(f32[1,512,512]{2,1,0:T(8,128)S(1)} %get-tuple-element.134), channel_id=1, source_target_pairs={{0,1},{1,2},{2,3},{3,4},{4,5},{5,6},{6,7},{7,8},{8,9},{9,10},{10,1... | collective-permute-start | bytes 3145736 | tf_op jit(solution)/shard_map/ppermute | solution.py:22
  83.9 17.0 %collective-permute-start.4 = (f32[1,512,512]{2,1,0:T(8,128)S(1)}, f32[1,512,512]{2,1,0:T(8,128)S(1)}, u32[]{:S(2)}, u32[]{:S(2)}) collective-permute-start(f32[1,512,512]{2,1,0:T(8,128)S(1)} %get-tuple-element.133), channel_id=1, source_target_pairs={{1,0},{2,1},{3,2},{4,3},{5,4},{6,5},{7,6},{8,7},{9,8},{10,9},{11,1... | collective-permute-start | bytes 3145736 | tf_op jit(solution)/shard_map/ppermute | solution.py:23
  85.9 16.1 %collective-permute-start.5 = (f32[1,512,512]{2,1,0:T(8,128)S(1)}, f32[1,512,512]{2,1,0:T(8,128)S(1)}, u32[]{:S(2)}, u32[]{:S(2)}) collective-permute-start(f32[1,512,512]{2,1,0:T(8,128)S(1)} %get-tuple-element.132), channel_id=1, source_target_pairs={{0,1},{1,2},{2,3},{3,4},{4,5},{5,6},{6,7},{7,8},{8,9},{9,10},{10,1... | collective-permute-start | bytes 3145736 | tf_op jit(solution)/shard_map/ppermute | solution.py:22
  107.9 22.6 %copy-start.15 = (f32[2,256,256]{2,1,0:T(8,128)S(1)}, f32[2,256,256]{2,1,0:T(8,128)}, u32[]{:S(2)}) copy-start(f32[2,256,256]{2,1,0:T(8,128)} %param.9) | copy-start | bytes 1572868
  125.9 19.8 %collective-permute-start.6 = (f32[1,512,512]{2,1,0:T(8,128)S(1)}, f32[1,512,512]{2,1,0:T(8,128)S(1)}, u32[]{:S(2)}, u32[]{:S(2)}) collective-permute-start(f32[1,512,512]{2,1,0:T(8,128)S(1)} %slice.608), channel_id=1, source_target_pairs={{0,1},{1,2},{2,3},{3,4},{4,5},{5,6},{6,7},{7,8},{8,9},{9,10},{10,1... | collective-permute-start | bytes 3145736 | tf_op jit(solution)/shard_map/ppermute | solution.py:31
  130.5 7.7 %collective-permute-start.7 = (f32[1,256,256]{2,1,0:T(8,128)S(1)}, f32[1,256,256]{2,1,0:T(8,128)S(1)}, u32[]{:S(2)}, u32[]{:S(2)}) collective-permute-start(f32[1,256,256]{2,1,0:T(8,128)S(1)} %get-tuple-element.147), channel_id=1, source_target_pairs={{1,0},{2,1},{3,2},{4,3},{5,4},{6,5},{7,6},{8,7},{9,8},{10,9},{11,1... | collective-permute-start | bytes 786440 | tf_op jit(solution)/shard_map/ppermute | solution.py:23
  132.4 12.5 %collective-permute-start.8 = (f32[1,256,256]{2,1,0:T(8,128)S(1)}, f32[1,256,256]{2,1,0:T(8,128)S(1)}, u32[]{:S(2)}, u32[]{:S(2)}) collective-permute-start(f32[1,256,256]{2,1,0:T(8,128)S(1)} %get-tuple-element.146), channel_id=1, source_target_pairs={{0,1},{1,2},{2,3},{3,4},{4,5},{5,6},{6,7},{7,8},{8,9},{9,10},{10,1... | collective-permute-start | bytes 786440 | tf_op jit(solution)/shard_map/ppermute | solution.py:22
  169.7 71.4 %copy-start.16 = (f32[2,256,256]{2,1,0:T(8,128)S(1)}, f32[2,256,256]{2,1,0:T(8,128)}, u32[]{:S(2)}) copy-start(f32[2,256,256]{2,1,0:T(8,128)} %param.9) | copy-start | bytes 1572868
  243.3 7.8 %collective-permute-start.10 = (f32[1,256,256]{2,1,0:T(8,128)S(1)}, f32[1,256,256]{2,1,0:T(8,128)S(1)}, u32[]{:S(2)}, u32[]{:S(2)}) collective-permute-start(f32[1,256,256]{2,1,0:T(8,128)S(1)} %get-tuple-element.144), channel_id=1, source_target_pairs={{0,1},{1,2},{2,3},{3,4},{4,5},{5,6},{6,7},{7,8},{8,9},{9,10},{10,1... | collective-permute-start | bytes 786440 | tf_op jit(solution)/shard_map/ppermute | solution.py:22
  247.8 7.7 %collective-permute-start.9 = (f32[1,256,256]{2,1,0:T(8,128)S(1)}, f32[1,256,256]{2,1,0:T(8,128)S(1)}, u32[]{:S(2)}, u32[]{:S(2)}) collective-permute-start(f32[1,256,256]{2,1,0:T(8,128)S(1)} %get-tuple-element.145), channel_id=1, source_target_pairs={{1,0},{2,1},{3,2},{4,3},{5,4},{6,5},{7,6},{8,7},{9,8},{10,9},{11,1... | collective-permute-start | bytes 786440 | tf_op jit(solution)/shard_map/ppermute | solution.py:23
  257.3 7.7 %collective-permute-start.11 = (f32[1,256,256]{2,1,0:T(8,128)S(1)}, f32[1,256,256]{2,1,0:T(8,128)S(1)}, u32[]{:S(2)}, u32[]{:S(2)}) collective-permute-start(f32[1,256,256]{2,1,0:T(8,128)S(1)} %get-tuple-element.143), channel_id=1, source_target_pairs={{1,0},{2,1},{3,2},{4,3},{5,4},{6,5},{7,6},{8,7},{9,8},{10,9},{11,1... | collective-permute-start | bytes 786440 | tf_op jit(solution)/shard_map/ppermute | solution.py:23
  259.2 6.9 %collective-permute-start.12 = (f32[1,256,256]{2,1,0:T(8,128)S(1)}, f32[1,256,256]{2,1,0:T(8,128)S(1)}, u32[]{:S(2)}, u32[]{:S(2)}) collective-permute-start(f32[1,256,256]{2,1,0:T(8,128)S(1)} %get-tuple-element.142), channel_id=1, source_target_pairs={{0,1},{1,2},{2,3},{3,4},{4,5},{5,6},{6,7},{7,8},{8,9},{9,10},{10,1... | collective-permute-start | bytes 786440 | tf_op jit(solution)/shard_map/ppermute | solution.py:22
  267.8 11.5 %collective-permute-start.13 = (f32[1,256,256]{2,1,0:T(8,128)S(1)}, f32[1,256,256]{2,1,0:T(8,128)S(1)}, u32[]{:S(2)}, u32[]{:S(2)}) collective-permute-start(f32[1,256,256]{2,1,0:T(8,128)S(1)} %slice.625), channel_id=1, source_target_pairs={{0,1},{1,2},{2,3},{3,4},{4,5},{5,6},{6,7},{7,8},{8,9},{9,10},{10,1... | collective-permute-start | bytes 786440 | tf_op jit(solution)/shard_map/ppermute | solution.py:31
  272.2 5.6 collective-permute-start.14
  274.1 5.0 collective-permute-start.15
  286.7 6.2 collective-permute-start.16
  288.6 5.6 collective-permute-start.17
  294.6 6.5 collective-permute-start.18
  296.5 5.6 collective-permute-start.19
  306.9 124.4 %copy-start = (f32[66,64,64]{2,1,0:T(8,128)}, f32[66,64,64]{2,1,0:T(8,128)S(1)}, u32[]{:S(2)}) copy-start(f32[66,64,64]{2,1,0:T(8,128)S(1)} %pad.113) | copy-start | bytes 3244036
  (105 other events, 514.2 us)
Sparse Core Ops, SparseCore 0:
  305.2 116.0 all-gather.1
where the time goes:
time: 664 us; the launch traced here: 656 us
  other arithmetic  238 us (36%)
  waiting for transfers between devices  171 us (26%)
  local copies, waits for them, and re-layouts  166 us (25%)
  starting transfers between devices  64.7 us (10%)
  between operations  15.1 us (2%)
    all_gather x1, waiting for transfers between devices, local(): gathered = lax.all_gather(in_plane, 'box', axis=0, tiled=True)  114 us
    add x15, other arithmetic, advance(): iterate = iterate + step_field  91.6 us
    sub x15, other arithmetic, advance(): remains - apply_operator(pad_first(step_field), coef_ext, diagonal)  60.6 us
    while x180, local copies, waits for them, and re-layouts  49.8 us
    ppermute x9, waiting for transfers between devices, with_halo(): after = lax.ppermute(initial, axis, down)  39.8 us
    ppermute x9, starting transfers between devices, with_halo(): before = lax.ppermute(last, axis, up)  36.6 us
    slice x6, local copies, waits for them, and re-layouts, restrict_axis(): lax.slice_in_dim(padded, 2, count + 1, 2, axis)  33.2 us
    slice x6, local copies, waits for them, and re-layouts, restrict_axis(): lax.slice_in_dim(padded, 1, count + 1, 2, axis)  33.2 us
  transfers between devices with their start and end apart: 21, of which 16 were waited for; matrix products, arithmetic and copies ran while one was open for 0% of the time, Pallas kernels for 0%

commit v1 on v0

v1 whole, which is shorter than its diff:
```python
import jax
import jax.numpy as jnp
import numpy as np
from jax import lax
from jax.experimental import pallas as pl
from jax.experimental.pallas import tpu as pltpu
from jax.sharding import PartitionSpec as P

CHEB = 16
OMEGA = 0.8
CENTER_VALUE = 1.04
HALF_WIDTH = 0.96
ROWS = 8
PAD = 8
LANES = 128
F32 = jnp.float32
BF16 = jnp.bfloat16


def restriction_matrix(fine, coarse_lanes, shift):
    weights = np.zeros((fine, coarse_lanes), np.float32)
    for k in range(fine // 2):
        weights[2 * k, k + shift] = 0.5
        weights[2 * k + 1, k + shift] = 0.25
        if k > 0:
            weights[2 * k - 1, k + shift] = 0.25
    return weights


def shape(*dims):
    return jax.ShapeDtypeStruct(dims, F32)


def call(body, outs, scratch, copies, flops, moved, megabytes, aliases=None):
    sems = [pltpu.SemaphoreType.DMA((copies,))]

    def run(scalars, *arrays):
        return pl.pallas_call(
            body,
            out_shape=outs,
            in_specs=[pl.BlockSpec(memory_space=pltpu.SMEM)]
            + [pl.BlockSpec(memory_space=pl.ANY)] * len(arrays),
            out_specs=[pl.BlockSpec(memory_space=pl.ANY)] * len(outs),
            scratch_shapes=scratch + sems,
            input_output_aliases=aliases or {},
            compiler_params=pltpu.CompilerParams(vmem_limit_bytes=megabytes << 20),
            cost_estimate=pl.CostEstimate(flops=flops, bytes_accessed=moved, transcendentals=0),
        )(scalars, *arrays)

    return run


class Copies:
    def __init__(self, sems):
        self.sems = sems
        self.used = 0

    def start(self, source, target):
        copy = pltpu.make_async_copy(source, target, self.sems.at[self.used])
        self.used += 1
        copy.start()
        return copy

    def choose(self, first_if, source, other, target):
        copy = pltpu.make_async_copy(source, target, self.sems.at[self.used])
        swap = pltpu.make_async_copy(other, target, self.sems.at[self.used])
        self.used += 1

        @pl.when(first_if)
        def _():
            copy.start()

        @pl.when(jnp.logical_not(first_if))
        def _():
            swap.start()

        return copy


def clear_pads(ref, size):
    planes, _, lanes = ref.shape
    zeros = jnp.zeros((planes, PAD, lanes), F32)
    ref[:, :PAD, :] = zeros
    ref[:, PAD + size :, :] = zeros


def inner(ref, plane, size):
    return ref.at[plane, pl.ds(PAD, size), :]


def at_rows(ref, plane, row, offset=0):
    return ref[plane, pl.ds(PAD + row + offset, ROWS), :]


def in_plane(ref, plane, row):
    centre = at_rows(ref, plane, row)
    lanes = centre.shape[1]
    lane = lax.broadcasted_iota(jnp.int32, centre.shape, 1)
    left = jnp.where(lane == 0, 0.0, pltpu.roll(centre, 1, 1))
    right = jnp.where(lane == lanes - 1, 0.0, pltpu.roll(centre, lanes - 1, 1))
    tall = ref[plane, pl.ds(PAD + row - 8, ROWS + 16), :]
    return centre, [tall[9 : 9 + ROWS], tall[7 : 7 + ROWS], left, right]


def around(ref, plane, row, sides):
    centre, beside = in_plane(ref, plane, row)
    return centre, beside + [at_rows(ref, plane + side, row) for side in sides]


def total(values):
    result = values[0]
    for value in values[1:]:
        result = result + value
    return result


def sweep(size, body):
    def step(index, carry):
        body(pl.multiple_of(index * ROWS, ROWS))
        return carry

    lax.fori_loop(0, size // ROWS, step, 0, unroll=2)


def faces(coef, coef_beside, field_beside):
    return total([(coef + c) * v for c, v in zip(coef_beside, field_beside)])


def put_tiles(tiles, plane, row, value):
    for tile in range(tiles.shape[1]):
        tiles[plane, tile, pl.ds(PAD + row, ROWS), :] = value[:, tile * LANES : (tile + 1) * LANES]


def clear_top(tiles):
    tiles[:, :, :PAD, :] = jnp.zeros((tiles.shape[0], tiles.shape[1], PAD, LANES), F32)


def thin_rows(tiles, plane, start, count):
    parts = []
    for tile in range(tiles.shape[1]):
        parts.append(
            0.25 * tiles[plane, tile, pl.ds(PAD - 1 + start, count, stride=2), :]
            + 0.5 * tiles[plane, tile, pl.ds(PAD + start, count, stride=2), :]
            + 0.25 * tiles[plane, tile, pl.ds(PAD + 1 + start, count, stride=2), :]
        )
    return jnp.concatenate(parts, axis=1)


def restrict_plane(tiles, plane, size, matrix):
    return project(thin_rows(tiles, plane, 0, size // 2), matrix)


def project(rows, matrix):
    high = rows.astype(BF16)
    rest = rows - high.astype(F32)
    middle = rest.astype(BF16)
    low = (rest - middle.astype(F32)).astype(BF16)
    return (
        jnp.dot(low, matrix, preferred_element_type=F32)
        + jnp.dot(middle, matrix, preferred_element_type=F32)
        + jnp.dot(high, matrix, preferred_element_type=F32)
    )


def plane_at(core, place):
    return place + core * (3 - 2 * place)


def first_inner(scalars, coef, rhs, first, partial, c, b, f, g, sems):
    core = scalars[0]
    size = coef.shape[1]
    go = Copies(sems)
    waits = [go.start(coef.at[plane_at(core, q)], inner(c, q, size)) for q in range(4)]
    more = [go.start(rhs.at[plane_at(core, q)], b.at[q - 1]) for q in (1, 2)]
    clear_pads(c, size)
    for copy in waits + more:
        copy.wait()
    out = []
    for slot, q, sides in ((0, 0, (1,)), (1, 3, (-1,))):

        def partial_rows(row):
            centre, beside = around(c, q, row, sides)
            g[slot, pl.ds(row, ROWS), :] = 3.0 * centre + 0.5 * total(beside)

        sweep(size, partial_rows)
        out.append(go.start(g.at[slot], partial.at[slot]))
    for q in (1, 2):

        def first_rows(row):
            centre, beside = around(c, q, row, (-1, 1))
            diagonal = 3.0 * centre + 0.5 * total(beside)
            f[q - 1, pl.ds(row, ROWS), :] = OMEGA * b[q - 1, pl.ds(row, ROWS), :] / diagonal

        sweep(size, first_rows)
        out.append(go.start(f.at[q - 1], first.at[q - 1]))
    for copy in out:
        copy.wait()


def first_rim(scalars, rhs, partial, coef_outer, coef_sibling, outer, sibling, b, g, h, f, sems):
    core = scalars[0]
    size = rhs.shape[1]
    go = Copies(sems)
    loads = []
    for slot, q, halo in ((0, 0, coef_outer), (1, 3, coef_sibling)):
        loads.append(
            [
                go.start(rhs.at[plane_at(core, q)], b.at[slot]),
                go.start(partial.at[slot], g.at[slot]),
                go.start(halo, h.at[slot]),
            ]
        )
    out = []
    for slot, target in ((0, outer), (1, sibling)):
        for copy in loads[slot]:
            copy.wait()

        def rows(row):
            part = pl.ds(row, ROWS)
            diagonal = g[slot, part, :] + 0.5 * h[slot, part, :]
            f[slot, part, :] = OMEGA * b[slot, part, :] / diagonal

        sweep(size, rows)
        out.append(go.start(f.at[slot], target))
    for copy in out:
        copy.wait()


def smooth_inner(
    scalars, coef, rhs, coef_outer, coef_sibling, first, first_outer, first_sibling,
    smooth, known, factor, c, v, b, s, g, h, sems,
):
    core = scalars[0]
    size = coef.shape[1]
    go = Copies(sems)
    c_loads = [go.start(coef_outer, inner(c, 0, size))]
    c_loads += [go.start(coef.at[plane_at(core, q)], inner(c, q + 1, size)) for q in range(4)]
    c_loads.append(go.start(coef_sibling, inner(c, 5, size)))
    sources = (first_outer, first.at[0], first.at[1], first_sibling)
    v_loads = [go.start(source, inner(v, q + 1, size)) for q, source in enumerate(sources)]
    b_loads = [go.start(rhs.at[plane_at(core, q)], b.at[q]) for q in range(4)]
    clear_pads(c, size)
    clear_pads(v, size)
    for copy in c_loads + v_loads + b_loads:
        copy.wait()
    out = []
    for slot, q, side in ((0, 1, 1), (1, 4, -1)):

        def rim_rows(row):
            part = pl.ds(row, ROWS)
            coef_here, coef_beside = around(c, q, row, (side,))
            here, beside = around(v, q, row, (side,))
            halo = at_rows(c, q - side, row)
            diagonal = 3.0 * coef_here + 0.5 * (total(coef_beside) + halo)
            scale = OMEGA / diagonal
            applied = diagonal * here - 0.5 * faces(coef_here, coef_beside, beside)
            g[slot, part, :] = here + scale * (b[q - 1, part, :] - applied)
            h[slot, part, :] = 0.5 * scale * (coef_here + halo)

        sweep(size, rim_rows)
        out.append(go.start(g.at[slot], known.at[slot]))
        out.append(go.start(h.at[slot], factor.at[slot]))
    for q in (2, 3):

        def rows(row):
            part = pl.ds(row, ROWS)
            coef_here, coef_beside = around(c, q, row, (-1, 1))
            here, beside = around(v, q, row, (-1, 1))
            diagonal = 3.0 * coef_here + 0.5 * total(coef_beside)
            applied = diagonal * here - 0.5 * faces(coef_here, coef_beside, beside)
            s[q - 2, part, :] = here + OMEGA * (b[q - 1, part, :] - applied) / diagonal

        sweep(size, rows)
        out.append(go.start(s.at[q - 2], smooth.at[plane_at(core, q - 1)]))
    for copy in out:
        copy.wait()


def smooth_rim(
    scalars, started, known, factor, halo_outer, halo_sibling,
    smooth, outer, sibling, g, h, v, s, sems,
):
    core = scalars[0]
    size = known.shape[1]
    go = Copies(sems)
    loads = []
    for slot, halo in ((0, halo_outer), (1, halo_sibling)):
        loads.append(
            [
                go.start(known.at[slot], g.at[slot]),
                go.start(factor.at[slot], h.at[slot]),
                go.start(halo, v.at[slot]),
            ]
        )
    out = []
    for slot, q, target in ((0, 0, outer), (1, 3, sibling)):
        for copy in loads[slot]:
            copy.wait()

        def rows(row):
            part = pl.ds(row, ROWS)
            s[slot, part, :] = g[slot, part, :] + h[slot, part, :] * v[slot, part, :]

        sweep(size, rows)
        out.append(go.start(s.at[slot], target))
        out.append(go.start(s.at[slot], smooth.at[plane_at(core, q)]))
    for copy in out:
        copy.wait()


def residual_inner(
    scalars, coef, rhs, coef_outer, coef_sibling, smooth, smooth_outer, smooth_sibling, matrix,
    lowered, known, factor, c, v, b, g, h, t, low, mat, sems,
):
    core = scalars[0]
    size = coef.shape[1]
    go = Copies(sems)
    loads = [go.start(coef_outer, inner(c, 0, size))]
    loads += [go.start(coef.at[plane_at(core, q)], inner(c, q + 1, size)) for q in range(4)]
    loads.append(go.start(coef_sibling, inner(c, 5, size)))
    sources = (
        smooth_outer, smooth.at[plane_at(core, 1)], smooth.at[plane_at(core, 2)], smooth_sibling,
    )
    loads += [go.start(source, inner(v, q + 1, size)) for q, source in enumerate(sources)]
    loads += [go.start(rhs.at[plane_at(core, q)], b.at[q]) for q in range(4)]
    loads.append(go.start(matrix, mat))
    clear_pads(c, size)
    clear_pads(v, size)
    clear_top(t)
    for copy in loads:
        copy.wait()
    out = []
    for slot, q, side in ((0, 1, 1), (1, 4, -1)):

        def rim_rows(row):
            part = pl.ds(row, ROWS)
            coef_here, coef_beside = around(c, q, row, (side,))
            here, beside = around(v, q, row, (side,))
            halo = at_rows(c, q - side, row)
            diagonal = 3.0 * coef_here + 0.5 * (total(coef_beside) + halo)
            applied = diagonal * here - 0.5 * faces(coef_here, coef_beside, beside)
            g[slot, part, :] = b[q - 1, part, :] - applied
            h[slot, part, :] = 0.5 * (coef_here + halo)

        sweep(size, rim_rows)
        out.append(go.start(g.at[slot], known.at[slot]))
        out.append(go.start(h.at[slot], factor.at[slot]))
    for q in (2, 3):

        def rows(row):
            part = pl.ds(row, ROWS)
            coef_here, coef_beside = around(c, q, row, (-1, 1))
            here, beside = around(v, q, row, (-1, 1))
            diagonal = 3.0 * coef_here + 0.5 * total(coef_beside)
            applied = diagonal * here - 0.5 * faces(coef_here, coef_beside, beside)
            put_tiles(t, q - 2, row, b[q - 1, part, :] - applied)

        sweep(size, rows)
        low[q - 2] = restrict_plane(t, q - 2, size, mat[...])
    out.append(go.start(low, lowered))
    for copy in out:
        copy.wait()


def residual_rim(
    scalars, known, factor, halo_outer, halo_sibling, lowered, matrix,
    packed, g, h, v, t, low, pack, mat, sems,
):
    core = scalars[0]
    size = known.shape[1]
    go = Copies(sems)
    loads = []
    for slot, halo in ((0, halo_outer), (1, halo_sibling)):
        loads.append(
            [
                go.start(known.at[slot], g.at[slot]),
                go.start(factor.at[slot], h.at[slot]),
                go.start(halo, v.at[slot]),
            ]
        )
    more = [go.start(lowered, low.at[pl.ds(1, 2)]), go.start(matrix, mat)]
    clear_top(t)
    for copy in more:
        copy.wait()
    for slot in (0, 1):
        for copy in loads[slot]:
            copy.wait()

        def rows(row):
            part = pl.ds(row, ROWS)
            put_tiles(t, slot, row, g[slot, part, :] + h[slot, part, :] * v[slot, part, :])

        sweep(size, rows)
        low[3 * slot] = restrict_plane(t, slot, size, mat[...])
    one = plane_at(core, 1)
    two = plane_at(core, 2)
    last = low[plane_at(core, 3)]
    pack[0] = 2.0 * low[plane_at(core, 0)] + low[one]
    pack[1] = low[one] + 2.0 * low[two] + last
    pack[2] = last
    copy = go.start(pack, packed)
    copy.wait()


def guarded(diagonal):
    return jnp.where(diagonal == 0.0, 1.0, diagonal)


def first_wide(c, b, f, planes, size):
    for q in range(planes):

        def rows(row):
            centre, beside = around(c, q + 1, row, (-1, 1))
            diagonal = guarded(3.0 * centre + 0.5 * total(beside))
            f[q, pl.ds(PAD + row, ROWS), :] = OMEGA * b[q, pl.ds(row, ROWS), :] / diagonal

        sweep(size, rows)


def smooth_wide(c, b, f, s, planes, size, inside):
    for q in range(planes):

        def rows(row):
            coef_here, coef_beside = around(c, q + 2, row, (-1, 1))
            here, beside = around(f, q + 1, row, (-1, 1))
            diagonal = guarded(3.0 * coef_here + 0.5 * total(coef_beside))
            applied = diagonal * here - 0.5 * faces(coef_here, coef_beside, beside)
            value = here + OMEGA * (b[q + 1, pl.ds(row, ROWS), :] - applied) / diagonal
            if inside[q] is not None:
                value = jnp.where(inside[q], value, 0.0)
            s[q, pl.ds(PAD + row, ROWS), :] = value

        sweep(size, rows)


def residual_wide(c, b, s, t, planes, size):
    for q in range(planes):

        def rows(row):
            coef_here, coef_beside = around(c, q + 3, row, (-1, 1))
            here, beside = around(s, q + 1, row, (-1, 1))
            diagonal = 3.0 * coef_here + 0.5 * total(coef_beside)
            applied = diagonal * here - 0.5 * faces(coef_here, coef_beside, beside)
            put_tiles(t, q, row, b[q + 2, pl.ds(row, ROWS), :] - applied)

        sweep(size, rows)


def middle_level(
    scalars, own, sibling, outer, before, coef, coef_sibling, coef_outer, coef_before, coef_after,
    matrix, smooth, packed, m, b, c, f, s, t, pack, mat, sems,
):
    core = scalars[0]
    place = scalars[1]
    final = scalars[2]
    size = coef.shape[1]
    even = core == 0
    go = Copies(sems)
    loads = [
        go.start(own, m.at[pl.ds(3, 3)]),
        go.choose(even, outer, sibling, m.at[pl.ds(0, 3)]),
        go.choose(even, sibling, outer, m.at[pl.ds(6, 3)]),
        go.start(before, m.at[9]),
        go.start(coef_before.at[pl.ds(0, size)], inner(c, 0, size)),
        go.start(coef_after.at[pl.ds(0, size)], inner(c, 7, size)),
        go.start(matrix, mat),
    ]
    for q in range(2):
        part = pl.ds(q * size, size)
        loads.append(go.choose(even, coef_outer.at[part], coef_sibling.at[part], inner(c, 1 + q, size)))
        loads.append(go.start(coef.at[q], inner(c, 3 + q, size)))
        loads.append(go.choose(even, coef_sibling.at[part], coef_outer.at[part], inner(c, 5 + q, size)))
    clear_pads(c, size)
    clear_pads(f, size)
    clear_pads(s, size)
    clear_top(t)
    for copy in loads:
        copy.wait()

    def rows(row):
        part = pl.ds(row, ROWS)
        b[0, part, :] = m[0, part, :] + m[9, part, :]
        b[1, part, :] = m[1, part, :]
        b[2, part, :] = m[3, part, :] + m[2, part, :]
        b[3, part, :] = m[4, part, :]
        b[4, part, :] = jnp.where(place < final, m[6, part, :] + m[5, part, :], 0.0)
        b[5, part, :] = m[7, part, :]

    sweep(size, rows)
    first_wide(c, b, f, 6, size)
    smooth_wide(c, b, f, s, 4, size, (place > 0, None, None, place < final))
    out = [go.start(inner(s, 1 + q, size), smooth.at[q]) for q in range(2)]
    residual_wide(c, b, s, t, 2, size)
    low = restrict_plane(t, 1, size, mat[...])
    pack[0] = 2.0 * restrict_plane(t, 0, size, mat[...]) + low
    pack[1] = low
    out.append(go.start(pack, packed))
    for copy in out:
        copy.wait()


def last_level(
    scalars, own, sibling, outer, before, after, rim, coef, coef_sibling, coef_outer, coef_before,
    coef_after, matrices, smooth, copies, m, b, c, f, s, t, w, mat, sems,
):
    core = scalars[0]
    place = scalars[1]
    final = scalars[2]
    size = coef.shape[1]
    half = size // 2
    base = 4 * size
    even = core == 0
    go = Copies(sems)
    loads = [
        go.start(before, m.at[pl.ds(0, 2)]),
        go.choose(even, outer, sibling, m.at[pl.ds(2, 2)]),
        go.start(own, m.at[pl.ds(4, 2)]),
        go.choose(even, sibling, outer, m.at[pl.ds(6, 2)]),
        go.start(after, m.at[pl.ds(8, 2)]),
        go.start(rim, m.at[10]),
        go.start(coef.at[0], inner(c, 3, size)),
        go.start(matrices, mat),
    ]
    for part in range(2):
        target = pl.ds(PAD + part * half, half)
        lanes = pl.ds(part * size, size)
        outer_part = coef_outer.at[pl.ds(base, half), lanes]
        sibling_part = coef_sibling.at[pl.ds(base, half), lanes]
        loads.append(go.choose(even, outer_part, sibling_part, c.at[2, target, :]))
        loads.append(go.choose(even, sibling_part, outer_part, c.at[4, target, :]))
        for source, nearer, farther in ((coef_before, 1, 0), (coef_after, 5, 6)):
            loads.append(go.start(source.at[pl.ds(2 * size, half), lanes], c.at[nearer, target, :]))
            loads.append(
                go.start(source.at[pl.ds(2 * size + half, half), lanes], c.at[farther, target, :])
            )
    clear_pads(c, size)
    clear_pads(f, size)
    clear_pads(s, size)
    clear_top(t)
    for copy in loads:
        copy.wait()

    def rows(row):
        part = pl.ds(row, ROWS)
        b[0, part, :] = m[0, part, :] + m[10, part, :]
        b[1, part, :] = m[2, part, :] + m[1, part, :]
        b[2, part, :] = m[4, part, :] + m[3, part, :]
        b[3, part, :] = jnp.where(place < final, m[6, part, :] + m[5, part, :], 0.0)
        b[4, part, :] = jnp.where(place < final - 1, m[8, part, :] + m[7, part, :], 0.0)

    sweep(size, rows)
    first_wide(c, b, f, 5, size)
    smooth_wide(c, b, f, s, 3, size, (place > 0, None, place < final))
    out = [go.start(inner(s, 1, size), smooth.at[0])]
    residual_wide(c, b, s, t, 1, size)
    top = thin_rows(t, 0, 0, size // 4)
    bottom = thin_rows(t, 0, half, size // 4)
    result = project(top, mat[0]) + project(bottom, mat[1])
    w[...] = jnp.broadcast_to(result[None], w.shape)
    out.append(go.start(w, copies))
    for copy in out:
        copy.wait()


def coarse_level(scalars, own, sibling, coef, solution, e, o, c, w, p, g, x, y, sems):
    core = scalars[0]
    even = core == 0
    half, size, lanes = coef.shape
    go = Copies(sems)
    loads = [
        go.start(coef, c.at[pl.ds(1, half)]),
        go.choose(even, own, sibling, e),
        go.choose(even, sibling, own, o.at[pl.ds(1, 2 * half)]),
    ]
    o[0] = jnp.zeros(o.shape[1:], F32)
    loads[0].wait()
    lane = lax.broadcasted_iota(jnp.int32, (size, lanes), 1)
    row = lax.broadcasted_iota(jnp.int32, (size, lanes), 0)
    upper = lane >= size
    low_edge = (lane % size) == 0
    high_edge = (lane % size) == size - 1
    c[0] = jnp.where(upper, pltpu.roll(c[half], size, 1), 0.0)
    c[half + 1] = jnp.where(upper, 0.0, pltpu.roll(c[1], size, 1))

    def beside(here):
        return [
            pltpu.roll(here, size - 1, 0), pltpu.roll(here, 1, 0),
            pltpu.roll(here, lanes - 1, 1), pltpu.roll(here, 1, 1),
        ]

    edges = [row == size - 1, row == 0, high_edge, low_edge]

    for copy in loads[1:]:
        copy.wait()
    short = lax.broadcasted_iota(jnp.int32, (size // 2, lanes), 1) >= size

    def prepare(q, carry):
        here = c[q + 1]
        sides = [jnp.where(edge, 0.0, value) for edge, value in zip(edges, beside(here))]
        sides += [c[q], c[q + 2]]
        inverse = 1.0 / (3.0 * here + 0.5 * total(sides))
        scaled = 0.5 * inverse
        for d, side in enumerate(sides):
            weight = (here + side) * scaled
            if d < 4:
                weight = jnp.where(edges[d], 0.0, weight)
            elif d == 4:
                weight = jnp.where(jnp.logical_and(q == 0, jnp.logical_not(upper)), 0.0, weight)
            else:
                weight = jnp.where(jnp.logical_and(q == half - 1, upper), 0.0, weight)
            w[d, q] = weight
        lower_rhs = o[q] + 2.0 * e[q] + o[q + 1]
        upper_rhs = o[q + half] + 2.0 * e[q + half] + o[q + half + 1]
        top = jnp.where(short, pltpu.roll(upper_rhs, size, 1), lower_rhs)
        bottom = jnp.where(short, upper_rhs, pltpu.roll(lower_rhs, size, 1))
        scaled_rhs = jnp.concatenate([top, bottom], axis=0) * inverse
        step = scaled_rhs * (1.0 / CENTER_VALUE)
        g[q] = scaled_rhs
        p[0, q + 1] = step
        x[q] = step
        return carry

    lax.fori_loop(0, half, prepare, 0)
    sigma = CENTER_VALUE / HALF_WIDTH
    rho = 1.0 / sigma
    for index in range(CHEB - 1):
        now, later = index % 2, (index + 1) % 2
        p[now, 0] = pltpu.roll(p[now, half], size, 1)
        p[now, half + 1] = pltpu.roll(p[now, 1], size, 1)
        rho_new = 1.0 / (2.0 * sigma - rho)
        keep = rho_new * rho
        gain = 2.0 * rho_new / HALF_WIDTH
        rho = rho_new
        final = index == CHEB - 2

        def advance(q, carry):
            here = p[now, q + 1]
            sides = beside(here) + [p[now, q], p[now, q + 2]]
            remains = g[q] - here + total([w[d, q] * side for d, side in enumerate(sides)])
            step = keep * here + gain * remains
            value = x[q] + step
            if final:
                y[q] = value[:, :size]
                y[q + half] = pltpu.roll(value, size, 1)[:, :size]
            else:
                g[q] = remains
                p[later, q + 1] = step
                x[q] = value
            return carry

        lax.fori_loop(0, half, advance, 0, unroll=2)
    copy = go.start(y, solution)
    copy.wait()


def vm(*dims):
    return pltpu.VMEM(dims, F32)


def swapped(value, pairs):
    return lax.ppermute(value, "box", pairs)


def local(rhs_fine, coef_zero, coef_one, coef_two, coef_three):
    count = lax.axis_size("box")
    place = lax.axis_index("box")
    core = place % 2
    scalars = jnp.stack([core, place, jnp.int32(count - 1)]).astype(jnp.int32)
    near = [(i, i ^ 1) for i in range(count)]
    far = [(i, i + 1) for i in range(1, count - 1, 2)]
    far = far + [(j, i) for i, j in far]

    def onward(value, distance):
        route = [(i, i + distance) for i in range(count) if 0 <= i + distance < count]
        return lax.ppermute(value, "box", route)

    n = coef_zero.shape[1]
    n1, n2 = n // 2, n // 4
    n3 = n // 8
    plane = n * n * 4
    matrix0 = jnp.asarray(restriction_matrix(n, n1, 0), BF16)
    matrix1 = jnp.asarray(restriction_matrix(n1, n2, 0), BF16)
    both = np.stack([restriction_matrix(n2, 2 * n3, 0), restriction_matrix(n2, 2 * n3, n3)])
    matrix2 = jnp.asarray(both, BF16)

    def side_plane(field, where):
        return lax.dynamic_index_in_dim(field, where, 0, keepdims=False)

    coef_outer = swapped(side_plane(coef_zero, 3 * core), far)
    coef_sibling = swapped(side_plane(coef_zero, 3 - 3 * core), near)
    first, partial = call(
        first_inner, [shape(2, n, n), shape(2, n, n)],
        [vm(4, n + 16, n), vm(2, n, n), vm(2, n, n), vm(2, n, n)], 10, 40 * n * n, 12 * plane, 40,
    )(scalars, coef_zero, rhs_fine)
    first_outer, first_sibling = call(
        first_rim, [shape(n, n), shape(n, n)],
        [vm(2, n, n)] * 4, 8, 10 * n * n, 8 * plane, 40,
    )(scalars, rhs_fine, partial, coef_outer, coef_sibling)

    halo_outer = swapped(first_outer, far)
    halo_sibling = swapped(first_sibling, near)
    smooth, known, factor = call(
        smooth_inner, [shape(4, n, n), shape(2, n, n), shape(2, n, n)],
        [vm(6, n + 16, n), vm(6, n + 16, n), vm(4, n, n), vm(2, n, n), vm(2, n, n), vm(2, n, n)],
        20, 160 * n * n, 20 * plane, 48,
    )(scalars, coef_zero, rhs_fine, coef_outer, coef_sibling, first, first_outer, first_sibling)
    smooth_zero, smooth_outer, smooth_sibling = call(
        smooth_rim, [shape(4, n, n), shape(n, n), shape(n, n)],
        [vm(2, n, n)] * 4, 10, 4 * n * n, 10 * plane, 40, {1: 0},
    )(scalars, smooth, known, factor, halo_outer, halo_sibling)

    halo_outer = swapped(smooth_outer, far)
    halo_sibling = swapped(smooth_sibling, near)

    def folded(field):
        return jnp.concatenate([field[: n2 // 2], field[n2 // 2 :]], axis=1)

    own_two = folded(coef_two[0])
    coefs = jnp.concatenate([coef_one[0], coef_one[1], own_two], axis=0)
    coefs_sibling = swapped(coefs, near)
    coefs_outer = swapped(coefs, far)
    left_two = jnp.where(core == 0, coefs_outer[2 * n1 :], coefs_sibling[2 * n1 :])
    right_two = jnp.where(core == 0, coefs_sibling[2 * n1 :], coefs_outer[2 * n1 :])
    coefs_before = onward(jnp.concatenate([coef_one[1], own_two, left_two], axis=0), 2)
    coefs_after = onward(jnp.concatenate([coef_one[0], own_two, right_two], axis=0), -2)

    lowered, known, factor = call(
        residual_inner, [shape(2, n1, n1), shape(2, n, n), shape(2, n, n)],
        [vm(6, n + 16, n), vm(6, n + 16, n), vm(4, n, n), vm(2, n, n), vm(2, n, n),
         vm(2, n // LANES, n + 16, LANES), vm(2, n1, n1), pltpu.VMEM((n, n1), BF16)],
        20, 160 * n * n, 20 * plane, 48,
    )(scalars, coef_zero, rhs_fine, coef_outer, coef_sibling, smooth_zero, smooth_outer,
      smooth_sibling, matrix0)
    (packed,) = call(
        residual_rim, [shape(3, n1, n1)],
        [vm(2, n, n), vm(2, n, n), vm(2, n, n), vm(2, n // LANES, n + 16, LANES), vm(4, n1, n1), vm(3, n1, n1),
         pltpu.VMEM((n, n1), BF16)],
        10, 20 * n * n, 8 * plane, 40,
    )(scalars, known, factor, halo_outer, halo_sibling, lowered, matrix0)

    packed_outer = swapped(packed, far)
    packed_before = onward(packed[2], 2)
    packed_sibling = swapped(packed, near)
    smooth_one, packed = call(
        middle_level, [shape(2, n1, n1), shape(2, n2, n2)],
        [vm(10, n1, n1), vm(6, n1, n1), vm(8, n1 + 16, n1), vm(6, n1 + 16, n1),
         vm(4, n1 + 16, n1), vm(2, n1 // LANES, n1 + 16, LANES), vm(2, n2, n2), pltpu.VMEM((n1, n2), BF16)],
        18, 400 * n1 * n1, 24 * n1 * n1 * 4, 40,
    )(scalars, packed, packed_sibling, packed_outer, packed_before, coef_one, coefs_sibling,
      coefs_outer, coefs_before, coefs_after, matrix1)

    packed_outer = swapped(packed, far)
    packed_before = onward(packed, 2)
    packed_after = onward(packed, -2)
    packed_rim = onward(packed[1], 3)
    packed_sibling = swapped(packed, near)
    groups = [[i for i in range(count) if i % 2 == r] for r in range(2)]
    smooth_two, copies = call(
        last_level, [shape(1, n2, n2), shape(count // 2, n3 // 2, 2 * n3)],
        [vm(11, n2, n2), vm(5, n2, n2), vm(7, n2 + 16, n2), vm(5, n2 + 16, n2),
         vm(3, n2 + 16, n2), vm(1, n2 // LANES, n2 + 16, LANES), vm(count // 2, n3 // 2, 2 * n3),
         pltpu.VMEM((2, n2, 2 * n3), BF16)],
        24, 300 * n2 * n2, 40 * n2 * n2 * 4, 40,
    )(scalars, packed, packed_sibling, packed_outer, packed_before, packed_after, packed_rim,
      coef_two, coefs_sibling, coefs_outer, coefs_before, coefs_after, matrix2)

    gathered = lax.all_to_all(copies, "box", 0, 0, tiled=True, axis_index_groups=groups)
    gathered_sibling = swapped(gathered, near)
    half = n3 // 2
    coef_pair = jnp.concatenate([coef_three[:half], coef_three[half:]], axis=2)
    (coarse_solution,) = call(
        coarse_level, [shape(n3, n3, n3)],
        [vm(n3, half, 2 * n3), vm(n3 + 1, half, 2 * n3), vm(half + 2, n3, 2 * n3),
         vm(6, half, n3, 2 * n3), vm(2, half + 2, n3, 2 * n3), vm(half, n3, 2 * n3),
         vm(half, n3, 2 * n3), vm(n3, n3, n3)],
        4, 300 * n3 * n3 * n3, 20 * n3 * n3 * n3, 48,
    )(scalars, gathered, gathered_sibling, coef_pair)
    return (smooth_zero, smooth_one, smooth_two, coarse_solution)


def solution(mesh):
    placed = (
        P("box", None, None),
        P("box", None, None),
        P("box", None, None),
        P("box", None, None),
        P(),
    )
    return jax.shard_map(
        local,
        mesh=mesh,
        in_specs=placed,
        out_specs=(P("box", None, None), P("box", None, None), P("box", None, None), P()),
        check_vma=False,
    )
```

time: 664 us -> 249 us (0.38); the launches traced: 656 us -> 248 us
  other arithmetic: 238 us -> 1.35 us
  waiting for transfers between devices: 171 us -> 17.3 us
  local copies, waits for them, and re-layouts: 166 us -> 12.9 us
  Pallas kernels: 0 us -> 130 us
  blocking collectives: 0 us -> 41.6 us
  starting transfers between devices: 64.7 us -> 43.9 us
  between operations: 15.1 us -> 1.2 us
    pallas_call x0 -> x9, Pallas kernels: none -> 130 us  [run(): pl.pallas_call(body, out_shape=outs, in_specs=[pl.BlockSpec(memory_space=...]
    add x25 -> x0, other arithmetic: 123 us -> none  [the longest x15 91.6 us: advance(): iterate = iterate + step_field]
    all_gather x1 -> x0, waiting for transfers between devices: 114 us -> none  [local(): gathered = lax.all_gather(in_plane, 'box', axis=0, tiled=True)]
    slice x26 -> x2, local copies, waits for them, and re-layouts: 106 us -> 0.24 us  [the longest x1 0.23 us: local(): coef_pair = jnp.concatenate([coef_three[:half], coef_three[half:]], axis=2)]
    sub x19 -> x0, other arithmetic: 85.9 us -> none  [the longest x15 60.6 us: advance(): remains - apply_operator(pad_first(step_field), coef_ext, diagonal)]
    while x180 -> x0, local copies, waits for them, and re-layouts: 49.8 us -> none
    all_to_all x0 -> x1, blocking collectives: none -> 41.6 us  [local(): lax.all_to_all(copies, 'box', 0, 0, tiled=True, axis_index_groups=groups)]
    ppermute x20 -> x19, waiting for transfers between devices: 56.1 us -> 17.3 us  [the longest x6 15.6 us: onward(): return lax.ppermute(value, 'box', route)]
  transfers between devices with their start and end apart: 21 -> 19, of which waited for: 16 -> 4; matrix products, arithmetic and copies ran while one was open for 0% -> 1% of each run, Pallas kernels for 0% -> 24%
where the time goes in v1:
time: 249 us; the launch traced here: 248 us
  Pallas kernels  130 us (52%)
  starting transfers between devices  43.9 us (18%)
  blocking collectives  41.6 us (17%)
  waiting for transfers between devices  17.3 us (7%)
  local copies, waits for them, and re-layouts  12.9 us (5%)
    pallas_call x9, Pallas kernels, run(): pl.pallas_call(body, out_shape=outs, in_specs=[pl.BlockSpec(memory_space=...  130 us
    all_to_all x1, blocking collectives, local(): lax.all_to_all(copies, 'box', 0, 0, tiled=True, axis_index_groups=groups)  41.6 us
    ppermute x13, starting transfers between devices, swapped(): return lax.ppermute(value, 'box', pairs)  25.3 us
    ppermute x6, starting transfers between devices, onward(): return lax.ppermute(value, 'box', route)  18.6 us
    ppermute x6, waiting for transfers between devices, onward(): return lax.ppermute(value, 'box', route)  15.6 us
    unnamed x46, local copies, waits for them, and re-layouts  10.7 us
  transfers between devices with their start and end apart: 19, of which 4 were waited for; matrix products, arithmetic and copies ran while one was open for 1% of the time, Pallas kernels for 24%

profile of v1, /device:TPU:1, one launch (start us, length us, event | category | flops | bytes accessed | tf_op | source)
XLA Modules:
  0.0 248.2 jit_solution(17188911365418161934)
XLA Ops:
  2.5 4.5 %collective-permute-start = (f32[512,512]{1,0:T(8,128)S(1)}, f32[512,512]{1,0:T(8,128)S(1)}, u32[]{:S(2)}, u32[]{:S(2)}) collective-permute-start(f32[512,512]{1,0:T(8,128)S(1)} %get-tuple-element.39), channel_id=1, source_target_pairs={{1,2},{3,4},{5,6},{7,8},{9,10},{11,12},{13,14},{15,16},{17,18},{19... | collective-permute-start | bytes 3145736 | tf_op jit(solution)/shard_map/ppermute | solution.py:661
  7.2 2.2 copy-done.1
  9.4 14.2 %shard_map.111 = (f32[2,512,512]{2,1,0:T(8,128)S(1)}, f32[2,512,512]{2,1,0:T(8,128)S(1)}) custom-call(s32[3]{0:T(128)S(1)} %pad_add_fusion.scalars, f32[4,512,512]{2,1,0:T(8,128)S(1)} %copy-done.1, f32[4,512,512]{2,1,0:T(8,128)S(1)} %copy-done), custom_call_target="tpu_custom_call" | custom-call | flops 10485760 | bytes 12582912 | tf_op jit(solution)/shard_map/pallas_call | solution.py:38
  25.0 2.3 shard_map.112
  27.3 3.5 %collective-permute-start.2 = (f32[512,512]{1,0:T(8,128)S(1)}, f32[512,512]{1,0:T(8,128)S(1)}, u32[]{:S(2)}, u32[]{:S(2)}) collective-permute-start(f32[512,512]{1,0:T(8,128)S(1)} %get-tuple-element.23.first_outer), channel_id=1, source_target_pairs={{1,2},{3,4},{5,6},{7,8},{9,10},{11,12},{13,14},{15,16},{17,18},{19... | collective-permute-start | bytes 3145736 | tf_op jit(solution)/shard_map/ppermute | solution.py:661
  30.9 20.9 %shard_map.113 = (f32[4,512,512]{2,1,0:T(8,128)}, f32[2,512,512]{2,1,0:T(8,128)}, f32[2,512,512]{2,1,0:T(8,128)}) custom-call(s32[3]{0:T(128)S(1)} %pad_add_fusion.scalars, f32[4,512,512]{2,1,0:T(8,128)} %coef.7, f32[4,512,512]{2,1,0:T(8,128)} %rhs.7, f32[512,512]{1,0:T(8,128)S(1)} %collective-permute-done.coef_outer, ...), custom_call_target="tpu_custom_call" | custom-call | flops 41943040 | bytes 20971520 | tf_op jit(solution)/shard_map/pallas_call | solution.py:38
  55.0 3.4 %shard_map.114 = (f32[4,512,512]{2,1,0:T(8,128)}, f32[512,512]{1,0:T(8,128)}, f32[512,512]{1,0:T(8,128)}) custom-call(s32[3]{0:T(128)S(1)} %pad_add_fusion.scalars, f32[4,512,512]{2,1,0:T(8,128)} %get-tuple-element.25.started, f32[2,512,512]{2,1,0:T(8,128)S(1)} %copy-done.3, f32[2,512,512]{2,1,0:T(8,128)S(1)} %copy-done.4, ...), custom_call_target="tpu_custom_call", output_to_operand_aliasing={{0}: (1, {})} | custom-call | flops 1048576 | bytes 10485760 | tf_op jit(solution)/shard_map/pallas_call | solution.py:38
  58.5 3.3 %collective-permute-start.4 = (f32[512,512]{1,0:T(8,128)}, f32[512,512]{1,0:T(8,128)}, u32[]{:S(2)}, u32[]{:S(2)}) collective-permute-start(f32[512,512]{1,0:T(8,128)} %get-tuple-element.29.smooth_outer), channel_id=1, source_target_pairs={{1,2},{3,4},{5,6},{7,8},{9,10},{11,12},{13,14},{15,16},{17,18},{19... | collective-permute-start | bytes 3145736 | tf_op jit(solution)/shard_map/ppermute | solution.py:661
  63.7 3.5 %collective-permute-start.10 = (f32[576,256]{1,0:T(8,128)}, f32[576,256]{1,0:T(8,128)S(1)}, u32[]{:S(2)}, u32[]{:S(2)}) collective-permute-start(f32[576,256]{1,0:T(8,128)} %maximum_maximum_fusion), channel_id=1, source_target_pairs={{1,2},{3,4},{5,6},{7,8},{9,10},{11,12},{13,14},{15,16},{17,18},{19... | collective-permute-start | bytes 1769480 | tf_op jit(solution)/shard_map/ppermute | solution.py:661
  67.3 20.9 %shard_map.115 = (f32[2,256,256]{2,1,0:T(8,128)S(1)}, f32[2,512,512]{2,1,0:T(8,128)}, f32[2,512,512]{2,1,0:T(8,128)}) custom-call(s32[3]{0:T(128)S(1)} %pad_add_fusion.scalars, f32[4,512,512]{2,1,0:T(8,128)} %coef.7, f32[4,512,512]{2,1,0:T(8,128)} %rhs.7, f32[512,512]{1,0:T(8,128)S(1)} %collective-permute-done.coef_outer, ...), custom_call_target="tpu_custom_call" | custom-call | flops 41943040 | bytes 20971520 | tf_op jit(solution)/shard_map/pallas_call | solution.py:38
  91.4 3.9 %shard_map.116.own = f32[3,256,256]{2,1,0:T(8,128)S(1)} custom-call(s32[3]{0:T(128)S(1)} %pad_add_fusion.scalars, f32[2,512,512]{2,1,0:T(8,128)S(1)} %copy-done.5, f32[2,512,512]{2,1,0:T(8,128)S(1)} %copy-done.6, f32[512,512]{1,0:T(8,128)} %collective-permute-done.4.halo_outer, f32[512,512]{1,0:T(8,128)} %collective-permute-done.5.halo_sibling, ...), custom_call_target="tpu_custom_call" | custom-call | flops 5242880 | bytes 8388608 | tf_op jit(solution)/shard_map/pallas_call | solution.py:38
  95.8 3.6 %collective-permute-start.7 = (f32[3,256,256]{2,1,0:T(8,128)S(1)}, f32[3,256,256]{2,1,0:T(8,128)S(1)}, u32[]{:S(2)}, u32[]{:S(2)}) collective-permute-start(f32[3,256,256]{2,1,0:T(8,128)S(1)} %shard_map.116.own), channel_id=1, source_target_pairs={{1,2},{3,4},{5,6},{7,8},{9,10},{11,12},{13,14},{15,16},{17,18},{19... | collective-permute-start | bytes 2359304 | tf_op jit(solution)/shard_map/ppermute | solution.py:661
  99.6 3.3 %collective-permute-start.11 = (f32[384,256]{1,0:T(8,128)S(1)}, f32[384,256]{1,0:T(8,128)S(1)}, u32[]{:S(2)}, u32[]{:S(2)}) collective-permute-start(f32[384,256]{1,0:T(8,128)S(1)} %get-tuple-element.47), channel_id=1, source_target_pairs={{0,2},{1,3},{2,4},{3,5},{4,6},{5,7},{6,8},{7,9},{8,10},{9,11},{10,... | collective-permute-start | bytes 1179656 | tf_op jit(solution)/shard_map/ppermute | solution.py:675
  104.3 4.4 %collective-permute-start.8 = (f32[256,256]{1,0:T(8,128)S(1)}, f32[256,256]{1,0:T(8,128)S(1)}, u32[]{:S(2)}, u32[]{:S(2)}) collective-permute-start(f32[256,256]{1,0:T(8,128)S(1)} %slice_bitcast_fusion), channel_id=1, source_target_pairs={{0,2},{1,3},{2,4},{3,5},{4,6},{5,7},{6,8},{7,9},{8,10},{9,11},{10,... | collective-permute-start | bytes 786440 | tf_op jit(solution)/shard_map/ppermute | solution.py:675
  108.7 10.9 %collective-permute-done.11.coef_before = f32[384,256]{1,0:T(8,128)S(1)} collective-permute-done((f32[384,256]{1,0:T(8,128)S(1)}, f32[384,256]{1,0:T(8,128)S(1)}, u32[]{:S(2)}, u32[]{:S(2)}) %collective-permute-start.11) | collective-permute-done | bytes 393248 | tf_op jit(solution)/shard_map/ppermute | solution.py:675
  119.7 2.8 %collective-permute-done.8.before = f32[256,256]{1,0:T(8,128)S(1)} collective-permute-done((f32[256,256]{1,0:T(8,128)S(1)}, f32[256,256]{1,0:T(8,128)S(1)}, u32[]{:S(2)}, u32[]{:S(2)}) %collective-permute-start.8) | collective-permute-done | bytes 262176 | tf_op jit(solution)/shard_map/ppermute | solution.py:675
  122.5 20.2 %shard_map.117 = (f32[2,256,256]{2,1,0:T(8,128)}, f32[2,128,128]{2,1,0:T(8,128)S(1)}) custom-call(s32[3]{0:T(128)S(1)} %pad_add_fusion.scalars, f32[3,256,256]{2,1,0:T(8,128)S(1)} %shard_map.116.own, f32[3,256,256]{2,1,0:T(8,128)S(1)} %collective-permute-done.6.sibling, f32[3,256,256]{2,1,0:T(8,128)S(1)} %collective-permute-done.7.outer, ...), custom_call_target="tpu_custom_call" | custom-call | flops 26214400 | bytes 6291456 | tf_op jit(solution)/shard_map/pallas_call | solution.py:38
  142.8 4.2 %collective-permute-start.14 = (f32[2,128,128]{2,1,0:T(8,128)S(1)}, f32[2,128,128]{2,1,0:T(8,128)S(1)}, u32[]{:S(2)}, u32[]{:S(2)}) collective-permute-start(f32[2,128,128]{2,1,0:T(8,128)S(1)} %get-tuple-element.35.own), channel_id=1, source_target_pairs={{1,2},{3,4},{5,6},{7,8},{9,10},{11,12},{13,14},{15,16},{17,18},{19... | collective-permute-start | bytes 393224 | tf_op jit(solution)/shard_map/ppermute | solution.py:661
  147.0 3.3 %collective-permute-start.15 = (f32[2,128,128]{2,1,0:T(8,128)S(1)}, f32[2,128,128]{2,1,0:T(8,128)S(1)}, u32[]{:S(2)}, u32[]{:S(2)}) collective-permute-start(f32[2,128,128]{2,1,0:T(8,128)S(1)} %get-tuple-element.35.own), channel_id=1, source_target_pairs={{0,2},{1,3},{2,4},{3,5},{4,6},{5,7},{6,8},{7,9},{8,10},{9,11},{10,... | collective-permute-start | bytes 393224 | tf_op jit(solution)/shard_map/ppermute | solution.py:675
  151.6 5.0 %collective-permute-start.17 = (f32[128,128]{1,0:T(8,128)S(1)}, f32[128,128]{1,0:T(8,128)S(1)}, u32[]{:S(2)}, u32[]{:S(2)}) collective-permute-start(f32[128,128]{1,0:T(8,128)S(1)} %slice_bitcast_fusion.3), channel_id=1, source_target_pairs={{0,3},{1,4},{2,5},{3,6},{4,7},{5,8},{6,9},{7,10},{8,11},{9,12},{10... | collective-permute-start | bytes 196616 | tf_op jit(solution)/shard_map/ppermute | solution.py:675
  156.6 1.9 collective-permute-done.17.rim
  158.6 8.8 %shard_map.118 = (f32[1,128,128]{2,1,0:T(8,128)}, f32[64,32,128]{2,1,0:T(8,128)S(1)}) custom-call(s32[3]{0:T(128)S(1)} %pad_add_fusion.scalars, f32[2,128,128]{2,1,0:T(8,128)S(1)} %get-tuple-element.35.own, f32[2,128,128]{2,1,0:T(8,128)S(1)} %collective-permute-done.13.sibling, f32[2,128,128]{2,1,0:T(8,128)S(1)} %collective-permute-done.14.outer, ...), custom_call_target="tpu_custom_call" | custom-call | flops 4915200 | bytes 2621440 | tf_op jit(solution)/shard_map/pallas_call | solution.py:38
  167.4 41.6 %all_to_all.5.own = f32[64,32,128]{2,1,0:T(8,128)S(1)} all-to-all(f32[64,32,128]{2,1,0:T(8,128)S(1)} %get-tuple-element.37), channel_id=1, replica_groups={{0,2,4,6,8,10,12,14,16,18,20,22,24,26,28,30,32,34,36,38,40,42,44,46,48,..., dimensions={0} | all-to-all | bytes 2097152 | tf_op jit(solution)/shard_map/all_to_all | solution.py:767
  213.0 35.2 %shard_map.119 = f32[64,64,64]{2,1,0:T(8,128)} custom-call(s32[3]{0:T(128)S(1)} %pad_add_fusion.scalars, f32[64,32,128]{2,1,0:T(8,128)S(1)} %all_to_all.5.own, f32[64,32,128]{2,1,0:T(8,128)S(1)} %collective-permute-done.18.sibling, f32[32,64,128]{2,1,0:T(8,128)S(1)} %pad_maximum_fusion.coef), custom_call_target="tpu_custom_call" | custom-call | flops 78643200 | bytes 5242880 | tf_op jit(solution)/shard_map/pallas_call | solution.py:38
  (81 shorter events, 19.0 us)
Async XLA Ops:
  2.5 22.4 %collective-permute-start = (f32[512,512]{1,0:T(8,128)S(1)}, f32[512,512]{1,0:T(8,128)S(1)}, u32[]{:S(2)}, u32[]{:S(2)}) collective-permute-start(f32[512,512]{1,0:T(8,128)S(1)} %get-tuple-element.39), channel_id=1, source_target_pairs={{1,2},{3,4},{5,6},{7,8},{9,10},{11,12},{13,14},{15,16},{17,18},{19... | collective-permute-start | bytes 3145736 | tf_op jit(solution)/shard_map/ppermute | solution.py:661
  7.1 17.9 %collective-permute-start.1 = (f32[512,512]{1,0:T(8,128)S(1)}, f32[512,512]{1,0:T(8,128)S(1)}, u32[]{:S(2)}, u32[]{:S(2)}) collective-permute-start(f32[512,512]{1,0:T(8,128)S(1)} %get-tuple-element.38), channel_id=1, source_target_pairs={{0,1},{1,0},{2,3},{3,2},{4,5},{5,4},{6,7},{7,6},{8,9},{9,8},{10,11... | collective-permute-start | bytes 3145736 | tf_op jit(solution)/shard_map/ppermute | solution.py:661
  27.3 24.5 %collective-permute-start.2 = (f32[512,512]{1,0:T(8,128)S(1)}, f32[512,512]{1,0:T(8,128)S(1)}, u32[]{:S(2)}, u32[]{:S(2)}) collective-permute-start(f32[512,512]{1,0:T(8,128)S(1)} %get-tuple-element.23.first_outer), channel_id=1, source_target_pairs={{1,2},{3,4},{5,6},{7,8},{9,10},{11,12},{13,14},{15,16},{17,18},{19... | collective-permute-start | bytes 3145736 | tf_op jit(solution)/shard_map/ppermute | solution.py:661
  30.8 21.0 %collective-permute-start.3 = (f32[512,512]{1,0:T(8,128)S(1)}, f32[512,512]{1,0:T(8,128)S(1)}, u32[]{:S(2)}, u32[]{:S(2)}) collective-permute-start(f32[512,512]{1,0:T(8,128)S(1)} %get-tuple-element.24.first_sibling), channel_id=1, source_target_pairs={{0,1},{1,0},{2,3},{3,2},{4,5},{5,4},{6,7},{7,6},{8,9},{9,8},{10,11... | collective-permute-start | bytes 3145736 | tf_op jit(solution)/shard_map/ppermute | solution.py:661
  58.5 29.7 %collective-permute-start.4 = (f32[512,512]{1,0:T(8,128)}, f32[512,512]{1,0:T(8,128)}, u32[]{:S(2)}, u32[]{:S(2)}) collective-permute-start(f32[512,512]{1,0:T(8,128)} %get-tuple-element.29.smooth_outer), channel_id=1, source_target_pairs={{1,2},{3,4},{5,6},{7,8},{9,10},{11,12},{13,14},{15,16},{17,18},{19... | collective-permute-start | bytes 3145736 | tf_op jit(solution)/shard_map/ppermute | solution.py:661
  61.8 26.4 %collective-permute-start.5 = (f32[512,512]{1,0:T(8,128)}, f32[512,512]{1,0:T(8,128)}, u32[]{:S(2)}, u32[]{:S(2)}) collective-permute-start(f32[512,512]{1,0:T(8,128)} %get-tuple-element.30.smooth_sibling), channel_id=1, source_target_pairs={{0,1},{1,0},{2,3},{3,2},{4,5},{5,4},{6,7},{7,6},{8,9},{9,8},{10,11... | collective-permute-start | bytes 3145736 | tf_op jit(solution)/shard_map/ppermute | solution.py:661
  63.7 35.8 %collective-permute-start.10 = (f32[576,256]{1,0:T(8,128)}, f32[576,256]{1,0:T(8,128)S(1)}, u32[]{:S(2)}, u32[]{:S(2)}) collective-permute-start(f32[576,256]{1,0:T(8,128)} %maximum_maximum_fusion), channel_id=1, source_target_pairs={{1,2},{3,4},{5,6},{7,8},{9,10},{11,12},{13,14},{15,16},{17,18},{19... | collective-permute-start | bytes 1769480 | tf_op jit(solution)/shard_map/ppermute | solution.py:661
  67.1 32.4 %collective-permute-start.9 = (f32[576,256]{1,0:T(8,128)}, f32[576,256]{1,0:T(8,128)S(1)}, u32[]{:S(2)}, u32[]{:S(2)}) collective-permute-start(f32[576,256]{1,0:T(8,128)} %maximum_maximum_fusion), channel_id=1, source_target_pairs={{0,1},{1,0},{2,3},{3,2},{4,5},{5,4},{6,7},{7,6},{8,9},{9,8},{10,11... | collective-permute-start | bytes 1769480 | tf_op jit(solution)/shard_map/ppermute | solution.py:661
  95.3 27.2 %copy-start.8 = (f32[2,256,256]{2,1,0:T(8,128)S(1)}, f32[2,256,256]{2,1,0:T(8,128)}, u32[]{:S(2)}) copy-start(f32[2,256,256]{2,1,0:T(8,128)} %coef.8) | copy-start | bytes 1572868
  95.3 27.2 %copy-start.12 = (bf16[256,128]{1,0:T(8,128)(2,1)S(1)}, bf16[256,128]{1,0:T(8,128)(2,1)}, u32[]{:S(2)}) copy-start(bf16[256,128]{1,0:T(8,128)(2,1)} %constant.38.clone.matrix) | copy-start | bytes 196612
  95.3 27.2 %collective-permute-start.6 = (f32[3,256,256]{2,1,0:T(8,128)S(1)}, f32[3,256,256]{2,1,0:T(8,128)S(1)}, u32[]{:S(2)}, u32[]{:S(2)}) collective-permute-start(f32[3,256,256]{2,1,0:T(8,128)S(1)} %shard_map.116.own), channel_id=1, source_target_pairs={{0,1},{1,0},{2,3},{3,2},{4,5},{5,4},{6,7},{7,6},{8,9},{9,8},{10,11... | collective-permute-start | bytes 2359304 | tf_op jit(solution)/shard_map/ppermute | solution.py:661
  95.8 26.6 %collective-permute-start.7 = (f32[3,256,256]{2,1,0:T(8,128)S(1)}, f32[3,256,256]{2,1,0:T(8,128)S(1)}, u32[]{:S(2)}, u32[]{:S(2)}) collective-permute-start(f32[3,256,256]{2,1,0:T(8,128)S(1)} %shard_map.116.own), channel_id=1, source_target_pairs={{1,2},{3,4},{5,6},{7,8},{9,10},{11,12},{13,14},{15,16},{17,18},{19... | collective-permute-start | bytes 2359304 | tf_op jit(solution)/shard_map/ppermute | solution.py:661
  99.6 20.0 %collective-permute-start.11 = (f32[384,256]{1,0:T(8,128)S(1)}, f32[384,256]{1,0:T(8,128)S(1)}, u32[]{:S(2)}, u32[]{:S(2)}) collective-permute-start(f32[384,256]{1,0:T(8,128)S(1)} %get-tuple-element.47), channel_id=1, source_target_pairs={{0,2},{1,3},{2,4},{3,5},{4,6},{5,7},{6,8},{7,9},{8,10},{9,11},{10,... | collective-permute-start | bytes 1179656 | tf_op jit(solution)/shard_map/ppermute | solution.py:675
  103.0 16.7 %collective-permute-start.12 = (f32[384,256]{1,0:T(8,128)S(1)}, f32[384,256]{1,0:T(8,128)S(1)}, u32[]{:S(2)}, u32[]{:S(2)}) collective-permute-start(f32[384,256]{1,0:T(8,128)S(1)} %get-tuple-element.46), channel_id=1, source_target_pairs={{2,0},{3,1},{4,2},{5,3},{6,4},{7,5},{8,6},{9,7},{10,8},{11,9},{12,... | collective-permute-start | bytes 1179656 | tf_op jit(solution)/shard_map/ppermute | solution.py:675
  104.3 54.3 %copy-start.11 = (f32[1,128,128]{2,1,0:T(8,128)S(1)}, f32[1,128,128]{2,1,0:T(8,128)}, u32[]{:S(2)}) copy-start(f32[1,128,128]{2,1,0:T(8,128)} %coef.9) | copy-start | bytes 196612
  104.3 54.3 %copy-start.13 = (bf16[2,128,128]{2,1,0:T(8,128)(2,1)S(1)}, bf16[2,128,128]{2,1,0:T(8,128)(2,1)}, u32[]{:S(2)}) copy-start(bf16[2,128,128]{2,1,0:T(8,128)(2,1)} %constant.39.clone.matrices) | copy-start | bytes 196612
  104.3 18.1 %collective-permute-start.8 = (f32[256,256]{1,0:T(8,128)S(1)}, f32[256,256]{1,0:T(8,128)S(1)}, u32[]{:S(2)}, u32[]{:S(2)}) collective-permute-start(f32[256,256]{1,0:T(8,128)S(1)} %slice_bitcast_fusion), channel_id=1, source_target_pairs={{0,2},{1,3},{2,4},{3,5},{4,6},{5,7},{6,8},{7,9},{8,10},{9,11},{10,... | collective-permute-start | bytes 786440 | tf_op jit(solution)/shard_map/ppermute | solution.py:675
  142.7 15.8 %collective-permute-start.13 = (f32[2,128,128]{2,1,0:T(8,128)S(1)}, f32[2,128,128]{2,1,0:T(8,128)S(1)}, u32[]{:S(2)}, u32[]{:S(2)}) collective-permute-start(f32[2,128,128]{2,1,0:T(8,128)S(1)} %get-tuple-element.35.own), channel_id=1, source_target_pairs={{0,1},{1,0},{2,3},{3,2},{4,5},{5,4},{6,7},{7,6},{8,9},{9,8},{10,11... | collective-permute-start | bytes 393224 | tf_op jit(solution)/shard_map/ppermute | solution.py:661
  142.8 15.7 %collective-permute-start.14 = (f32[2,128,128]{2,1,0:T(8,128)S(1)}, f32[2,128,128]{2,1,0:T(8,128)S(1)}, u32[]{:S(2)}, u32[]{:S(2)}) collective-permute-start(f32[2,128,128]{2,1,0:T(8,128)S(1)} %get-tuple-element.35.own), channel_id=1, source_target_pairs={{1,2},{3,4},{5,6},{7,8},{9,10},{11,12},{13,14},{15,16},{17,18},{19... | collective-permute-start | bytes 393224 | tf_op jit(solution)/shard_map/ppermute | solution.py:661
  147.0 11.6 %collective-permute-start.15 = (f32[2,128,128]{2,1,0:T(8,128)S(1)}, f32[2,128,128]{2,1,0:T(8,128)S(1)}, u32[]{:S(2)}, u32[]{:S(2)}) collective-permute-start(f32[2,128,128]{2,1,0:T(8,128)S(1)} %get-tuple-element.35.own), channel_id=1, source_target_pairs={{0,2},{1,3},{2,4},{3,5},{4,6},{5,7},{6,8},{7,9},{8,10},{9,11},{10,... | collective-permute-start | bytes 393224 | tf_op jit(solution)/shard_map/ppermute | solution.py:675
  150.3 8.2 %collective-permute-start.16 = (f32[2,128,128]{2,1,0:T(8,128)S(1)}, f32[2,128,128]{2,1,0:T(8,128)S(1)}, u32[]{:S(2)}, u32[]{:S(2)}) collective-permute-start(f32[2,128,128]{2,1,0:T(8,128)S(1)} %get-tuple-element.35.own), channel_id=1, source_target_pairs={{2,0},{3,1},{4,2},{5,3},{6,4},{7,5},{8,6},{9,7},{10,8},{11,9},{12,... | collective-permute-start | bytes 393224 | tf_op jit(solution)/shard_map/ppermute | solution.py:675
  151.6 59.1 %copy-start.18 = (f32[64,64,64]{2,1,0:T(8,128)S(1)}, f32[64,64,64]{2,1,0:T(8,128)}, u32[]{:S(2)}) copy-start(f32[64,64,64]{2,1,0:T(8,128)} %param.12) | copy-start | bytes 3145732
  151.6 6.9 %collective-permute-start.17 = (f32[128,128]{1,0:T(8,128)S(1)}, f32[128,128]{1,0:T(8,128)S(1)}, u32[]{:S(2)}, u32[]{:S(2)}) collective-permute-start(f32[128,128]{1,0:T(8,128)S(1)} %slice_bitcast_fusion.3), channel_id=1, source_target_pairs={{0,3},{1,4},{2,5},{3,6},{4,7},{5,8},{6,9},{7,10},{8,11},{9,12},{10... | collective-permute-start | bytes 196616 | tf_op jit(solution)/shard_map/ppermute | solution.py:675
  209.0 4.0 %collective-permute-start.18 = (f32[64,32,128]{2,1,0:T(8,128)S(1)}, f32[64,32,128]{2,1,0:T(8,128)S(1)}, u32[]{:S(2)}, u32[]{:S(2)}) collective-permute-start(f32[64,32,128]{2,1,0:T(8,128)S(1)} %all_to_all.5.own), channel_id=1, source_target_pairs={{0,1},{1,0},{2,3},{3,2},{4,5},{5,4},{6,7},{7,6},{8,9},{9,8},{10,11... | collective-permute-start | bytes 3145736 | tf_op jit(solution)/shard_map/ppermute | solution.py:661
  (18 other events, 74.5 us)

commit v2 on v1

v2 whole, which is shorter than its diff:
```python
import jax
import jax.numpy as jnp
import numpy as np
from jax import lax
from jax.experimental import pallas as pl
from jax.experimental.pallas import tpu as pltpu
from jax.sharding import PartitionSpec as P

CHEB = 16
OMEGA = 0.8
CENTER_VALUE = 1.04
HALF_WIDTH = 0.96
ROWS = 8
UNROLL = 16
PAD = 8
LANES = 128
F32 = jnp.float32
BF16 = jnp.bfloat16


def restriction_matrix(fine, coarse_lanes, shift):
    weights = np.zeros((fine, coarse_lanes), np.float32)
    for k in range(fine // 2):
        weights[2 * k, k + shift] = 0.5
        weights[2 * k + 1, k + shift] = 0.25
        if k > 0:
            weights[2 * k - 1, k + shift] = 0.25
    return weights


def shape(*dims):
    return jax.ShapeDtypeStruct(dims, F32)


def call(body, outs, scratch, copies, flops, moved, megabytes, aliases=None):
    sems = [pltpu.SemaphoreType.DMA((copies,))]

    def run(scalars, *arrays):
        return pl.pallas_call(
            body,
            out_shape=outs,
            in_specs=[pl.BlockSpec(memory_space=pltpu.SMEM)]
            + [pl.BlockSpec(memory_space=pl.ANY)] * len(arrays),
            out_specs=[pl.BlockSpec(memory_space=pl.ANY)] * len(outs),
            scratch_shapes=scratch + sems,
            input_output_aliases=aliases or {},
            compiler_params=pltpu.CompilerParams(vmem_limit_bytes=megabytes << 20),
            cost_estimate=pl.CostEstimate(flops=flops, bytes_accessed=moved, transcendentals=0),
        )(scalars, *arrays)

    return run


class Group:
    def __init__(self, copies):
        self.copies = list(copies)

    def wait(self):
        for copy in self.copies:
            copy.wait()


class Copies:
    def __init__(self, sems):
        self.sems = sems
        self.used = 0

    def start(self, source, target):
        copy = pltpu.make_async_copy(source, target, self.sems.at[self.used])
        self.used += 1
        copy.start()
        return copy

    def tiles(self, source, target, rows=None):
        rows = source.shape[0] if rows is None else rows
        return Group(
            self.start(source.at[:, columns(t)], target.at[t, pl.ds(PAD, rows), :])
            for t in range(source.shape[1] // LANES)
        )

    def untiled(self, source, target):
        rows = target.shape[0]
        return Group(
            self.start(source.at[t, pl.ds(PAD, rows), :], target.at[:, columns(t)])
            for t in range(target.shape[1] // LANES)
        )

    def choose(self, first_if, source, other, target):
        copy = pltpu.make_async_copy(source, target, self.sems.at[self.used])
        swap = pltpu.make_async_copy(other, target, self.sems.at[self.used])
        self.used += 1

        @pl.when(first_if)
        def _():
            copy.start()

        @pl.when(jnp.logical_not(first_if))
        def _():
            swap.start()

        return copy


def clear_pads(tiles, size):
    zeros = jnp.zeros(tiles.shape[:2] + (PAD, LANES), F32)
    tiles[:, :, :PAD, :] = zeros
    tiles[:, :, PAD + size :, :] = zeros


def clear_top(tiles):
    tiles[:, :, :PAD, :] = jnp.zeros(tiles.shape[:2] + (PAD, LANES), F32)


def columns(tile):
    return pl.ds(tile * LANES, LANES)


def load_rows(ref, plane, row, offset=0):
    return [ref[plane, t, pl.ds(PAD + row + offset, ROWS), :] for t in range(ref.shape[1])]


def load_flat(ref, plane, row):
    part = pl.ds(row, ROWS)
    return [ref[plane, part, columns(t)] for t in range(ref.shape[2] // LANES)]


def store_rows(ref, plane, row, values):
    for t, value in enumerate(values):
        ref[plane, t, pl.ds(PAD + row, ROWS), :] = value


def store_flat(ref, plane, row, values):
    for t, value in enumerate(values):
        ref[plane, pl.ds(row, ROWS), columns(t)] = value


def store_whole(ref, plane, row, value):
    ref[plane, pl.ds(row, ROWS), :] = value


def each(function, *lists):
    return [function(*values) for values in zip(*lists)]


def lane_sides(centre):
    lane = lax.broadcasted_iota(jnp.int32, (ROWS, LANES), 1)
    first = lane == 0
    last = lane == LANES - 1
    up = [pltpu.roll(value, 1, 1) for value in centre]
    down = [pltpu.roll(value, LANES - 1, 1) for value in centre]
    left = [jnp.where(first, up[t - 1] if t else 0.0, up[t]) for t in range(len(centre))]
    right = [
        jnp.where(last, down[t + 1] if t + 1 < len(centre) else 0.0, down[t])
        for t in range(len(centre))
    ]
    return [left, right]


def around(ref, plane, row, sides):
    centre = load_rows(ref, plane, row)
    beside = lane_sides(centre)
    beside += [load_rows(ref, plane, row, 1), load_rows(ref, plane, row, -1)]
    beside += [load_rows(ref, plane + side, row) for side in sides]
    return centre, beside


def face_totals(coef, beside):
    result = each(lambda c, s: c + s, coef, beside[0])
    for side in beside[1:]:
        result = each(lambda r, c, s: r + (c + s), result, coef, side)
    return result


def stencil(coefs, fields, row, coef_plane, field_plane, sides):
    coef, coef_beside = around(coefs, coef_plane, row, sides)
    here, beside = around(fields, field_plane, row, sides)
    weights = [each(lambda c, s: c + s, coef, side) for side in coef_beside]
    twice = weights[0]
    gathered = each(lambda w, v: w * v, weights[0], beside[0])
    for weight, side in zip(weights[1:], beside[1:]):
        twice = each(lambda a, b: a + b, twice, weight)
        gathered = each(lambda a, w, v: a + w * v, gathered, weight, side)
    return twice, gathered, here, coef


def first_of(rhs, twice):
    return each(lambda b, d: (2.0 * OMEGA) * b / d, rhs, twice)


def smoothed_of(rhs, twice, gathered, here):
    return each(
        lambda b, d, g, v: (1.0 - OMEGA) * v + ((2.0 * OMEGA) * b + OMEGA * g) / d,
        rhs, twice, gathered, here,
    )


def residual_of(rhs, twice, gathered, here):
    return each(lambda b, d, g, v: b - 0.5 * (d * v - g), rhs, twice, gathered, here)


def total(values):
    result = values[0]
    for value in values[1:]:
        result = result + value
    return result


def sweep(size, body):
    def step(index, carry):
        for store, ref, plane, row, values in body(pl.multiple_of(index * ROWS, ROWS)):
            store(ref, plane, row, values)
        return carry

    lax.fori_loop(0, size // ROWS, step, 0, unroll=UNROLL)


def thin_rows(tiles, plane, start, count):
    parts = []
    for tile in range(tiles.shape[1]):
        parts.append(
            0.25 * tiles[plane, tile, pl.ds(PAD - 1 + start, count, stride=2), :]
            + 0.5 * tiles[plane, tile, pl.ds(PAD + start, count, stride=2), :]
            + 0.25 * tiles[plane, tile, pl.ds(PAD + 1 + start, count, stride=2), :]
        )
    return jnp.concatenate(parts, axis=1)


def restrict_plane(tiles, plane, size, matrix):
    return project(thin_rows(tiles, plane, 0, size // 2), matrix)


def project(rows, matrix):
    high = rows.astype(BF16)
    rest = rows - high.astype(F32)
    middle = rest.astype(BF16)
    low = (rest - middle.astype(F32)).astype(BF16)
    return (
        jnp.dot(low, matrix, preferred_element_type=F32)
        + jnp.dot(middle, matrix, preferred_element_type=F32)
        + jnp.dot(high, matrix, preferred_element_type=F32)
    )


def plane_at(core, place):
    return place + core * (3 - 2 * place)


def first_inner(scalars, coef, rhs, first, partial, c, b, f, g, sems):
    core = scalars[0]
    size = coef.shape[1]
    go = Copies(sems)
    waits = [go.tiles(coef.at[plane_at(core, q)], c.at[q]) for q in (0, 1)]
    later = [[go.tiles(coef.at[plane_at(core, 2)], c.at[2])]]
    later[0].append(go.start(rhs.at[plane_at(core, 1)], b.at[0]))
    later.append([go.tiles(coef.at[plane_at(core, 3)], c.at[3])])
    later[1].append(go.start(rhs.at[plane_at(core, 2)], b.at[1]))
    clear_pads(c, size)
    for copy in waits:
        copy.wait()
    out = []

    def partial_plane(slot, q, side):
        def rows(row):
            coef_here, beside = around(c, q, row, (side,))
            twice = face_totals(coef_here, beside)
            return [(store_flat, g, slot, row, each(lambda d, v: d + v, twice, coef_here))]

        sweep(size, rows)
        out.append(go.start(g.at[slot], partial.at[slot]))

    def first_plane(q):
        def rows(row):
            twice = face_totals(*around(c, q, row, (-1, 1)))
            return [(store_flat, f, q - 1, row, first_of(load_flat(b, q - 1, row), twice))]

        sweep(size, rows)
        out.append(go.start(f.at[q - 1], first.at[q - 1]))

    partial_plane(0, 0, 1)
    for copy in later[0]:
        copy.wait()
    first_plane(1)
    for copy in later[1]:
        copy.wait()
    first_plane(2)
    partial_plane(1, 3, -1)
    for copy in out:
        copy.wait()


def first_rim(scalars, rhs, partial, coef_outer, coef_sibling, outer, sibling, b, g, h, f, sems):
    core = scalars[0]
    size = rhs.shape[1]
    go = Copies(sems)
    loads = []
    for slot, q, halo in ((0, 0, coef_outer), (1, 3, coef_sibling)):
        loads.append(
            [
                go.start(rhs.at[plane_at(core, q)], b.at[slot]),
                go.start(partial.at[slot], g.at[slot]),
                go.start(halo, h.at[slot]),
            ]
        )
    out = []
    for slot, target in ((0, outer), (1, sibling)):
        for copy in loads[slot]:
            copy.wait()

        def rows(row):
            twice = each(lambda g, h: g + h, load_flat(g, slot, row), load_flat(h, slot, row))
            return [(store_flat, f, slot, row, first_of(load_flat(b, slot, row), twice))]

        sweep(size, rows)
        out.append(go.start(f.at[slot], target))
    for copy in out:
        copy.wait()


def loads_in_order(go, core, coef, rhs, coef_outer, coef_sibling, sources, c, v, b):
    def coef_in(q):
        if q == 0:
            return go.tiles(coef_outer, c.at[0])
        if q == 5:
            return go.tiles(coef_sibling, c.at[5])
        return go.tiles(coef.at[plane_at(core, q - 1)], c.at[q])

    def field_in(q):
        return go.tiles(sources[q - 1], v.at[q])

    def rhs_in(q):
        return go.start(rhs.at[plane_at(core, q - 1)], b.at[q - 1])

    waits = [[coef_in(0), coef_in(1), coef_in(2), field_in(1), field_in(2), rhs_in(1)]]
    waits.append([coef_in(3), field_in(3), rhs_in(2)])
    waits.append([coef_in(4), field_in(4), rhs_in(3)])
    waits.append([coef_in(5), rhs_in(4)])
    return waits


def smooth_inner(
    scalars, coef, rhs, coef_outer, coef_sibling, first, first_outer, first_sibling,
    smooth, known, factor, c, v, b, s, g, h, sems,
):
    core = scalars[0]
    size = coef.shape[1]
    go = Copies(sems)
    sources = (first_outer, first.at[0], first.at[1], first_sibling)
    waits = loads_in_order(go, core, coef, rhs, coef_outer, coef_sibling, sources, c, v, b)
    clear_pads(c, size)
    clear_pads(v, size)
    out = []

    def rim(slot, q, side):
        def rows(row):
            twice, gathered, here, coef_here = stencil(c, v, row, q, q, (side,))
            edge = each(lambda c, h: c + h, coef_here, load_rows(c, q - side, row))
            twice = each(lambda d, e: d + e, twice, edge)
            scale = [1.0 / value for value in twice]
            known_rows = each(
                lambda b, d, g, v: (1.0 - OMEGA) * v + ((2.0 * OMEGA) * b + OMEGA * g) * d,
                load_flat(b, q - 1, row), scale, gathered, here,
            )
            factor_rows = each(lambda d, e: (OMEGA * e) * d, scale, edge)
            return [(store_flat, g, slot, row, known_rows), (store_flat, h, slot, row, factor_rows)]

        sweep(size, rows)
        out.append(go.start(g.at[slot], known.at[slot]))
        out.append(go.start(h.at[slot], factor.at[slot]))

    def middle(q):
        def rows(row):
            twice, gathered, here, _ = stencil(c, v, row, q, q, (-1, 1))
            values = smoothed_of(load_flat(b, q - 1, row), twice, gathered, here)
            return [(store_flat, s, q - 2, row, values)]

        sweep(size, rows)
        out.append(go.start(s.at[q - 2], smooth.at[plane_at(core, q - 1)]))

    steps = ((rim, (0, 1, 1)), (middle, (2,)), (middle, (3,)), (rim, (1, 4, -1)))
    for needed, (work, arguments) in zip(waits, steps):
        for copy in needed:
            copy.wait()
        work(*arguments)
    for copy in out:
        copy.wait()


def smooth_rim(
    scalars, started, known, factor, halo_outer, halo_sibling,
    smooth, outer, sibling, g, h, v, s, sems,
):
    core = scalars[0]
    size = known.shape[1]
    go = Copies(sems)
    loads = []
    for slot, halo in ((0, halo_outer), (1, halo_sibling)):
        loads.append(
            [
                go.start(known.at[slot], g.at[slot]),
                go.start(factor.at[slot], h.at[slot]),
                go.start(halo, v.at[slot]),
            ]
        )
    out = []
    for slot, q, target in ((0, 0, outer), (1, 3, sibling)):
        for copy in loads[slot]:
            copy.wait()

        def rows(row):
            flat = [load_flat(ref, slot, row) for ref in (g, h, v)]
            return [(store_flat, s, slot, row, each(lambda g, h, v: g + h * v, *flat))]

        sweep(size, rows)
        out.append(go.start(s.at[slot], target))
        out.append(go.start(s.at[slot], smooth.at[plane_at(core, q)]))
    for copy in out:
        copy.wait()


def residual_inner(
    scalars, coef, rhs, coef_outer, coef_sibling, smooth, smooth_outer, smooth_sibling, matrix,
    lowered, known, factor, c, v, b, g, h, t, low, mat, sems,
):
    core = scalars[0]
    size = coef.shape[1]
    go = Copies(sems)
    sources = (
        smooth_outer, smooth.at[plane_at(core, 1)], smooth.at[plane_at(core, 2)], smooth_sibling,
    )
    waits = loads_in_order(go, core, coef, rhs, coef_outer, coef_sibling, sources, c, v, b)
    waits[0].append(go.start(matrix, mat))
    clear_pads(c, size)
    clear_pads(v, size)
    clear_top(t)
    out = []

    def rim(slot, q, side):
        def rows(row):
            twice, gathered, here, coef_here = stencil(c, v, row, q, q, (side,))
            edge = each(lambda c, h: c + h, coef_here, load_rows(c, q - side, row))
            twice = each(lambda d, e: d + e, twice, edge)
            known_rows = residual_of(load_flat(b, q - 1, row), twice, gathered, here)
            factor_rows = [0.5 * value for value in edge]
            return [(store_flat, g, slot, row, known_rows), (store_flat, h, slot, row, factor_rows)]

        sweep(size, rows)
        out.append(go.start(g.at[slot], known.at[slot]))
        out.append(go.start(h.at[slot], factor.at[slot]))

    def middle(q):
        def rows(row):
            twice, gathered, here, _ = stencil(c, v, row, q, q, (-1, 1))
            values = residual_of(load_flat(b, q - 1, row), twice, gathered, here)
            return [(store_rows, t, q - 2, row, values)]

        sweep(size, rows)
        low[q - 2] = restrict_plane(t, q - 2, size, mat[...])

    steps = ((rim, (0, 1, 1)), (middle, (2,)), (middle, (3,)), (rim, (1, 4, -1)))
    for needed, (work, arguments) in zip(waits, steps):
        for copy in needed:
            copy.wait()
        work(*arguments)
    out.append(go.start(low, lowered))
    for copy in out:
        copy.wait()


def residual_rim(
    scalars, known, factor, halo_outer, halo_sibling, lowered, matrix,
    packed, g, h, v, t, low, pack, mat, sems,
):
    core = scalars[0]
    size = known.shape[1]
    go = Copies(sems)
    loads = []
    for slot, halo in ((0, halo_outer), (1, halo_sibling)):
        loads.append(
            [
                go.start(known.at[slot], g.at[slot]),
                go.start(factor.at[slot], h.at[slot]),
                go.start(halo, v.at[slot]),
            ]
        )
    more = [go.start(lowered, low.at[pl.ds(1, 2)]), go.start(matrix, mat)]
    clear_top(t)
    for copy in more:
        copy.wait()
    for slot in (0, 1):
        for copy in loads[slot]:
            copy.wait()

        def rows(row):
            flat = [load_flat(ref, slot, row) for ref in (g, h, v)]
            return [(store_rows, t, slot, row, each(lambda g, h, v: g + h * v, *flat))]

        sweep(size, rows)
        low[3 * slot] = restrict_plane(t, slot, size, mat[...])
    one = plane_at(core, 1)
    two = plane_at(core, 2)
    last = low[plane_at(core, 3)]
    pack[0] = 2.0 * low[plane_at(core, 0)] + low[one]
    pack[1] = low[one] + 2.0 * low[two] + last
    pack[2] = last
    copy = go.start(pack, packed)
    copy.wait()


def guarded(values):
    return [jnp.where(value == 0.0, 1.0, value) for value in values]


def first_wide(c, b, f, planes, size):
    def plane(q):
        def rows(row):
            twice = guarded(face_totals(*around(c, q + 1, row, (-1, 1))))
            return [(store_rows, f, q, row, first_of(load_flat(b, q, row), twice))]

        sweep(size, rows)

    pl.loop(0, planes)(plane)


def smooth_wide(c, b, f, s, planes, size, inside):
    def plane(q):
        keep = inside(q)

        def rows(row):
            twice, gathered, here, _ = stencil(c, f, row, q + 2, q + 1, (-1, 1))
            values = smoothed_of(load_flat(b, q + 1, row), guarded(twice), gathered, here)
            return [(store_rows, s, q, row, [jnp.where(keep, value, 0.0) for value in values])]

        sweep(size, rows)

    pl.loop(0, planes)(plane)


def residual_wide(c, b, s, t, planes, size):
    for q in range(planes):

        def rows(row):
            twice, gathered, here, _ = stencil(c, s, row, q + 3, q + 1, (-1, 1))
            values = residual_of(load_flat(b, q + 2, row), twice, gathered, here)
            return [(store_rows, t, q, row, values)]

        sweep(size, rows)


def middle_level(
    scalars, own, sibling, outer, before, coef, coef_sibling, coef_outer, coef_before, coef_after,
    matrix, smooth, packed, m, b, c, f, s, t, pack, mat, sems,
):
    core = scalars[0]
    place = scalars[1]
    final = scalars[2]
    size = coef.shape[1]
    even = core == 0
    go = Copies(sems)
    loads = [
        go.start(own, m.at[pl.ds(3, 3)]),
        go.choose(even, outer, sibling, m.at[pl.ds(0, 3)]),
        go.choose(even, sibling, outer, m.at[pl.ds(6, 3)]),
        go.start(before, m.at[9]),
        go.tiles(coef_before.at[pl.ds(0, size)], c.at[0]),
        go.tiles(coef_after.at[pl.ds(0, size)], c.at[7]),
        go.start(matrix, mat),
    ]
    for q in range(2):
        part = pl.ds(q * size, size)
        loads.append(go.tiles(coef.at[q], c.at[3 + q]))
        for tile in range(size // LANES):
            outer_part = coef_outer.at[part, columns(tile)]
            sibling_part = coef_sibling.at[part, columns(tile)]
            left = c.at[1 + q, tile, pl.ds(PAD, size), :]
            right = c.at[5 + q, tile, pl.ds(PAD, size), :]
            loads.append(go.choose(even, outer_part, sibling_part, left))
            loads.append(go.choose(even, sibling_part, outer_part, right))
    clear_pads(c, size)
    clear_pads(f, size)
    clear_pads(s, size)
    clear_top(t)
    for copy in loads:
        copy.wait()

    def rows(row):
        part = pl.ds(row, ROWS)
        values = [
            m[0, part, :] + m[9, part, :],
            m[1, part, :],
            m[3, part, :] + m[2, part, :],
            m[4, part, :],
            jnp.where(place < final, m[6, part, :] + m[5, part, :], 0.0),
            m[7, part, :],
        ]
        return [(store_whole, b, q, row, value) for q, value in enumerate(values)]

    sweep(size, rows)
    first_wide(c, b, f, 6, size)
    lowest = jnp.where(place > 0, 0, 1)
    highest = jnp.where(place < final, 3, 2)
    smooth_wide(c, b, f, s, 4, size, lambda q: jnp.logical_and(q >= lowest, q <= highest))
    out = [go.untiled(s.at[1 + q], smooth.at[q]) for q in range(2)]
    residual_wide(c, b, s, t, 2, size)
    low = restrict_plane(t, 1, size, mat[...])
    pack[0] = 2.0 * restrict_plane(t, 0, size, mat[...]) + low
    pack[1] = low
    out.append(go.start(pack, packed))
    for copy in out:
        copy.wait()


def last_level(
    scalars, own, sibling, outer, before, after, rim, coef, coef_sibling, coef_outer, coef_before,
    coef_after, matrices, smooth, copies, m, b, c, f, s, t, w, mat, sems,
):
    core = scalars[0]
    place = scalars[1]
    final = scalars[2]
    size = coef.shape[1]
    half = size // 2
    base = 4 * size
    even = core == 0
    go = Copies(sems)
    loads = [
        go.start(before, m.at[pl.ds(0, 2)]),
        go.choose(even, outer, sibling, m.at[pl.ds(2, 2)]),
        go.start(own, m.at[pl.ds(4, 2)]),
        go.choose(even, sibling, outer, m.at[pl.ds(6, 2)]),
        go.start(after, m.at[pl.ds(8, 2)]),
        go.start(rim, m.at[10]),
        go.tiles(coef.at[0], c.at[3]),
        go.start(matrices, mat),
    ]
    for part in range(2):
        target = pl.ds(PAD + part * half, half)
        lanes = pl.ds(part * size, size)
        outer_part = coef_outer.at[pl.ds(base, half), lanes]
        sibling_part = coef_sibling.at[pl.ds(base, half), lanes]
        loads.append(go.choose(even, outer_part, sibling_part, c.at[2, 0, target, :]))
        loads.append(go.choose(even, sibling_part, outer_part, c.at[4, 0, target, :]))
        for source, nearer, farther in ((coef_before, 1, 0), (coef_after, 5, 6)):
            loads.append(go.start(source.at[pl.ds(2 * size, half), lanes], c.at[nearer, 0, target, :]))
            loads.append(
                go.start(source.at[pl.ds(2 * size + half, half), lanes], c.at[farther, 0, target, :])
            )
    clear_pads(c, size)
    clear_pads(f, size)
    clear_pads(s, size)
    clear_top(t)
    for copy in loads:
        copy.wait()

    def rows(row):
        part = pl.ds(row, ROWS)
        values = [
            m[0, part, :] + m[10, part, :],
            m[2, part, :] + m[1, part, :],
            m[4, part, :] + m[3, part, :],
            jnp.where(place < final, m[6, part, :] + m[5, part, :], 0.0),
            jnp.where(place < final - 1, m[8, part, :] + m[7, part, :], 0.0),
        ]
        return [(store_whole, b, q, row, value) for q, value in enumerate(values)]

    sweep(size, rows)
    first_wide(c, b, f, 5, size)
    lowest = jnp.where(place > 0, 0, 1)
    highest = jnp.where(place < final, 2, 1)
    smooth_wide(c, b, f, s, 3, size, lambda q: jnp.logical_and(q >= lowest, q <= highest))
    out = [go.untiled(s.at[1], smooth.at[0])]
    residual_wide(c, b, s, t, 1, size)
    top = thin_rows(t, 0, 0, size // 4)
    bottom = thin_rows(t, 0, half, size // 4)
    result = project(top, mat[0]) + project(bottom, mat[1])
    w[...] = jnp.broadcast_to(result[None], w.shape)
    out.append(go.start(w, copies))
    for copy in out:
        copy.wait()


def coarse_level(scalars, own, sibling, coef, solution, e, o, c, w, p0, p1, g, y, sems):
    core = scalars[0]
    even = core == 0
    half, size, lanes = coef.shape
    go = Copies(sems)
    loads = [
        go.start(coef, c.at[pl.ds(1, half)]),
        go.choose(even, own, sibling, e),
        go.choose(even, sibling, own, o.at[pl.ds(1, 2 * half)]),
    ]
    o[0] = jnp.zeros(o.shape[1:], F32)
    loads[0].wait()
    lane = lax.broadcasted_iota(jnp.int32, (size, lanes), 1)
    row = lax.broadcasted_iota(jnp.int32, (size, lanes), 0)
    upper = lane >= size
    low_edge = (lane % size) == 0
    high_edge = (lane % size) == size - 1
    c[0] = jnp.where(upper, pltpu.roll(c[half], size, 1), 0.0)
    c[half + 1] = jnp.where(upper, 0.0, pltpu.roll(c[1], size, 1))

    edges = [row == size - 1, row == 0, high_edge, low_edge]
    for copy in loads[1:]:
        copy.wait()
    short = lax.broadcasted_iota(jnp.int32, (size // 2, lanes), 1) >= size

    def prepare(q, carry):
        here = c[q + 1]
        sides = [
            pltpu.roll(here, size - 1, 0), pltpu.roll(here, 1, 0),
            pltpu.roll(here, lanes - 1, 1), pltpu.roll(here, 1, 1),
        ]
        sides = [jnp.where(edge, 0.0, value) for edge, value in zip(edges, sides)]
        sides += [c[q], c[q + 2]]
        inverse = 1.0 / (3.0 * here + 0.5 * total(sides))
        scaled = 0.5 * inverse
        for d, side in enumerate(sides):
            weight = (here + side) * scaled
            if d < 4:
                weight = jnp.where(edges[d], 0.0, weight)
            elif d == 4:
                weight = jnp.where(jnp.logical_and(q == 0, jnp.logical_not(upper)), 0.0, weight)
            else:
                weight = jnp.where(jnp.logical_and(q == half - 1, upper), 0.0, weight)
            w[d, q] = weight
        lower_rhs = o[q] + 2.0 * e[q] + o[q + 1]
        upper_rhs = o[q + half] + 2.0 * e[q + half] + o[q + half + 1]
        top = jnp.where(short, pltpu.roll(upper_rhs, size, 1), lower_rhs)
        bottom = jnp.where(short, upper_rhs, pltpu.roll(lower_rhs, size, 1))
        scaled_rhs = jnp.concatenate([top, bottom], axis=0) * inverse
        g[q] = scaled_rhs
        p1[q + 1, PAD : PAD + size] = scaled_rhs * (1.0 / CENTER_VALUE)
        p0[q + 1, PAD : PAD + size] = jnp.zeros((size, lanes), F32)
        return carry

    zeros = jnp.zeros((half + 2, PAD, lanes), F32)
    for p in (p0, p1):
        p[:, :PAD] = zeros
        p[:, PAD + size :] = zeros
    lax.fori_loop(0, half, prepare, 0, unroll=4)
    sigma = CENTER_VALUE / HALF_WIDTH
    rho = 1.0 / sigma
    block = pl.ds(PAD, size)
    for index in range(CHEB - 1):
        older, now = (p0, p1) if index % 2 == 0 else (p1, p0)
        now[0, block] = pltpu.roll(now[half, block], size, 1)
        now[half + 1, block] = pltpu.roll(now[1, block], size, 1)
        rho_new = 1.0 / (2.0 * sigma - rho)
        keep = rho_new * rho
        gain = 2.0 * rho_new / HALF_WIDTH
        rho = rho_new
        final = index == CHEB - 2

        def advance(q, carry):
            values = []
            for start in range(0, size, ROWS):
                part = pl.ds(PAD + start, ROWS)
                flat = pl.ds(start, ROWS)
                here = now[q + 1, part]
                sides = [
                    now[q + 1, pl.ds(PAD + start + 1, ROWS)],
                    now[q + 1, pl.ds(PAD + start - 1, ROWS)],
                    pltpu.roll(here, lanes - 1, 1), pltpu.roll(here, 1, 1),
                    now[q, part], now[q + 2, part],
                ]
                near = total([w[d, q, flat] * side for d, side in enumerate(sides)])
                remains = (g[q, flat] - here) + near
                values.append(here + keep * (here - older[q + 1, part]) + gain * remains)
            for index, value in enumerate(values):
                start = index * ROWS
                if final:
                    flat = pl.ds(start, ROWS)
                    y[q, flat] = value[:, :size]
                    y[q + half, flat] = pltpu.roll(value, size, 1)[:, :size]
                else:
                    older[q + 1, pl.ds(PAD + start, ROWS)] = value
            return carry

        lax.fori_loop(0, half, advance, 0, unroll=UNROLL)
    copy = go.start(y, solution)
    copy.wait()


def vm(*dims):
    return pltpu.VMEM(dims, F32)


def tiled(planes, size):
    return vm(planes, size // LANES, size + 2 * PAD, LANES)


def swapped(value, pairs):
    return lax.ppermute(value, "box", pairs)


def local(rhs_fine, coef_zero, coef_one, coef_two, coef_three):
    count = lax.axis_size("box")
    place = lax.axis_index("box")
    core = place % 2
    scalars = jnp.stack([core, place, jnp.int32(count - 1)]).astype(jnp.int32)
    near = [(i, i ^ 1) for i in range(count)]
    far = [(i, i + 1) for i in range(1, count - 1, 2)]
    far = far + [(j, i) for i, j in far]

    def onward(value, distance):
        route = [(i, i + distance) for i in range(count) if 0 <= i + distance < count]
        return lax.ppermute(value, "box", route)

    n = coef_zero.shape[1]
    n1, n2 = n // 2, n // 4
    n3 = n // 8
    plane = n * n * 4
    matrix0 = jnp.asarray(restriction_matrix(n, n1, 0), BF16)
    matrix1 = jnp.asarray(restriction_matrix(n1, n2, 0), BF16)
    both = np.stack([restriction_matrix(n2, 2 * n3, 0), restriction_matrix(n2, 2 * n3, n3)])
    matrix2 = jnp.asarray(both, BF16)

    def side_plane(field, where):
        return lax.dynamic_index_in_dim(field, where, 0, keepdims=False)

    coef_outer = swapped(side_plane(coef_zero, 3 * core), far)
    coef_sibling = swapped(side_plane(coef_zero, 3 - 3 * core), near)
    first, partial = call(
        first_inner, [shape(2, n, n), shape(2, n, n)],
        [tiled(4, n), vm(2, n, n), vm(2, n, n), vm(2, n, n)], 24, 40 * n * n, 12 * plane, 32,
    )(scalars, coef_zero, rhs_fine)
    first_outer, first_sibling = call(
        first_rim, [shape(n, n), shape(n, n)],
        [vm(2, n, n)] * 4, 8, 10 * n * n, 8 * plane, 32,
    )(scalars, rhs_fine, partial, coef_outer, coef_sibling)

    halo_outer = swapped(first_outer, far)
    halo_sibling = swapped(first_sibling, near)
    smooth, known, factor = call(
        smooth_inner, [shape(4, n, n), shape(2, n, n), shape(2, n, n)],
        [tiled(6, n), tiled(6, n), vm(4, n, n), vm(2, n, n), vm(2, n, n), vm(2, n, n)],
        54, 160 * n * n, 20 * plane, 32,
    )(scalars, coef_zero, rhs_fine, coef_outer, coef_sibling, first, first_outer, first_sibling)
    def folded(field):
        return jnp.concatenate([field[: n2 // 2], field[n2 // 2 :]], axis=1)

    own_two = folded(coef_two[0])
    coefs = jnp.concatenate([coef_one[0], coef_one[1], own_two], axis=0)
    coefs_sibling = swapped(coefs, near)
    coefs_outer = swapped(coefs, far)
    known, coefs_sibling, coefs_outer = lax.optimization_barrier(
        (known, coefs_sibling, coefs_outer)
    )
    smooth_zero, smooth_outer, smooth_sibling = call(
        smooth_rim, [shape(4, n, n), shape(n, n), shape(n, n)],
        [vm(2, n, n)] * 4, 10, 4 * n * n, 10 * plane, 32, {1: 0},
    )(scalars, smooth, known, factor, halo_outer, halo_sibling)

    halo_outer = swapped(smooth_outer, far)
    halo_sibling = swapped(smooth_sibling, near)

    lowered, known, factor = call(
        residual_inner, [shape(2, n1, n1), shape(2, n, n), shape(2, n, n)],
        [tiled(6, n), tiled(6, n), vm(4, n, n), vm(2, n, n), vm(2, n, n),
         tiled(2, n), vm(2, n1, n1), pltpu.VMEM((n, n1), BF16)],
        54, 160 * n * n, 20 * plane, 32,
    )(scalars, coef_zero, rhs_fine, coef_outer, coef_sibling, smooth_zero, smooth_outer,
      smooth_sibling, matrix0)
    left_two = jnp.where(core == 0, coefs_outer[2 * n1 :], coefs_sibling[2 * n1 :])
    right_two = jnp.where(core == 0, coefs_sibling[2 * n1 :], coefs_outer[2 * n1 :])
    coefs_before = onward(jnp.concatenate([coef_one[1], own_two, left_two], axis=0), 2)
    coefs_after = onward(jnp.concatenate([coef_one[0], own_two, right_two], axis=0), -2)
    lowered, coefs_before, coefs_after = lax.optimization_barrier(
        (lowered, coefs_before, coefs_after)
    )
    (packed,) = call(
        residual_rim, [shape(3, n1, n1)],
        [vm(2, n, n), vm(2, n, n), vm(2, n, n), tiled(2, n), vm(4, n1, n1), vm(3, n1, n1),
         pltpu.VMEM((n, n1), BF16)],
        10, 20 * n * n, 8 * plane, 32,
    )(scalars, known, factor, halo_outer, halo_sibling, lowered, matrix0)

    packed_outer = swapped(packed, far)
    packed_before = onward(packed[2], 2)
    packed_sibling = swapped(packed, near)
    smooth_one, packed = call(
        middle_level, [shape(2, n1, n1), shape(2, n2, n2)],
        [vm(10, n1, n1), vm(6, n1, n1), tiled(8, n1), tiled(6, n1),
         tiled(4, n1), tiled(2, n1), vm(2, n2, n2), pltpu.VMEM((n1, n2), BF16)],
        40, 400 * n1 * n1, 24 * n1 * n1 * 4, 40,
    )(scalars, packed, packed_sibling, packed_outer, packed_before, coef_one, coefs_sibling,
      coefs_outer, coefs_before, coefs_after, matrix1)

    packed_outer = swapped(packed, far)
    packed_before = onward(packed, 2)
    packed_after = onward(packed, -2)
    packed_rim = onward(packed[1], 3)
    packed_sibling = swapped(packed, near)
    groups = [[i for i in range(count) if i % 2 == r] for r in range(2)]
    smooth_two, copies = call(
        last_level, [shape(1, n2, n2), shape(count // 2, n3 // 2, 2 * n3)],
        [vm(11, n2, n2), vm(5, n2, n2), tiled(7, n2), tiled(5, n2),
         tiled(3, n2), tiled(1, n2), vm(count // 2, n3 // 2, 2 * n3),
         pltpu.VMEM((2, n2, 2 * n3), BF16)],
        24, 300 * n2 * n2, 40 * n2 * n2 * 4, 40,
    )(scalars, packed, packed_sibling, packed_outer, packed_before, packed_after, packed_rim,
      coef_two, coefs_sibling, coefs_outer, coefs_before, coefs_after, matrix2)

    gathered = lax.all_to_all(copies, "box", 0, 0, tiled=True, axis_index_groups=groups)
    gathered_sibling = swapped(gathered, near)
    half = n3 // 2
    coef_pair = jnp.concatenate([coef_three[:half], coef_three[half:]], axis=2)
    (coarse_solution,) = call(
        coarse_level, [shape(n3, n3, n3)],
        [vm(n3, half, 2 * n3), vm(n3 + 1, half, 2 * n3), vm(half + 2, n3, 2 * n3),
         vm(6, half, n3, 2 * n3), vm(half + 2, n3 + 16, 2 * n3), vm(half + 2, n3 + 16, 2 * n3), vm(half, n3, 2 * n3),
         vm(n3, n3, n3)],
        4, 300 * n3 * n3 * n3, 20 * n3 * n3 * n3, 48,
    )(scalars, gathered, gathered_sibling, coef_pair)
    return (smooth_zero, smooth_one, smooth_two, coarse_solution)


def solution(mesh):
    placed = (
        P("box", None, None),
        P("box", None, None),
        P("box", None, None),
        P("box", None, None),
        P(),
    )
    return jax.shard_map(
        local,
        mesh=mesh,
        in_specs=placed,
        out_specs=(P("box", None, None), P("box", None, None), P("box", None, None), P()),
        check_vma=False,
    )
```

time: 249 us -> 200 us (0.80)
  Pallas kernels: 130 us -> 64.5 us
  starting transfers between devices: 43.9 us -> 52.7 us
  waiting for transfers between devices: 17.3 us -> 22 us
  blocking collectives: 41.6 us -> 46 us
    pallas_call x9, Pallas kernels: 130 us -> 64.5 us  [run(): pl.pallas_call(body, out_shape=outs, in_specs=[pl.BlockSpec(memory_space=...]
    ppermute x13, waiting for transfers between devices: 1.71 us -> 12.2 us  [swapped(): return lax.ppermute(value, 'box', pairs)]
    ppermute x6, waiting for transfers between devices: 15.6 us -> 9.73 us  [onward(): return lax.ppermute(value, 'box', route)]
    ppermute x6, starting transfers between devices: 18.6 us -> 23.3 us  [onward(): return lax.ppermute(value, 'box', route)]
    all_to_all x1, blocking collectives: 41.6 us -> 46 us  [local(): lax.all_to_all(copies, 'box', 0, 0, tiled=True, axis_index_groups=groups)]
    ppermute x13, starting transfers between devices: 25.3 us -> 29.4 us  [swapped(): return lax.ppermute(value, 'box', pairs)]
    unnamed x46 -> x36, local copies, waits for them, and re-layouts: 10.7 us -> 8.82 us
  transfers between devices with their start and end apart: 19 -> 19, of which waited for: 4 -> 5; matrix products, arithmetic and copies ran while one was open for 1% -> 1% of each run, Pallas kernels for 24% -> 12%
where the time goes in v2:
time: 200 us; the launch traced here: 199 us
  Pallas kernels  64.5 us (32%)
  starting transfers between devices  52.7 us (26%)
  blocking collectives  46 us (23%)
  waiting for transfers between devices  22 us (11%)
  local copies, waits for them, and re-layouts  11 us (6%)
    pallas_call x9, Pallas kernels, run(): pl.pallas_call(body, out_shape=outs, in_specs=[pl.BlockSpec(memory_space=...  64.5 us
    all_to_all x1, blocking collectives, local(): lax.all_to_all(copies, 'box', 0, 0, tiled=True, axis_index_groups=groups)  46 us
    ppermute x13, starting transfers between devices, swapped(): return lax.ppermute(value, 'box', pairs)  29.4 us
    ppermute x6, starting transfers between devices, onward(): return lax.ppermute(value, 'box', route)  23.3 us
    ppermute x13, waiting for transfers between devices, swapped(): return lax.ppermute(value, 'box', pairs)  12.2 us
    ppermute x6, waiting for transfers between devices, onward(): return lax.ppermute(value, 'box', route)  9.73 us
    unnamed x36, local copies, waits for them, and re-layouts  8.82 us
  transfers between devices with their start and end apart: 19, of which 5 were waited for; matrix products, arithmetic and copies ran while one was open for 1% of the time, Pallas kernels for 12%

profile of v2, /device:TPU:1, one launch (start us, length us, event | category | flops | bytes accessed | tf_op | source)
XLA Modules:
  0.0 199.1 jit_solution(1032699134415083812)
XLA Ops:
  2.5 4.5 %collective-permute-start = (f32[512,512]{1,0:T(8,128)S(1)}, f32[512,512]{1,0:T(8,128)S(1)}, u32[]{:S(2)}, u32[]{:S(2)}) collective-permute-start(f32[512,512]{1,0:T(8,128)S(1)} %get-tuple-element.51), channel_id=1, source_target_pairs={{1,2},{3,4},{5,6},{7,8},{9,10},{11,12},{13,14},{15,16},{17,18},{19... | collective-permute-start | bytes 3145736 | tf_op jit(solution)/shard_map/ppermute | solution.py:791
  7.2 2.2 %copy-done.2 = f32[4,512,512]{2,1,0:T(8,128)S(1)} copy-done((f32[4,512,512]{2,1,0:T(8,128)S(1)}, f32[4,512,512]{2,1,0:T(8,128)}, u32[]{:S(2)}) %copy-start.2) | copy-done | bytes 4194328
  9.4 5.2 %shard_map.111 = (f32[2,512,512]{2,1,0:T(8,128)S(1)}, f32[2,512,512]{2,1,0:T(8,128)S(1)}) custom-call(s32[3]{0:T(128)S(1)} %pad_add_fusion.scalars, f32[4,512,512]{2,1,0:T(8,128)S(1)} %copy-done.2, f32[4,512,512]{2,1,0:T(8,128)S(1)} %copy-done), custom_call_target="tpu_custom_call" | custom-call | flops 10485760 | bytes 12582912 | tf_op jit(solution)/shard_map/pallas_call | solution.py:39
  14.7 4.9 %collective-permute-done.coef_outer = f32[512,512]{1,0:T(8,128)S(1)} collective-permute-done((f32[512,512]{1,0:T(8,128)S(1)}, f32[512,512]{1,0:T(8,128)S(1)}, u32[]{:S(2)}, u32[]{:S(2)}) %collective-permute-start) | collective-permute-done | bytes 1048608 | tf_op jit(solution)/shard_map/ppermute | solution.py:791
  21.2 3.6 %collective-permute-start.4 = (f32[512,512]{1,0:T(8,128)S(1)}, f32[512,512]{1,0:T(8,128)S(1)}, u32[]{:S(2)}, u32[]{:S(2)}) collective-permute-start(f32[512,512]{1,0:T(8,128)S(1)} %get-tuple-element.29.first_outer), channel_id=1, source_target_pairs={{1,2},{3,4},{5,6},{7,8},{9,10},{11,12},{13,14},{15,16},{17,18},{19... | collective-permute-start | bytes 3145736 | tf_op jit(solution)/shard_map/ppermute | solution.py:791
  25.7 3.0 %collective-permute-start.3 = (f32[576,256]{1,0:T(8,128)S(1)}, f32[576,256]{1,0:T(8,128)S(1)}, u32[]{:S(2)}, u32[]{:S(2)}) collective-permute-start(f32[576,256]{1,0:T(8,128)S(1)} %maximum_maximum_fusion), channel_id=1, source_target_pairs={{1,2},{3,4},{5,6},{7,8},{9,10},{11,12},{13,14},{15,16},{17,18},{19... | collective-permute-start | bytes 1769480 | tf_op jit(solution)/shard_map/ppermute | solution.py:791
  28.8 9.2 %shard_map.113 = (f32[4,512,512]{2,1,0:T(8,128)}, f32[2,512,512]{2,1,0:T(8,128)S(1)}, f32[2,512,512]{2,1,0:T(8,128)S(1)}) custom-call(s32[3]{0:T(128)S(1)} %pad_add_fusion.scalars, f32[4,512,512]{2,1,0:T(8,128)S(1)} %copy-done.3, f32[4,512,512]{2,1,0:T(8,128)S(1)} %copy-done, f32[512,512]{1,0:T(8,128)S(1)} %collective-permute-done.coef_outer, ...), custom_call_target="tpu_custom_call" | custom-call | flops 41943040 | bytes 20971520 | tf_op jit(solution)/shard_map/pallas_call | solution.py:39
  38.0 5.7 %collective-permute-done.3.coef_outer = f32[576,256]{1,0:T(8,128)S(1)} collective-permute-done((f32[576,256]{1,0:T(8,128)S(1)}, f32[576,256]{1,0:T(8,128)S(1)}, u32[]{:S(2)}, u32[]{:S(2)}) %collective-permute-start.3) | collective-permute-done | bytes 589856 | tf_op jit(solution)/shard_map/ppermute | solution.py:791
  43.7 3.3 %shard_map.114 = (f32[4,512,512]{2,1,0:T(8,128)}, f32[512,512]{1,0:T(8,128)}, f32[512,512]{1,0:T(8,128)}) custom-call(s32[3]{0:T(128)S(1)} %pad_add_fusion.scalars, f32[4,512,512]{2,1,0:T(8,128)} %get-tuple-element.31.started, f32[2,512,512]{2,1,0:T(8,128)S(1)} %get-tuple-element.33.known, ...), custom_call_target="tpu_custom_call", output_to_operand_aliasing={{0}: (1, {})} | custom-call | flops 1048576 | bytes 10485760 | tf_op jit(solution)/shard_map/pallas_call | solution.py:39
  46.9 3.6 %collective-permute-start.6 = (f32[512,512]{1,0:T(8,128)}, f32[512,512]{1,0:T(8,128)}, u32[]{:S(2)}, u32[]{:S(2)}) collective-permute-start(f32[512,512]{1,0:T(8,128)} %get-tuple-element.36.smooth_outer), channel_id=1, source_target_pairs={{1,2},{3,4},{5,6},{7,8},{9,10},{11,12},{13,14},{15,16},{17,18},{19... | collective-permute-start | bytes 3145736 | tf_op jit(solution)/shard_map/ppermute | solution.py:791
  51.8 3.1 %collective-permute-start.8 = (f32[384,256]{1,0:T(8,128)S(1)}, f32[384,256]{1,0:T(8,128)S(1)}, u32[]{:S(2)}, u32[]{:S(2)}) collective-permute-start(f32[384,256]{1,0:T(8,128)S(1)} %get-tuple-element.59), channel_id=1, source_target_pairs={{0,2},{1,3},{2,4},{3,5},{4,6},{5,7},{6,8},{7,9},{8,10},{9,11},{10,... | collective-permute-start | bytes 1179656 | tf_op jit(solution)/shard_map/ppermute | solution.py:805
  58.7 2.2 %copy-done.4 = f32[4,512,512]{2,1,0:T(8,128)S(1)} copy-done((f32[4,512,512]{2,1,0:T(8,128)S(1)}, f32[4,512,512]{2,1,0:T(8,128)}, u32[]{:S(2)}) %copy-start.4) | copy-done | bytes 4194328
  63.0 9.8 %shard_map.115 = (f32[2,256,256]{2,1,0:T(8,128)S(1)}, f32[2,512,512]{2,1,0:T(8,128)S(1)}, f32[2,512,512]{2,1,0:T(8,128)S(1)}) custom-call(s32[3]{0:T(128)S(1)} %pad_add_fusion.scalars, f32[4,512,512]{2,1,0:T(8,128)S(1)} %copy-done.4, f32[4,512,512]{2,1,0:T(8,128)S(1)} %copy-done.1, f32[512,512]{1,0:T(8,128)S(1)} %collective-permute-done.coef_outer, ...), custom_call_target="tpu_custom_call" | custom-call | flops 41943040 | bytes 20971520 | tf_op jit(solution)/shard_map/pallas_call | solution.py:39
  73.0 3.6 %shard_map.116.own = f32[3,256,256]{2,1,0:T(8,128)S(1)} custom-call(s32[3]{0:T(128)S(1)} %pad_add_fusion.scalars, f32[2,512,512]{2,1,0:T(8,128)S(1)} %get-tuple-element.38.known, f32[2,512,512]{2,1,0:T(8,128)S(1)} %get-tuple-element.39.factor, f32[512,512]{1,0:T(8,128)} %collective-permute-done.6.halo_outer, f32[512,512]{1,0:T(8,128)} %collective-permute-done.7.halo_sibling, ...), custom_call_target="tpu_custom_call" | custom-call | flops 5242880 | bytes 8388608 | tf_op jit(solution)/shard_map/pallas_call | solution.py:39
  77.4 4.2 %collective-permute-start.11 = (f32[3,256,256]{2,1,0:T(8,128)S(1)}, f32[3,256,256]{2,1,0:T(8,128)S(1)}, u32[]{:S(2)}, u32[]{:S(2)}) collective-permute-start(f32[3,256,256]{2,1,0:T(8,128)S(1)} %shard_map.116.own), channel_id=1, source_target_pairs={{1,2},{3,4},{5,6},{7,8},{9,10},{11,12},{13,14},{15,16},{17,18},{19... | collective-permute-start | bytes 2359304 | tf_op jit(solution)/shard_map/ppermute | solution.py:791
  81.6 6.6 %collective-permute-start.12 = (f32[256,256]{1,0:T(8,128)S(1)}, f32[256,256]{1,0:T(8,128)S(1)}, u32[]{:S(2)}, u32[]{:S(2)}) collective-permute-start(f32[256,256]{1,0:T(8,128)S(1)} %slice_bitcast_fusion), channel_id=1, source_target_pairs={{0,2},{1,3},{2,4},{3,5},{4,6},{5,7},{6,8},{7,9},{8,10},{9,11},{10,... | collective-permute-start | bytes 786440 | tf_op jit(solution)/shard_map/ppermute | solution.py:805
  88.3 7.8 %collective-permute-done.12.before = f32[256,256]{1,0:T(8,128)S(1)} collective-permute-done((f32[256,256]{1,0:T(8,128)S(1)}, f32[256,256]{1,0:T(8,128)S(1)}, u32[]{:S(2)}, u32[]{:S(2)}) %collective-permute-start.12) | collective-permute-done | bytes 262176 | tf_op jit(solution)/shard_map/ppermute | solution.py:805
  96.1 6.8 %shard_map.117 = (f32[2,256,256]{2,1,0:T(8,128)}, f32[2,128,128]{2,1,0:T(8,128)S(1)}) custom-call(s32[3]{0:T(128)S(1)} %pad_add_fusion.scalars, f32[3,256,256]{2,1,0:T(8,128)S(1)} %shard_map.116.own, f32[3,256,256]{2,1,0:T(8,128)S(1)} %collective-permute-done.10.sibling, f32[3,256,256]{2,1,0:T(8,128)S(1)} %collective-permute-done.11.outer, ...), custom_call_target="tpu_custom_call" | custom-call | flops 26214400 | bytes 6291456 | tf_op jit(solution)/shard_map/pallas_call | solution.py:39
  103.0 6.9 %collective-permute-start.14 = (f32[2,128,128]{2,1,0:T(8,128)S(1)}, f32[2,128,128]{2,1,0:T(8,128)S(1)}, u32[]{:S(2)}, u32[]{:S(2)}) collective-permute-start(f32[2,128,128]{2,1,0:T(8,128)S(1)} %get-tuple-element.47.own), channel_id=1, source_target_pairs={{1,2},{3,4},{5,6},{7,8},{9,10},{11,12},{13,14},{15,16},{17,18},{19... | collective-permute-start | bytes 393224 | tf_op jit(solution)/shard_map/ppermute | solution.py:791
  109.9 3.8 %collective-permute-start.15 = (f32[2,128,128]{2,1,0:T(8,128)S(1)}, f32[2,128,128]{2,1,0:T(8,128)S(1)}, u32[]{:S(2)}, u32[]{:S(2)}) collective-permute-start(f32[2,128,128]{2,1,0:T(8,128)S(1)} %get-tuple-element.47.own), channel_id=1, source_target_pairs={{0,2},{1,3},{2,4},{3,5},{4,6},{5,7},{6,8},{7,9},{8,10},{9,11},{10,... | collective-permute-start | bytes 393224 | tf_op jit(solution)/shard_map/ppermute | solution.py:805
  115.0 6.9 %collective-permute-start.17 = (f32[128,128]{1,0:T(8,128)S(1)}, f32[128,128]{1,0:T(8,128)S(1)}, u32[]{:S(2)}, u32[]{:S(2)}) collective-permute-start(f32[128,128]{1,0:T(8,128)S(1)} %slice_bitcast_fusion.3), channel_id=1, source_target_pairs={{0,3},{1,4},{2,5},{3,6},{4,7},{5,8},{6,9},{7,10},{8,11},{9,12},{10... | collective-permute-start | bytes 196616 | tf_op jit(solution)/shard_map/ppermute | solution.py:805
  123.9 3.7 %shard_map.118 = (f32[1,128,128]{2,1,0:T(8,128)}, f32[64,32,128]{2,1,0:T(8,128)S(1)}) custom-call(s32[3]{0:T(128)S(1)} %pad_add_fusion.scalars, f32[2,128,128]{2,1,0:T(8,128)S(1)} %get-tuple-element.47.own, f32[2,128,128]{2,1,0:T(8,128)S(1)} %collective-permute-done.13.sibling, f32[2,128,128]{2,1,0:T(8,128)S(1)} %collective-permute-done.14.outer, ...), custom_call_target="tpu_custom_call" | custom-call | flops 4915200 | bytes 2621440 | tf_op jit(solution)/shard_map/pallas_call | solution.py:39
  127.6 46.0 %all_to_all.5.own = f32[64,32,128]{2,1,0:T(8,128)S(1)} all-to-all(f32[64,32,128]{2,1,0:T(8,128)S(1)} %get-tuple-element.49), channel_id=1, replica_groups={{0,2,4,6,8,10,12,14,16,18,20,22,24,26,28,30,32,34,36,38,40,42,44,46,48,..., dimensions={0} | all-to-all | bytes 2097152 | tf_op jit(solution)/shard_map/all_to_all | solution.py:902
  177.7 21.2 %shard_map.119 = f32[64,64,64]{2,1,0:T(8,128)} custom-call(s32[3]{0:T(128)S(1)} %pad_add_fusion.scalars, f32[64,32,128]{2,1,0:T(8,128)S(1)} %all_to_all.5.own, f32[64,32,128]{2,1,0:T(8,128)S(1)} %collective-permute-done.18.sibling, f32[32,64,128]{2,1,0:T(8,128)S(1)} %pad_maximum_fusion.coef), custom_call_target="tpu_custom_call" | custom-call | flops 78643200 | bytes 5242880 | tf_op jit(solution)/shard_map/pallas_call | solution.py:39
  (71 shorter events, 19.8 us)
Async XLA Ops:
  2.5 17.0 %collective-permute-start = (f32[512,512]{1,0:T(8,128)S(1)}, f32[512,512]{1,0:T(8,128)S(1)}, u32[]{:S(2)}, u32[]{:S(2)}) collective-permute-start(f32[512,512]{1,0:T(8,128)S(1)} %get-tuple-element.51), channel_id=1, source_target_pairs={{1,2},{3,4},{5,6},{7,8},{9,10},{11,12},{13,14},{15,16},{17,18},{19... | collective-permute-start | bytes 3145736 | tf_op jit(solution)/shard_map/ppermute | solution.py:791
  7.1 12.5 %collective-permute-start.1 = (f32[512,512]{1,0:T(8,128)S(1)}, f32[512,512]{1,0:T(8,128)S(1)}, u32[]{:S(2)}, u32[]{:S(2)}) collective-permute-start(f32[512,512]{1,0:T(8,128)S(1)} %get-tuple-element.50), channel_id=1, source_target_pairs={{0,1},{1,0},{2,3},{3,2},{4,5},{5,4},{6,7},{7,6},{8,9},{9,8},{10,11... | collective-permute-start | bytes 3145736 | tf_op jit(solution)/shard_map/ppermute | solution.py:791
  21.2 22.4 %collective-permute-start.4 = (f32[512,512]{1,0:T(8,128)S(1)}, f32[512,512]{1,0:T(8,128)S(1)}, u32[]{:S(2)}, u32[]{:S(2)}) collective-permute-start(f32[512,512]{1,0:T(8,128)S(1)} %get-tuple-element.29.first_outer), channel_id=1, source_target_pairs={{1,2},{3,4},{5,6},{7,8},{9,10},{11,12},{13,14},{15,16},{17,18},{19... | collective-permute-start | bytes 3145736 | tf_op jit(solution)/shard_map/ppermute | solution.py:791
  24.9 18.8 %collective-permute-start.5 = (f32[512,512]{1,0:T(8,128)S(1)}, f32[512,512]{1,0:T(8,128)S(1)}, u32[]{:S(2)}, u32[]{:S(2)}) collective-permute-start(f32[512,512]{1,0:T(8,128)S(1)} %get-tuple-element.30.first_sibling), channel_id=1, source_target_pairs={{0,1},{1,0},{2,3},{3,2},{4,5},{5,4},{6,7},{7,6},{8,9},{9,8},{10,11... | collective-permute-start | bytes 3145736 | tf_op jit(solution)/shard_map/ppermute | solution.py:791
  25.1 12.9 %collective-permute-start.2 = (f32[576,256]{1,0:T(8,128)S(1)}, f32[576,256]{1,0:T(8,128)S(1)}, u32[]{:S(2)}, u32[]{:S(2)}) collective-permute-start(f32[576,256]{1,0:T(8,128)S(1)} %maximum_maximum_fusion), channel_id=1, source_target_pairs={{0,1},{1,0},{2,3},{3,2},{4,5},{5,4},{6,7},{7,6},{8,9},{9,8},{10,11... | collective-permute-start | bytes 1769480 | tf_op jit(solution)/shard_map/ppermute | solution.py:791
  25.7 18.0 %collective-permute-start.3 = (f32[576,256]{1,0:T(8,128)S(1)}, f32[576,256]{1,0:T(8,128)S(1)}, u32[]{:S(2)}, u32[]{:S(2)}) collective-permute-start(f32[576,256]{1,0:T(8,128)S(1)} %maximum_maximum_fusion), channel_id=1, source_target_pairs={{1,2},{3,4},{5,6},{7,8},{9,10},{11,12},{13,14},{15,16},{17,18},{19... | collective-permute-start | bytes 1769480 | tf_op jit(solution)/shard_map/ppermute | solution.py:791
  46.9 26.0 %collective-permute-start.6 = (f32[512,512]{1,0:T(8,128)}, f32[512,512]{1,0:T(8,128)}, u32[]{:S(2)}, u32[]{:S(2)}) collective-permute-start(f32[512,512]{1,0:T(8,128)} %get-tuple-element.36.smooth_outer), channel_id=1, source_target_pairs={{1,2},{3,4},{5,6},{7,8},{9,10},{11,12},{13,14},{15,16},{17,18},{19... | collective-permute-start | bytes 3145736 | tf_op jit(solution)/shard_map/ppermute | solution.py:791
  50.6 22.3 %collective-permute-start.7 = (f32[512,512]{1,0:T(8,128)}, f32[512,512]{1,0:T(8,128)}, u32[]{:S(2)}, u32[]{:S(2)}) collective-permute-start(f32[512,512]{1,0:T(8,128)} %get-tuple-element.37.smooth_sibling), channel_id=1, source_target_pairs={{0,1},{1,0},{2,3},{3,2},{4,5},{5,4},{6,7},{7,6},{8,9},{9,8},{10,11... | collective-permute-start | bytes 3145736 | tf_op jit(solution)/shard_map/ppermute | solution.py:791
  51.8 21.1 %collective-permute-start.8 = (f32[384,256]{1,0:T(8,128)S(1)}, f32[384,256]{1,0:T(8,128)S(1)}, u32[]{:S(2)}, u32[]{:S(2)}) collective-permute-start(f32[384,256]{1,0:T(8,128)S(1)} %get-tuple-element.59), channel_id=1, source_target_pairs={{0,2},{1,3},{2,4},{3,5},{4,6},{5,7},{6,8},{7,9},{8,10},{9,11},{10,... | collective-permute-start | bytes 1179656 | tf_op jit(solution)/shard_map/ppermute | solution.py:805
  55.0 17.9 %collective-permute-start.9 = (f32[384,256]{1,0:T(8,128)S(1)}, f32[384,256]{1,0:T(8,128)S(1)}, u32[]{:S(2)}, u32[]{:S(2)}) collective-permute-start(f32[384,256]{1,0:T(8,128)S(1)} %get-tuple-element.58), channel_id=1, source_target_pairs={{2,0},{3,1},{4,2},{5,3},{6,4},{7,5},{8,6},{9,7},{10,8},{11,9},{12,... | collective-permute-start | bytes 1179656 | tf_op jit(solution)/shard_map/ppermute | solution.py:805
  72.9 23.2 %copy-start.7 = (f32[2,256,256]{2,1,0:T(8,128)S(1)}, f32[2,256,256]{2,1,0:T(8,128)}, u32[]{:S(2)}) copy-start(f32[2,256,256]{2,1,0:T(8,128)} %coef.8) | copy-start | bytes 1572868
  72.9 23.2 %copy-start.11 = (bf16[256,128]{1,0:T(8,128)(2,1)S(1)}, bf16[256,128]{1,0:T(8,128)(2,1)}, u32[]{:S(2)}) copy-start(bf16[256,128]{1,0:T(8,128)(2,1)} %constant.38.clone.matrix) | copy-start | bytes 196612
  76.5 19.6 %collective-permute-start.10 = (f32[3,256,256]{2,1,0:T(8,128)S(1)}, f32[3,256,256]{2,1,0:T(8,128)S(1)}, u32[]{:S(2)}, u32[]{:S(2)}) collective-permute-start(f32[3,256,256]{2,1,0:T(8,128)S(1)} %shard_map.116.own), channel_id=1, source_target_pairs={{0,1},{1,0},{2,3},{3,2},{4,5},{5,4},{6,7},{7,6},{8,9},{9,8},{10,11... | collective-permute-start | bytes 2359304 | tf_op jit(solution)/shard_map/ppermute | solution.py:791
  77.4 18.7 %collective-permute-start.11 = (f32[3,256,256]{2,1,0:T(8,128)S(1)}, f32[3,256,256]{2,1,0:T(8,128)S(1)}, u32[]{:S(2)}, u32[]{:S(2)}) collective-permute-start(f32[3,256,256]{2,1,0:T(8,128)S(1)} %shard_map.116.own), channel_id=1, source_target_pairs={{1,2},{3,4},{5,6},{7,8},{9,10},{11,12},{13,14},{15,16},{17,18},{19... | collective-permute-start | bytes 2359304 | tf_op jit(solution)/shard_map/ppermute | solution.py:791
  81.6 42.3 %copy-start.10 = (f32[1,128,128]{2,1,0:T(8,128)S(1)}, f32[1,128,128]{2,1,0:T(8,128)}, u32[]{:S(2)}) copy-start(f32[1,128,128]{2,1,0:T(8,128)} %coef.9) | copy-start | bytes 196612
  81.6 42.3 %copy-start.12 = (bf16[2,128,128]{2,1,0:T(8,128)(2,1)S(1)}, bf16[2,128,128]{2,1,0:T(8,128)(2,1)}, u32[]{:S(2)}) copy-start(bf16[2,128,128]{2,1,0:T(8,128)(2,1)} %constant.39.clone.matrices) | copy-start | bytes 196612
  81.6 14.5 %collective-permute-start.12 = (f32[256,256]{1,0:T(8,128)S(1)}, f32[256,256]{1,0:T(8,128)S(1)}, u32[]{:S(2)}, u32[]{:S(2)}) collective-permute-start(f32[256,256]{1,0:T(8,128)S(1)} %slice_bitcast_fusion), channel_id=1, source_target_pairs={{0,2},{1,3},{2,4},{3,5},{4,6},{5,7},{6,8},{7,9},{8,10},{9,11},{10,... | collective-permute-start | bytes 786440 | tf_op jit(solution)/shard_map/ppermute | solution.py:805
  102.9 21.0 %collective-permute-start.13 = (f32[2,128,128]{2,1,0:T(8,128)S(1)}, f32[2,128,128]{2,1,0:T(8,128)S(1)}, u32[]{:S(2)}, u32[]{:S(2)}) collective-permute-start(f32[2,128,128]{2,1,0:T(8,128)S(1)} %get-tuple-element.47.own), channel_id=1, source_target_pairs={{0,1},{1,0},{2,3},{3,2},{4,5},{5,4},{6,7},{7,6},{8,9},{9,8},{10,11... | collective-permute-start | bytes 393224 | tf_op jit(solution)/shard_map/ppermute | solution.py:791
  103.0 20.9 %collective-permute-start.14 = (f32[2,128,128]{2,1,0:T(8,128)S(1)}, f32[2,128,128]{2,1,0:T(8,128)S(1)}, u32[]{:S(2)}, u32[]{:S(2)}) collective-permute-start(f32[2,128,128]{2,1,0:T(8,128)S(1)} %get-tuple-element.47.own), channel_id=1, source_target_pairs={{1,2},{3,4},{5,6},{7,8},{9,10},{11,12},{13,14},{15,16},{17,18},{19... | collective-permute-start | bytes 393224 | tf_op jit(solution)/shard_map/ppermute | solution.py:791
  109.9 14.0 %collective-permute-start.15 = (f32[2,128,128]{2,1,0:T(8,128)S(1)}, f32[2,128,128]{2,1,0:T(8,128)S(1)}, u32[]{:S(2)}, u32[]{:S(2)}) collective-permute-start(f32[2,128,128]{2,1,0:T(8,128)S(1)} %get-tuple-element.47.own), channel_id=1, source_target_pairs={{0,2},{1,3},{2,4},{3,5},{4,6},{5,7},{6,8},{7,9},{8,10},{9,11},{10,... | collective-permute-start | bytes 393224 | tf_op jit(solution)/shard_map/ppermute | solution.py:805
  113.7 10.2 %collective-permute-start.16 = (f32[2,128,128]{2,1,0:T(8,128)S(1)}, f32[2,128,128]{2,1,0:T(8,128)S(1)}, u32[]{:S(2)}, u32[]{:S(2)}) collective-permute-start(f32[2,128,128]{2,1,0:T(8,128)S(1)} %get-tuple-element.47.own), channel_id=1, source_target_pairs={{2,0},{3,1},{4,2},{5,3},{6,4},{7,5},{8,6},{9,7},{10,8},{11,9},{12,... | collective-permute-start | bytes 393224 | tf_op jit(solution)/shard_map/ppermute | solution.py:805
  115.0 60.4 %copy-start.15 = (f32[64,64,64]{2,1,0:T(8,128)S(1)}, f32[64,64,64]{2,1,0:T(8,128)}, u32[]{:S(2)}) copy-start(f32[64,64,64]{2,1,0:T(8,128)} %param.12) | copy-start | bytes 3145732
  115.0 8.8 %collective-permute-start.17 = (f32[128,128]{1,0:T(8,128)S(1)}, f32[128,128]{1,0:T(8,128)S(1)}, u32[]{:S(2)}, u32[]{:S(2)}) collective-permute-start(f32[128,128]{1,0:T(8,128)S(1)} %slice_bitcast_fusion.3), channel_id=1, source_target_pairs={{0,3},{1,4},{2,5},{3,6},{4,7},{5,8},{6,9},{7,10},{8,11},{9,12},{10... | collective-permute-start | bytes 196616 | tf_op jit(solution)/shard_map/ppermute | solution.py:805
  173.6 4.0 %collective-permute-start.18 = (f32[64,32,128]{2,1,0:T(8,128)S(1)}, f32[64,32,128]{2,1,0:T(8,128)S(1)}, u32[]{:S(2)}, u32[]{:S(2)}) collective-permute-start(f32[64,32,128]{2,1,0:T(8,128)S(1)} %all_to_all.5.own), channel_id=1, source_target_pairs={{0,1},{1,0},{2,3},{3,2},{4,5},{5,4},{6,7},{7,6},{8,9},{9,8},{10,11... | collective-permute-start | bytes 3145736 | tf_op jit(solution)/shard_map/ppermute | solution.py:791
  (13 other events, 63.1 us)

commit v3 on v2

--- a/solution.py
+++ b/solution.py
@@ -205,13 +205,17 @@
     return result
 
 
-def sweep(size, body):
+def sweep(size, body, start=0):
     def step(index, carry):
         for store, ref, plane, row, values in body(pl.multiple_of(index * ROWS, ROWS)):
             store(ref, plane, row, values)
         return carry
 
-    lax.fori_loop(0, size // ROWS, step, 0, unroll=UNROLL)
+    lax.fori_loop(start // ROWS, size // ROWS, step, 0, unroll=UNROLL)
+
+
+def in_halves(size):
+    return ((0, size // 2), (size // 2, size))
 
 
 def thin_rows(tiles, plane, start, count):
@@ -293,25 +297,29 @@
     size = rhs.shape[1]
     go = Copies(sems)
     loads = []
-    for slot, q, halo in ((0, 0, coef_outer), (1, 3, coef_sibling)):
-        loads.append(
-            [
-                go.start(rhs.at[plane_at(core, q)], b.at[slot]),
-                go.start(partial.at[slot], g.at[slot]),
-                go.start(halo, h.at[slot]),
-            ]
-        )
+    for slot, q, halo in ((1, 3, coef_sibling), (0, 0, coef_outer)):
+        for start, stop in in_halves(size):
+            part = pl.ds(start, stop - start)
+            loads.append(
+                [
+                    go.start(rhs.at[plane_at(core, q), part], b.at[slot, part]),
+                    go.start(partial.at[slot, part], g.at[slot, part]),
+                    go.start(halo.at[part], h.at[slot, part]),
+                ]
+            )
     out = []
-    for slot, target in ((0, outer), (1, sibling)):
-        for copy in loads[slot]:
-            copy.wait()
-
-        def rows(row):
-            twice = each(lambda g, h: g + h, load_flat(g, slot, row), load_flat(h, slot, row))
-            return [(store_flat, f, slot, row, first_of(load_flat(b, slot, row), twice))]
-
-        sweep(size, rows)
-        out.append(go.start(f.at[slot], target))
+    for slot, target in ((1, sibling), (0, outer)):
+        for start, stop in in_halves(size):
+            for copy in loads.pop(0):
+                copy.wait()
+
+            def rows(row):
+                twice = each(lambda g, h: g + h, load_flat(g, slot, row), load_flat(h, slot, row))
+                return [(store_flat, f, slot, row, first_of(load_flat(b, slot, row), twice))]
+
+            sweep(stop, rows, start)
+            part = pl.ds(start, stop - start)
+            out.append(go.start(f.at[slot, part], target.at[part]))
     for copy in out:
         copy.wait()
 
@@ -385,6 +393,21 @@
         copy.wait()
 
 
+def rim_loads(go, known, factor, halo_outer, halo_sibling, g, h, v):
+    loads = []
+    for slot, halo in ((1, halo_sibling), (0, halo_outer)):
+        for start, stop in in_halves(known.shape[1]):
+            part = pl.ds(start, stop - start)
+            loads.append(
+                [
+                    go.start(known.at[slot, part], g.at[slot, part]),
+                    go.start(factor.at[slot, part], h.at[slot, part]),
+                    go.start(halo.at[part], v.at[slot, part]),
+                ]
+            )
+    return loads
+
+
 def smooth_rim(
     scalars, started, known, factor, halo_outer, halo_sibling,
     smooth, outer, sibling, g, h, v, s, sems,
@@ -392,27 +415,21 @@
     core = scalars[0]
     size = known.shape[1]
     go = Copies(sems)
-    loads = []
-    for slot, halo in ((0, halo_outer), (1, halo_sibling)):
-        loads.append(
-            [
-                go.start(known.at[slot], g.at[slot]),
-                go.start(factor.at[slot], h.at[slot]),
-                go.start(halo, v.at[slot]),
-            ]
-        )
+    loads = rim_loads(go, known, factor, halo_outer, halo_sibling, g, h, v)
     out = []
-    for slot, q, target in ((0, 0, outer), (1, 3, sibling)):
-        for copy in loads[slot]:
-            copy.wait()
-
-        def rows(row):
-            flat = [load_flat(ref, slot, row) for ref in (g, h, v)]
-            return [(store_flat, s, slot, row, each(lambda g, h, v: g + h * v, *flat))]
-
-        sweep(size, rows)
-        out.append(go.start(s.at[slot], target))
-        out.append(go.start(s.at[slot], smooth.at[plane_at(core, q)]))
+    for slot, q, target in ((1, 3, sibling), (0, 0, outer)):
+        for start, stop in in_halves(size):
+            for copy in loads.pop(0):
+                copy.wait()
+
+            def rows(row):
+                flat = [load_flat(ref, slot, row) for ref in (g, h, v)]
+                return [(store_flat, s, slot, row, each(lambda g, h, v: g + h * v, *flat))]
+
+            sweep(stop, rows, start)
+            part = pl.ds(start, stop - start)
+            out.append(go.start(s.at[slot, part], target.at[part]))
+            out.append(go.start(s.at[slot, part], smooth.at[plane_at(core, q), part]))
     for copy in out:
         copy.wait()
 
@@ -473,28 +490,21 @@
     core = scalars[0]
     size = known.shape[1]
     go = Copies(sems)
-    loads = []
-    for slot, halo in ((0, halo_outer), (1, halo_sibling)):
-        loads.append(
-            [
-                go.start(known.at[slot], g.at[slot]),
-                go.start(factor.at[slot], h.at[slot]),
-                go.start(halo, v.at[slot]),
-            ]
-        )
     more = [go.start(lowered, low.at[pl.ds(1, 2)]), go.start(matrix, mat)]
+    loads = rim_loads(go, known, factor, halo_outer, halo_sibling, g, h, v)
     clear_top(t)
     for copy in more:
         copy.wait()
-    for slot in (0, 1):
-        for copy in loads[slot]:
-            copy.wait()
-
-        def rows(row):
-            flat = [load_flat(ref, slot, row) for ref in (g, h, v)]
-            return [(store_rows, t, slot, row, each(lambda g, h, v: g + h * v, *flat))]
-
-        sweep(size, rows)
+    for slot in (1, 0):
+        for start, stop in in_halves(size):
+            for copy in loads.pop(0):
+                copy.wait()
+
+            def rows(row):
+                flat = [load_flat(ref, slot, row) for ref in (g, h, v)]
+                return [(store_rows, t, slot, row, each(lambda g, h, v: g + h * v, *flat))]
+
+            sweep(stop, rows, start)
         low[3 * slot] = restrict_plane(t, slot, size, mat[...])
     one = plane_at(core, 1)
     two = plane_at(core, 2)
@@ -547,8 +557,8 @@
 
 
 def middle_level(
-    scalars, own, sibling, outer, before, coef, coef_sibling, coef_outer, coef_before, coef_after,
-    matrix, smooth, packed, m, b, c, f, s, t, pack, mat, sems,
+    scalars, own, sibling, outer, rim_outer, rim_sibling, coef, coef_sibling, coef_outer,
+    coef_beyond, matrix, smooth, packed, m, b, c, f, s, t, pack, mat, sems,
 ):
     core = scalars[0]
     place = scalars[1]
@@ -556,25 +566,26 @@
     size = coef.shape[1]
     even = core == 0
     go = Copies(sems)
+    three = pl.ds(0, 3)
     loads = [
         go.start(own, m.at[pl.ds(3, 3)]),
-        go.choose(even, outer, sibling, m.at[pl.ds(0, 3)]),
+        go.choose(even, outer, sibling, m.at[three]),
         go.choose(even, sibling, outer, m.at[pl.ds(6, 3)]),
-        go.start(before, m.at[9]),
-        go.tiles(coef_before.at[pl.ds(0, size)], c.at[0]),
-        go.tiles(coef_after.at[pl.ds(0, size)], c.at[7]),
+        go.choose(even, rim_outer, rim_sibling, m.at[9]),
         go.start(matrix, mat),
     ]
-    for q in range(2):
-        part = pl.ds(q * size, size)
-        loads.append(go.tiles(coef.at[q], c.at[3 + q]))
-        for tile in range(size // LANES):
-            outer_part = coef_outer.at[part, columns(tile)]
-            sibling_part = coef_sibling.at[part, columns(tile)]
+    for tile in range(size // LANES):
+        part = columns(tile)
+        for q in range(2):
             left = c.at[1 + q, tile, pl.ds(PAD, size), :]
             right = c.at[5 + q, tile, pl.ds(PAD, size), :]
-            loads.append(go.choose(even, outer_part, sibling_part, left))
-            loads.append(go.choose(even, sibling_part, outer_part, right))
+            loads.append(go.choose(even, coef_outer.at[q, :, part], coef_sibling.at[q, :, part], left))
+            loads.append(go.choose(even, coef_sibling.at[q, :, part], coef_outer.at[q, :, part], right))
+        left = c.at[0, tile, pl.ds(PAD, size), :]
+        right = c.at[7, tile, pl.ds(PAD, size), :]
+        loads.append(go.choose(even, coef_outer.at[2, :, part], coef_beyond.at[:, part], left))
+        loads.append(go.choose(even, coef_beyond.at[:, part], coef_outer.at[2, :, part], right))
+    loads += [go.tiles(coef.at[q], c.at[3 + q]) for q in range(2)]
     clear_pads(c, size)
     clear_pads(f, size)
     clear_pads(s, size)
@@ -610,54 +621,47 @@
 
 
 def last_level(
-    scalars, own, sibling, outer, before, after, rim, coef, coef_sibling, coef_outer, coef_before,
-    coef_after, matrices, smooth, copies, m, b, c, f, s, t, w, mat, sems,
+    scalars, own, sibling, even_chip, odd_chip, even_beside, odd_beside, third, matrices,
+    smooth, copies, n, b, c, f, s, t, w, mat, sems,
 ):
     core = scalars[0]
     place = scalars[1]
     final = scalars[2]
-    size = coef.shape[1]
+    size = own.shape[1]
     half = size // 2
-    base = 4 * size
-    even = core == 0
+    left_core = core == 0
+    left_is_odd = (place // 2) % 2 == 0
     go = Copies(sems)
-    loads = [
-        go.start(before, m.at[pl.ds(0, 2)]),
-        go.choose(even, outer, sibling, m.at[pl.ds(2, 2)]),
-        go.start(own, m.at[pl.ds(4, 2)]),
-        go.choose(even, sibling, outer, m.at[pl.ds(6, 2)]),
-        go.start(after, m.at[pl.ds(8, 2)]),
-        go.start(rim, m.at[10]),
-        go.tiles(coef.at[0], c.at[3]),
+    nearer = [
+        go.start(own, n.at[3]),
+        go.start(sibling, n.at[jnp.where(left_core, 4, 2)]),
+        go.choose(left_is_odd, odd_chip, even_chip, n.at[1]),
+        go.choose(left_is_odd, even_chip, odd_chip, n.at[5]),
+        go.choose(left_is_odd, odd_beside, even_beside, n.at[jnp.where(left_core, 2, 0)]),
+        go.choose(left_is_odd, even_beside, odd_beside, n.at[jnp.where(left_core, 6, 4)]),
+        go.start(third, n.at[jnp.where(left_core, 0, 6), pl.ds(1, 2)]),
         go.start(matrices, mat),
     ]
-    for part in range(2):
-        target = pl.ds(PAD + part * half, half)
-        lanes = pl.ds(part * size, size)
-        outer_part = coef_outer.at[pl.ds(base, half), lanes]
-        sibling_part = coef_sibling.at[pl.ds(base, half), lanes]
-        loads.append(go.choose(even, outer_part, sibling_part, c.at[2, 0, target, :]))
-        loads.append(go.choose(even, sibling_part, outer_part, c.at[4, 0, target, :]))
-        for source, nearer, farther in ((coef_before, 1, 0), (coef_after, 5, 6)):
-            loads.append(go.start(source.at[pl.ds(2 * size, half), lanes], c.at[nearer, 0, target, :]))
-            loads.append(
-                go.start(source.at[pl.ds(2 * size + half, half), lanes], c.at[farther, 0, target, :])
-            )
     clear_pads(c, size)
     clear_pads(f, size)
     clear_pads(s, size)
     clear_top(t)
-    for copy in loads:
-        copy.wait()
+    for copy in nearer:
+        copy.wait()
+
+    def coef_rows(row):
+        return [(store_rows, c, q, row, [n[q, 2, pl.ds(row, ROWS), :]]) for q in range(7)]
+
+    sweep(size, coef_rows)
 
     def rows(row):
         part = pl.ds(row, ROWS)
         values = [
-            m[0, part, :] + m[10, part, :],
-            m[2, part, :] + m[1, part, :],
-            m[4, part, :] + m[3, part, :],
-            jnp.where(place < final, m[6, part, :] + m[5, part, :], 0.0),
-            jnp.where(place < final - 1, m[8, part, :] + m[7, part, :], 0.0),
+            n[1, 0, part, :] + n[0, 1, part, :],
+            n[2, 0, part, :] + n[1, 1, part, :],
+            n[3, 0, part, :] + n[2, 1, part, :],
+            jnp.where(place < final, n[4, 0, part, :] + n[3, 1, part, :], 0.0),
+            jnp.where(place < final - 1, n[5, 0, part, :] + n[4, 1, part, :], 0.0),
         ]
         return [(store_whole, b, q, row, value) for q, value in enumerate(values)]
 
@@ -800,10 +804,6 @@
     far = [(i, i + 1) for i in range(1, count - 1, 2)]
     far = far + [(j, i) for i, j in far]
 
-    def onward(value, distance):
-        route = [(i, i + distance) for i in range(count) if 0 <= i + distance < count]
-        return lax.ppermute(value, "box", route)
-
     n = coef_zero.shape[1]
     n1, n2 = n // 2, n // 4
     n3 = n // 8
@@ -816,15 +816,21 @@
     def side_plane(field, where):
         return lax.dynamic_index_in_dim(field, where, 0, keepdims=False)
 
-    coef_outer = swapped(side_plane(coef_zero, 3 * core), far)
-    coef_sibling = swapped(side_plane(coef_zero, 3 - 3 * core), near)
+    coef_outer = side_plane(coef_zero, 3 * core)
+    rest, coef_outer = lax.optimization_barrier((coef_zero, coef_outer))
+    coef_outer = swapped(coef_outer, far)
+    coef_sibling = swapped(side_plane(rest, 3 - 3 * core), near)
     first, partial = call(
         first_inner, [shape(2, n, n), shape(2, n, n)],
-        [tiled(4, n), vm(2, n, n), vm(2, n, n), vm(2, n, n)], 24, 40 * n * n, 12 * plane, 32,
+        [tiled(4, n), vm(2, n, n), vm(2, n, n), vm(2, n, n)], 24, 40 * n * n, 12 * plane, 60,
     )(scalars, coef_zero, rhs_fine)
+    coefs_sibling = swapped(coef_one, near)
+    beyond = lax.dynamic_slice_in_dim(coefs_sibling, core, 1, 0)
+    coefs_out = jnp.concatenate([coef_one, beyond], axis=0)
+    partial, coefs_out = lax.optimization_barrier((partial, coefs_out))
     first_outer, first_sibling = call(
         first_rim, [shape(n, n), shape(n, n)],
-        [vm(2, n, n)] * 4, 8, 10 * n * n, 8 * plane, 32,
+        [vm(2, n, n)] * 4, 16, 10 * n * n, 8 * plane, 60,
     )(scalars, rhs_fine, partial, coef_outer, coef_sibling)
 
     halo_outer = swapped(first_outer, far)
@@ -832,72 +838,71 @@
     smooth, known, factor = call(
         smooth_inner, [shape(4, n, n), shape(2, n, n), shape(2, n, n)],
         [tiled(6, n), tiled(6, n), vm(4, n, n), vm(2, n, n), vm(2, n, n), vm(2, n, n)],
-        54, 160 * n * n, 20 * plane, 32,
+        54, 160 * n * n, 20 * plane, 60,
     )(scalars, coef_zero, rhs_fine, coef_outer, coef_sibling, first, first_outer, first_sibling)
-    def folded(field):
-        return jnp.concatenate([field[: n2 // 2], field[n2 // 2 :]], axis=1)
-
-    own_two = folded(coef_two[0])
-    coefs = jnp.concatenate([coef_one[0], coef_one[1], own_two], axis=0)
-    coefs_sibling = swapped(coefs, near)
-    coefs_outer = swapped(coefs, far)
-    known, coefs_sibling, coefs_outer = lax.optimization_barrier(
-        (known, coefs_sibling, coefs_outer)
-    )
+    coefs_out, known = lax.optimization_barrier((coefs_out, known))
+    coefs_outer = swapped(coefs_out, far)
     smooth_zero, smooth_outer, smooth_sibling = call(
         smooth_rim, [shape(4, n, n), shape(n, n), shape(n, n)],
-        [vm(2, n, n)] * 4, 10, 4 * n * n, 10 * plane, 32, {1: 0},
+        [vm(2, n, n)] * 4, 20, 4 * n * n, 10 * plane, 60, {1: 0},
     )(scalars, smooth, known, factor, halo_outer, halo_sibling)
 
     halo_outer = swapped(smooth_outer, far)
     halo_sibling = swapped(smooth_sibling, near)
 
+    smooth_outer, coefs_outer = lax.optimization_barrier((smooth_outer, coefs_outer))
     lowered, known, factor = call(
         residual_inner, [shape(2, n1, n1), shape(2, n, n), shape(2, n, n)],
         [tiled(6, n), tiled(6, n), vm(4, n, n), vm(2, n, n), vm(2, n, n),
          tiled(2, n), vm(2, n1, n1), pltpu.VMEM((n, n1), BF16)],
-        54, 160 * n * n, 20 * plane, 32,
+        54, 160 * n * n, 20 * plane, 60,
     )(scalars, coef_zero, rhs_fine, coef_outer, coef_sibling, smooth_zero, smooth_outer,
       smooth_sibling, matrix0)
-    left_two = jnp.where(core == 0, coefs_outer[2 * n1 :], coefs_sibling[2 * n1 :])
-    right_two = jnp.where(core == 0, coefs_sibling[2 * n1 :], coefs_outer[2 * n1 :])
-    coefs_before = onward(jnp.concatenate([coef_one[1], own_two, left_two], axis=0), 2)
-    coefs_after = onward(jnp.concatenate([coef_one[0], own_two, right_two], axis=0), -2)
-    lowered, coefs_before, coefs_after = lax.optimization_barrier(
-        (lowered, coefs_before, coefs_after)
-    )
+    coefs_beyond = swapped(lax.dynamic_index_in_dim(coefs_outer, 1 - core, 0, False), near)
+    lowered, coefs_beyond = lax.optimization_barrier((lowered, coefs_beyond))
     (packed,) = call(
         residual_rim, [shape(3, n1, n1)],
         [vm(2, n, n), vm(2, n, n), vm(2, n, n), tiled(2, n), vm(4, n1, n1), vm(3, n1, n1),
          pltpu.VMEM((n, n1), BF16)],
-        10, 20 * n * n, 8 * plane, 32,
+        15, 20 * n * n, 8 * plane, 60,
     )(scalars, known, factor, halo_outer, halo_sibling, lowered, matrix0)
 
     packed_outer = swapped(packed, far)
-    packed_before = onward(packed[2], 2)
     packed_sibling = swapped(packed, near)
+    rim_outer = swapped(packed_sibling[2], far)
+    rim_sibling = swapped(packed_outer[2], near)
     smooth_one, packed = call(
         middle_level, [shape(2, n1, n1), shape(2, n2, n2)],
         [vm(10, n1, n1), vm(6, n1, n1), tiled(8, n1), tiled(6, n1),
          tiled(4, n1), tiled(2, n1), vm(2, n2, n2), pltpu.VMEM((n1, n2), BF16)],
         40, 400 * n1 * n1, 24 * n1 * n1 * 4, 40,
-    )(scalars, packed, packed_sibling, packed_outer, packed_before, coef_one, coefs_sibling,
-      coefs_outer, coefs_before, coefs_after, matrix1)
-
-    packed_outer = swapped(packed, far)
-    packed_before = onward(packed, 2)
-    packed_after = onward(packed, -2)
-    packed_rim = onward(packed[1], 3)
-    packed_sibling = swapped(packed, near)
+    )(scalars, packed, packed_sibling, packed_outer, rim_outer, rim_sibling, coef_one,
+      coefs_sibling, coefs_outer, coefs_beyond, matrix1)
+
+    chip_even = [(i, i ^ 2) for i in range(count)]
+    chip_odd = [(i, i + 2) for i in range(count - 2) if i & 2]
+    chip_odd = chip_odd + [(j, i) for i, j in chip_odd]
+    third = [(i, i + 3) for i in range(1, count - 3, 2)]
+    third = third + [(j, i) for i, j in third]
+    sent = jnp.concatenate([packed, coef_two], axis=0)
+    even_chip = swapped(sent, chip_even)
+    odd_chip = swapped(sent, chip_odd)
+    packed_third = swapped(sent[1:], third)
+    packed_sibling = swapped(sent, near)
+    even_chip, odd_chip, packed_third = lax.optimization_barrier(
+        (even_chip, odd_chip, packed_third)
+    )
+    even_beside = swapped(even_chip, near)
+    odd_beside = swapped(odd_chip, near)
     groups = [[i for i in range(count) if i % 2 == r] for r in range(2)]
     smooth_two, copies = call(
         last_level, [shape(1, n2, n2), shape(count // 2, n3 // 2, 2 * n3)],
-        [vm(11, n2, n2), vm(5, n2, n2), tiled(7, n2), tiled(5, n2),
+        [vm(7, 3, n2, n2), vm(5, n2, n2), tiled(7, n2), tiled(5, n2),
          tiled(3, n2), tiled(1, n2), vm(count // 2, n3 // 2, 2 * n3),
          pltpu.VMEM((2, n2, 2 * n3), BF16)],
         24, 300 * n2 * n2, 40 * n2 * n2 * 4, 40,
-    )(scalars, packed, packed_sibling, packed_outer, packed_before, packed_after, packed_rim,
-      coef_two, coefs_sibling, coefs_outer, coefs_before, coefs_after, matrix2)
+    )(scalars, sent, packed_sibling, even_chip, odd_chip, even_beside, odd_beside, packed_third,
+      matrix2)
 
     gathered = lax.all_to_all(copies, "box", 0, 0, tiled=True, axis_index_groups=groups)
     gathered_sibling = swapped(gathered, near)

time: 200 us -> 188 us (0.940)
  starting transfers between devices: 52.7 us -> 35.2 us
  Pallas kernels: 64.5 us -> 78.6 us
  blocking collectives: 46 us -> 41.4 us
  local copies, waits for them, and re-layouts: 11 us -> 7.05 us
    ppermute x6 -> x0, starting transfers between devices: 23.3 us -> none  [onward(): return lax.ppermute(value, 'box', route)]
    pallas_call x9, Pallas kernels: 64.5 us -> 78.6 us  [run(): pl.pallas_call(body, out_shape=outs, in_specs=[pl.BlockSpec(memory_space=...]
    ppermute x13 -> x20, waiting for transfers between devices: 12.2 us -> 22 us  [swapped(): return lax.ppermute(value, 'box', pairs)]
    ppermute x6 -> x0, waiting for transfers between devices: 9.73 us -> none  [onward(): return lax.ppermute(value, 'box', route)]
    ppermute x13 -> x20, starting transfers between devices: 29.4 us -> 35.2 us  [swapped(): return lax.ppermute(value, 'box', pairs)]
    unnamed x36 -> x21, local copies, waits for them, and re-layouts: 8.82 us -> 3.09 us
    all_to_all x1, blocking collectives: 46 us -> 41.4 us  [local(): lax.all_to_all(copies, 'box', 0, 0, tiled=True, axis_index_groups=groups)]
  transfers between devices with their start and end apart: 19 -> 20, of which waited for: 5 -> 8; matrix products, arithmetic and copies ran while one was open for 1% -> 1% of each run, Pallas kernels for 12% -> 21%
where the time goes in v3:
time: 188 us; the launch traced here: 187 us
  Pallas kernels  78.6 us (42%)
  blocking collectives  41.4 us (22%)
  starting transfers between devices  35.2 us (19%)
  waiting for transfers between devices  22 us (12%)
  local copies, waits for them, and re-layouts  7.05 us (4%)
  other arithmetic  1.96 us (1%)
    pallas_call x9, Pallas kernels, run(): pl.pallas_call(body, out_shape=outs, in_specs=[pl.BlockSpec(memory_space=...  78.6 us
    all_to_all x1, blocking collectives, local(): lax.all_to_all(copies, 'box', 0, 0, tiled=True, axis_index_groups=groups)  41.4 us
    ppermute x20, starting transfers between devices, swapped(): return lax.ppermute(value, 'box', pairs)  35.2 us
    ppermute x20, waiting for transfers between devices, swapped(): return lax.ppermute(value, 'box', pairs)  22 us
  transfers between devices with their start and end apart: 20, of which 8 were waited for; matrix products, arithmetic and copies ran while one was open for 1% of the time, Pallas kernels for 21%

profile of v3, /device:TPU:1, one launch (start us, length us, event | category | flops | bytes accessed | tf_op | source)
XLA Modules:
  0.0 187.4 jit_solution(11334067850244743861)
XLA Ops:
  2.0 2.3 %dynamic-slice_bitcast_fusion = f32[512,512]{1,0:T(8,128)} fusion(f32[4,512,512]{2,1,0:T(8,128)} %coef.6, s32[]{:T(128)S(6)} %select_n.23), kind=kLoop, calls=%fused_computation.1 | loop fusion | bytes 2097156 | tf_op jit(solution)/shard_map/jit(dynamic_index_in_dim)/squeeze | solution.py:817
  5.7 3.1 %collective-permute-start = (f32[512,512]{1,0:T(8,128)S(1)}, f32[512,512]{1,0:T(8,128)}, u32[]{:S(2)}, u32[]{:S(2)}) collective-permute-start(f32[512,512]{1,0:T(8,128)S(1)} %dynamic-slice_bitcast_fusion.1), channel_id=1, source_target_pairs={{1,2},{3,4},{5,6},{7,8},{9,10},{11,12},{13,14},{15,16},{17,18},{19... | collective-permute-start | bytes 3145736 | tf_op jit(solution)/shard_map/ppermute | solution.py:795
  9.6 6.8 %shard_map.111 = (f32[2,512,512]{2,1,0:T(8,128)}, f32[2,512,512]{2,1,0:T(8,128)}) custom-call(s32[3]{0:T(128)} %pad_add_fusion.scalars, f32[4,512,512]{2,1,0:T(8,128)} %coef.6, f32[4,512,512]{2,1,0:T(8,128)} %rhs.7), custom_call_target="tpu_custom_call" | custom-call | flops 10485760 | bytes 12582912 | tf_op jit(solution)/shard_map/pallas_call | solution.py:39
  17.4 4.5 %collective-permute-done.coef_outer = f32[512,512]{1,0:T(8,128)} collective-permute-done((f32[512,512]{1,0:T(8,128)S(1)}, f32[512,512]{1,0:T(8,128)}, u32[]{:S(2)}, u32[]{:S(2)}) %collective-permute-start) | collective-permute-done | bytes 1048608 | tf_op jit(solution)/shard_map/ppermute | solution.py:795
  21.9 4.8 %shard_map.112 = (f32[512,512]{1,0:T(8,128)}, f32[512,512]{1,0:T(8,128)}) custom-call(s32[3]{0:T(128)} %pad_add_fusion.scalars, f32[4,512,512]{2,1,0:T(8,128)} %rhs.7, f32[2,512,512]{2,1,0:T(8,128)} %get-tuple-element.38.partial, f32[512,512]{1,0:T(8,128)} %collective-permute-done.coef_outer, f32[512,512]{1,0:T(8,128)} %copy-done.5), custom_call_target="tpu_custom_call" | custom-call | flops 2621440 | bytes 8388608 | tf_op jit(solution)/shard_map/pallas_call | solution.py:39
  26.8 3.1 %collective-permute-start.3 = (f32[512,512]{1,0:T(8,128)}, f32[512,512]{1,0:T(8,128)S(1)}, u32[]{:S(2)}, u32[]{:S(2)}) collective-permute-start(f32[512,512]{1,0:T(8,128)} %get-tuple-element.39.first_outer), channel_id=1, source_target_pairs={{1,2},{3,4},{5,6},{7,8},{9,10},{11,12},{13,14},{15,16},{17,18},{19... | collective-permute-start | bytes 3145736 | tf_op jit(solution)/shard_map/ppermute | solution.py:795
  30.0 11.3 %shard_map.113 = (f32[4,512,512]{2,1,0:T(8,128)}, f32[2,512,512]{2,1,0:T(8,128)}, f32[2,512,512]{2,1,0:T(8,128)}) custom-call(s32[3]{0:T(128)} %pad_add_fusion.scalars, f32[4,512,512]{2,1,0:T(8,128)} %coef.6, f32[4,512,512]{2,1,0:T(8,128)} %rhs.7, f32[512,512]{1,0:T(8,128)} %collective-permute-done.coef_outer, f32[512,512]{1,0:T(8,128)} %copy-done.5, ...), custom_call_target="tpu_custom_call" | custom-call | flops 41943040 | bytes 20971520 | tf_op jit(solution)/shard_map/pallas_call | solution.py:39
  41.2 3.5 %collective-permute-start.5 = (f32[3,256,256]{2,1,0:T(8,128)}, f32[3,256,256]{2,1,0:T(8,128)S(1)}, u32[]{:S(2)}, u32[]{:S(2)}) collective-permute-start(f32[3,256,256]{2,1,0:T(8,128)} %pad_maximum_fusion.1), channel_id=1, source_target_pairs={{1,2},{3,4},{5,6},{7,8},{9,10},{11,12},{13,14},{15,16},{17,18},{19... | collective-permute-start | bytes 2359304 | tf_op jit(solution)/shard_map/ppermute | solution.py:795
  45.7 5.7 %shard_map.114 = (f32[4,512,512]{2,1,0:T(8,128)}, f32[512,512]{1,0:T(8,128)}, f32[512,512]{1,0:T(8,128)}) custom-call(s32[3]{0:T(128)} %pad_add_fusion.scalars, f32[4,512,512]{2,1,0:T(8,128)} %get-tuple-element.41.started, f32[2,512,512]{2,1,0:T(8,128)} %get-tuple-element.44.known, ...), custom_call_target="tpu_custom_call", output_to_operand_aliasing={{0}: (1, {})} | custom-call | flops 1048576 | bytes 10485760 | tf_op jit(solution)/shard_map/pallas_call | solution.py:39
  51.4 2.1 %collective-permute-start.6 = (f32[512,512]{1,0:T(8,128)}, f32[512,512]{1,0:T(8,128)S(1)}, u32[]{:S(2)}, u32[]{:S(2)}) collective-permute-start(f32[512,512]{1,0:T(8,128)} %get-tuple-element.49.smooth_outer), channel_id=1, source_target_pairs={{1,2},{3,4},{5,6},{7,8},{9,10},{11,12},{13,14},{15,16},{17,18},{19... | collective-permute-start | bytes 3145736 | tf_op jit(solution)/shard_map/ppermute | solution.py:795
  54.9 14.7 %shard_map.115 = (f32[2,256,256]{2,1,0:T(8,128)}, f32[2,512,512]{2,1,0:T(8,128)}, f32[2,512,512]{2,1,0:T(8,128)}) custom-call(s32[3]{0:T(128)} %pad_add_fusion.scalars, f32[4,512,512]{2,1,0:T(8,128)} %coef.6, f32[4,512,512]{2,1,0:T(8,128)} %rhs.7, f32[512,512]{1,0:T(8,128)} %collective-permute-done.coef_outer, f32[512,512]{1,0:T(8,128)} %copy-done.5, ...), custom_call_target="tpu_custom_call" | custom-call | flops 41943040 | bytes 20971520 | tf_op jit(solution)/shard_map/pallas_call | solution.py:39
  70.6 5.5 %shard_map.116.own = f32[3,256,256]{2,1,0:T(8,128)} custom-call(s32[3]{0:T(128)} %pad_add_fusion.scalars, f32[2,512,512]{2,1,0:T(8,128)} %get-tuple-element.51.known, f32[2,512,512]{2,1,0:T(8,128)} %get-tuple-element.52.factor, f32[512,512]{1,0:T(8,128)} %copy-done.7, f32[512,512]{1,0:T(8,128)} %collective-permute-done.7.halo_sibling, ...), custom_call_target="tpu_custom_call" | custom-call | flops 5242880 | bytes 8388608 | tf_op jit(solution)/shard_map/pallas_call | solution.py:39
  76.7 3.5 %collective-permute-start.10 = (f32[3,256,256]{2,1,0:T(8,128)}, f32[3,256,256]{2,1,0:T(8,128)S(1)}, u32[]{:S(2)}, u32[]{:S(2)}) collective-permute-start(f32[3,256,256]{2,1,0:T(8,128)} %shard_map.116.own), channel_id=1, source_target_pairs={{1,2},{3,4},{5,6},{7,8},{9,10},{11,12},{13,14},{15,16},{17,18},{19... | collective-permute-start | bytes 2359304 | tf_op jit(solution)/shard_map/ppermute | solution.py:795
  80.3 2.1 %collective-permute-start.11 = (f32[256,256]{1,0:T(8,128)S(1)}, f32[256,256]{1,0:T(8,128)S(1)}, u32[]{:S(2)}, u32[]{:S(2)}) collective-permute-start(f32[256,256]{1,0:T(8,128)S(1)} %slice_bitcast_fusion.1), channel_id=1, source_target_pairs={{1,2},{3,4},{5,6},{7,8},{9,10},{11,12},{13,14},{15,16},{17,18},{19... | collective-permute-start | bytes 786440 | tf_op jit(solution)/shard_map/ppermute | solution.py:795
  82.4 7.9 %collective-permute-done.10.outer = f32[3,256,256]{2,1,0:T(8,128)S(1)} collective-permute-done((f32[3,256,256]{2,1,0:T(8,128)}, f32[3,256,256]{2,1,0:T(8,128)S(1)}, u32[]{:S(2)}, u32[]{:S(2)}) %collective-permute-start.10) | collective-permute-done | bytes 786464 | tf_op jit(solution)/shard_map/ppermute | solution.py:795
  90.3 2.7 %collective-permute-done.11.rim_outer = f32[256,256]{1,0:T(8,128)S(1)} collective-permute-done((f32[256,256]{1,0:T(8,128)S(1)}, f32[256,256]{1,0:T(8,128)S(1)}, u32[]{:S(2)}, u32[]{:S(2)}) %collective-permute-start.11) | collective-permute-done | bytes 262176 | tf_op jit(solution)/shard_map/ppermute | solution.py:795
  94.2 6.6 %shard_map.117 = (f32[2,256,256]{2,1,0:T(8,128)}, f32[2,128,128]{2,1,0:T(8,128)S(1)}) custom-call(s32[3]{0:T(128)S(1)} %copy-done.4, f32[3,256,256]{2,1,0:T(8,128)S(1)} %copy-done, f32[3,256,256]{2,1,0:T(8,128)S(1)} %collective-permute-done.9.sibling, f32[3,256,256]{2,1,0:T(8,128)S(1)} %collective-permute-done.10.outer, ...), custom_call_target="tpu_custom_call" | custom-call | flops 26214400 | bytes 6291456 | tf_op jit(solution)/shard_map/pallas_call | solution.py:39
  100.8 2.6 %collective-permute-start.14 = (f32[3,128,128]{2,1,0:T(8,128)S(1)}, f32[3,128,128]{2,1,0:T(8,128)S(1)}, u32[]{:S(2)}, u32[]{:S(2)}) collective-permute-start(f32[3,128,128]{2,1,0:T(8,128)S(1)} %constant_dynamic-update-slice_fusion.own), channel_id=1, source_target_pairs={{0,2},{1,3},{2,0},{3,1},{4,6},{5,7},{6,4},{7,5},{8,10},{9,11},{10,... | collective-permute-start | bytes 589832 | tf_op jit(solution)/shard_map/ppermute | solution.py:795
  104.2 9.9 %collective-permute-start.16 = (f32[2,128,128]{2,1,0:T(8,128)S(1)}, f32[2,128,128]{2,1,0:T(8,128)S(1)}, u32[]{:S(2)}, u32[]{:S(2)}) collective-permute-start(f32[2,128,128]{2,1,0:T(8,128)S(1)} %slice.22), channel_id=1, source_target_pairs={{1,4},{3,6},{5,8},{7,10},{9,12},{11,14},{13,16},{15,18},{17,20},{1... | collective-permute-start | bytes 393224 | tf_op jit(solution)/shard_map/ppermute | solution.py:795
  114.1 2.8 %collective-permute-done.16.third = f32[2,128,128]{2,1,0:T(8,128)S(1)} collective-permute-done((f32[2,128,128]{2,1,0:T(8,128)S(1)}, f32[2,128,128]{2,1,0:T(8,128)S(1)}, u32[]{:S(2)}, u32[]{:S(2)}) %collective-permute-start.16) | collective-permute-done | bytes 131104 | tf_op jit(solution)/shard_map/ppermute | solution.py:795
  118.7 4.4 %shard_map.118 = (f32[1,128,128]{2,1,0:T(8,128)}, f32[64,32,128]{2,1,0:T(8,128)S(1)}) custom-call(s32[3]{0:T(128)S(1)} %copy-done.4, f32[3,128,128]{2,1,0:T(8,128)S(1)} %constant_dynamic-update-slice_fusion.own, f32[3,128,128]{2,1,0:T(8,128)S(1)} %collective-permute-done.13.sibling, f32[3,128,128]{2,1,0:T(8,128)S(1)} %collective-permute-done.14.even_chip, ...), custom_call_target="tpu_custom_call" | custom-call | flops 4915200 | bytes 2621440 | tf_op jit(solution)/shard_map/pallas_call | solution.py:39
  123.1 41.4 %all_to_all.5.own = f32[64,32,128]{2,1,0:T(8,128)S(1)} all-to-all(f32[64,32,128]{2,1,0:T(8,128)S(1)} %get-tuple-element.63), channel_id=1, replica_groups={{0,2,4,6,8,10,12,14,16,18,20,22,24,26,28,30,32,34,36,38,40,42,44,46,48,..., dimensions={0} | all-to-all | bytes 2097152 | tf_op jit(solution)/shard_map/all_to_all | solution.py:907
  164.5 1.7 collective-permute-start.19
  168.4 18.8 %shard_map.119 = f32[64,64,64]{2,1,0:T(8,128)} custom-call(s32[3]{0:T(128)S(1)} %copy-done.4, f32[64,32,128]{2,1,0:T(8,128)S(1)} %all_to_all.5.own, f32[64,32,128]{2,1,0:T(8,128)S(1)} %collective-permute-done.19.sibling, f32[32,64,128]{2,1,0:T(8,128)S(1)} %pad_maximum_fusion.coef), custom_call_target="tpu_custom_call" | custom-call | flops 78643200 | bytes 5242880 | tf_op jit(solution)/shard_map/pallas_call | solution.py:39
  (59 shorter events, 14.5 us)
Async XLA Ops:
  4.3 13.1 %collective-permute-start.1 = (f32[512,512]{1,0:T(8,128)}, f32[512,512]{1,0:T(8,128)S(1)}, u32[]{:S(2)}, u32[]{:S(2)}) collective-permute-start(f32[512,512]{1,0:T(8,128)} %dynamic-slice_bitcast_fusion), channel_id=1, source_target_pairs={{0,1},{1,0},{2,3},{3,2},{4,5},{5,4},{6,7},{7,6},{8,9},{9,8},{10,11... | collective-permute-start | bytes 3145736 | tf_op jit(solution)/shard_map/ppermute | solution.py:795
  5.7 16.2 %collective-permute-start = (f32[512,512]{1,0:T(8,128)S(1)}, f32[512,512]{1,0:T(8,128)}, u32[]{:S(2)}, u32[]{:S(2)}) collective-permute-start(f32[512,512]{1,0:T(8,128)S(1)} %dynamic-slice_bitcast_fusion.1), channel_id=1, source_target_pairs={{1,2},{3,4},{5,6},{7,8},{9,10},{11,12},{13,14},{15,16},{17,18},{19... | collective-permute-start | bytes 3145736 | tf_op jit(solution)/shard_map/ppermute | solution.py:795
  8.8 7.6 %collective-permute-start.2 = (f32[2,256,256]{2,1,0:T(8,128)S(1)}, f32[2,256,256]{2,1,0:T(8,128)S(1)}, u32[]{:S(2)}, u32[]{:S(2)}) collective-permute-start(f32[2,256,256]{2,1,0:T(8,128)S(1)} %copy-done.1), channel_id=1, source_target_pairs={{0,1},{1,0},{2,3},{3,2},{4,5},{5,4},{6,7},{7,6},{8,9},{9,8},{10,11... | collective-permute-start | bytes 1572872 | tf_op jit(solution)/shard_map/ppermute | solution.py:795
  26.8 18.0 %collective-permute-start.3 = (f32[512,512]{1,0:T(8,128)}, f32[512,512]{1,0:T(8,128)S(1)}, u32[]{:S(2)}, u32[]{:S(2)}) collective-permute-start(f32[512,512]{1,0:T(8,128)} %get-tuple-element.39.first_outer), channel_id=1, source_target_pairs={{1,2},{3,4},{5,6},{7,8},{9,10},{11,12},{13,14},{15,16},{17,18},{19... | collective-permute-start | bytes 3145736 | tf_op jit(solution)/shard_map/ppermute | solution.py:795
  29.9 14.9 %collective-permute-start.4 = (f32[512,512]{1,0:T(8,128)}, f32[512,512]{1,0:T(8,128)}, u32[]{:S(2)}, u32[]{:S(2)}) collective-permute-start(f32[512,512]{1,0:T(8,128)} %get-tuple-element.40.first_sibling), channel_id=1, source_target_pairs={{0,1},{1,0},{2,3},{3,2},{4,5},{5,4},{6,7},{7,6},{8,9},{9,8},{10,11... | collective-permute-start | bytes 3145736 | tf_op jit(solution)/shard_map/ppermute | solution.py:795
  41.2 13.5 %collective-permute-start.5 = (f32[3,256,256]{2,1,0:T(8,128)}, f32[3,256,256]{2,1,0:T(8,128)S(1)}, u32[]{:S(2)}, u32[]{:S(2)}) collective-permute-start(f32[3,256,256]{2,1,0:T(8,128)} %pad_maximum_fusion.1), channel_id=1, source_target_pairs={{1,2},{3,4},{5,6},{7,8},{9,10},{11,12},{13,14},{15,16},{17,18},{19... | collective-permute-start | bytes 2359304 | tf_op jit(solution)/shard_map/ppermute | solution.py:795
  51.4 18.2 %collective-permute-start.6 = (f32[512,512]{1,0:T(8,128)}, f32[512,512]{1,0:T(8,128)S(1)}, u32[]{:S(2)}, u32[]{:S(2)}) collective-permute-start(f32[512,512]{1,0:T(8,128)} %get-tuple-element.49.smooth_outer), channel_id=1, source_target_pairs={{1,2},{3,4},{5,6},{7,8},{9,10},{11,12},{13,14},{15,16},{17,18},{19... | collective-permute-start | bytes 3145736 | tf_op jit(solution)/shard_map/ppermute | solution.py:795
  53.5 16.1 %collective-permute-start.7 = (f32[512,512]{1,0:T(8,128)}, f32[512,512]{1,0:T(8,128)}, u32[]{:S(2)}, u32[]{:S(2)}) collective-permute-start(f32[512,512]{1,0:T(8,128)} %get-tuple-element.50.smooth_sibling), channel_id=1, source_target_pairs={{0,1},{1,0},{2,3},{3,2},{4,5},{5,4},{6,7},{7,6},{8,9},{9,8},{10,11... | collective-permute-start | bytes 3145736 | tf_op jit(solution)/shard_map/ppermute | solution.py:795
  54.8 14.8 %collective-permute-start.8 = (f32[256,256]{1,0:T(8,128)S(1)}, f32[256,256]{1,0:T(8,128)S(1)}, u32[]{:S(2)}, u32[]{:S(2)}) collective-permute-start(f32[256,256]{1,0:T(8,128)S(1)} %dynamic-slice_bitcast_fusion.2), channel_id=1, source_target_pairs={{0,1},{1,0},{2,3},{3,2},{4,5},{5,4},{6,7},{7,6},{8,9},{9,8},{10,11... | collective-permute-start | bytes 786440 | tf_op jit(solution)/shard_map/ppermute | solution.py:795
  70.6 22.4 %copy-start.3 = (bf16[256,128]{1,0:T(8,128)(2,1)S(1)}, bf16[256,128]{1,0:T(8,128)(2,1)}, u32[]{:S(2)}) copy-start(bf16[256,128]{1,0:T(8,128)(2,1)} %constant.44.clone.matrix) | copy-start | bytes 196612
  70.6 22.4 %copy-start.4 = (s32[3]{0:T(128)S(1)}, s32[3]{0:T(128)}, u32[]{:S(2)}) copy-start(s32[3]{0:T(128)} %pad_add_fusion.scalars) | copy-start | bytes 40
  76.2 4.1 %collective-permute-start.9 = (f32[3,256,256]{2,1,0:T(8,128)}, f32[3,256,256]{2,1,0:T(8,128)S(1)}, u32[]{:S(2)}, u32[]{:S(2)}) collective-permute-start(f32[3,256,256]{2,1,0:T(8,128)} %shard_map.116.own), channel_id=1, source_target_pairs={{0,1},{1,0},{2,3},{3,2},{4,5},{5,4},{6,7},{7,6},{8,9},{9,8},{10,11... | collective-permute-start | bytes 2359304 | tf_op jit(solution)/shard_map/ppermute | solution.py:795
  76.7 13.5 %collective-permute-start.10 = (f32[3,256,256]{2,1,0:T(8,128)}, f32[3,256,256]{2,1,0:T(8,128)S(1)}, u32[]{:S(2)}, u32[]{:S(2)}) collective-permute-start(f32[3,256,256]{2,1,0:T(8,128)} %shard_map.116.own), channel_id=1, source_target_pairs={{1,2},{3,4},{5,6},{7,8},{9,10},{11,12},{13,14},{15,16},{17,18},{19... | collective-permute-start | bytes 2359304 | tf_op jit(solution)/shard_map/ppermute | solution.py:795
  80.3 12.8 %collective-permute-start.11 = (f32[256,256]{1,0:T(8,128)S(1)}, f32[256,256]{1,0:T(8,128)S(1)}, u32[]{:S(2)}, u32[]{:S(2)}) collective-permute-start(f32[256,256]{1,0:T(8,128)S(1)} %slice_bitcast_fusion.1), channel_id=1, source_target_pairs={{1,2},{3,4},{5,6},{7,8},{9,10},{11,12},{13,14},{15,16},{17,18},{19... | collective-permute-start | bytes 786440 | tf_op jit(solution)/shard_map/ppermute | solution.py:795
  90.2 28.5 %copy-start.2 = (bf16[2,128,128]{2,1,0:T(8,128)(2,1)S(1)}, bf16[2,128,128]{2,1,0:T(8,128)(2,1)}, u32[]{:S(2)}) copy-start(bf16[2,128,128]{2,1,0:T(8,128)(2,1)} %constant.45.clone.matrices) | copy-start | bytes 196612
  90.3 2.8 %collective-permute-start.12 = (f32[256,256]{1,0:T(8,128)S(1)}, f32[256,256]{1,0:T(8,128)S(1)}, u32[]{:S(2)}, u32[]{:S(2)}) collective-permute-start(f32[256,256]{1,0:T(8,128)S(1)} %slice_bitcast_fusion), channel_id=1, source_target_pairs={{0,1},{1,0},{2,3},{3,2},{4,5},{5,4},{6,7},{7,6},{8,9},{9,8},{10,11... | collective-permute-start | bytes 786440 | tf_op jit(solution)/shard_map/ppermute | solution.py:795
  100.8 65.4 %copy-start.6 = (f32[64,64,64]{2,1,0:T(8,128)S(1)}, f32[64,64,64]{2,1,0:T(8,128)}, u32[]{:S(2)}) copy-start(f32[64,64,64]{2,1,0:T(8,128)} %param.12) | copy-start | bytes 3145732
  100.8 16.2 %collective-permute-start.14 = (f32[3,128,128]{2,1,0:T(8,128)S(1)}, f32[3,128,128]{2,1,0:T(8,128)S(1)}, u32[]{:S(2)}, u32[]{:S(2)}) collective-permute-start(f32[3,128,128]{2,1,0:T(8,128)S(1)} %constant_dynamic-update-slice_fusion.own), channel_id=1, source_target_pairs={{0,2},{1,3},{2,0},{3,1},{4,6},{5,7},{6,4},{7,5},{8,10},{9,11},{10,... | collective-permute-start | bytes 589832 | tf_op jit(solution)/shard_map/ppermute | solution.py:795
  103.5 13.5 %collective-permute-start.15 = (f32[3,128,128]{2,1,0:T(8,128)S(1)}, f32[3,128,128]{2,1,0:T(8,128)S(1)}, u32[]{:S(2)}, u32[]{:S(2)}) collective-permute-start(f32[3,128,128]{2,1,0:T(8,128)S(1)} %constant_dynamic-update-slice_fusion.own), channel_id=1, source_target_pairs={{2,4},{3,5},{6,8},{7,9},{10,12},{11,13},{14,16},{15,17},{18,20},{1... | collective-permute-start | bytes 589832 | tf_op jit(solution)/shard_map/ppermute | solution.py:795
  104.2 12.8 %collective-permute-start.16 = (f32[2,128,128]{2,1,0:T(8,128)S(1)}, f32[2,128,128]{2,1,0:T(8,128)S(1)}, u32[]{:S(2)}, u32[]{:S(2)}) collective-permute-start(f32[2,128,128]{2,1,0:T(8,128)S(1)} %slice.22), channel_id=1, source_target_pairs={{1,4},{3,6},{5,8},{7,10},{9,12},{11,14},{13,16},{15,18},{17,20},{1... | collective-permute-start | bytes 393224 | tf_op jit(solution)/shard_map/ppermute | solution.py:795
  114.1 3.5 %collective-permute-start.13 = (f32[3,128,128]{2,1,0:T(8,128)S(1)}, f32[3,128,128]{2,1,0:T(8,128)S(1)}, u32[]{:S(2)}, u32[]{:S(2)}) collective-permute-start(f32[3,128,128]{2,1,0:T(8,128)S(1)} %constant_dynamic-update-slice_fusion.own), channel_id=1, source_target_pairs={{0,1},{1,0},{2,3},{3,2},{4,5},{5,4},{6,7},{7,6},{8,9},{9,8},{10,11... | collective-permute-start | bytes 589832 | tf_op jit(solution)/shard_map/ppermute | solution.py:795
  117.0 1.4 collective-permute-start.17
  117.0 1.7 collective-permute-start.18
  164.5 4.0 %collective-permute-start.19 = (f32[64,32,128]{2,1,0:T(8,128)S(1)}, f32[64,32,128]{2,1,0:T(8,128)S(1)}, u32[]{:S(2)}, u32[]{:S(2)}) collective-permute-start(f32[64,32,128]{2,1,0:T(8,128)S(1)} %all_to_all.5.own), channel_id=1, source_target_pairs={{0,1},{1,0},{2,3},{3,2},{4,5},{5,4},{6,7},{7,6},{8,9},{9,8},{10,11... | collective-permute-start | bytes 3145736 | tf_op jit(solution)/shard_map/ppermute | solution.py:795
  (6 other events, 26.4 us)

commit v4 on v3

--- a/solution.py
+++ b/solution.py
@@ -778,7 +778,7 @@
                     older[q + 1, pl.ds(PAD + start, ROWS)] = value
             return carry
 
-        lax.fori_loop(0, half, advance, 0, unroll=UNROLL)
+        lax.fori_loop(0, half, advance, 0, unroll=2 * UNROLL)
     copy = go.start(y, solution)
     copy.wait()
 
@@ -816,13 +816,11 @@
     def side_plane(field, where):
         return lax.dynamic_index_in_dim(field, where, 0, keepdims=False)
 
-    coef_outer = side_plane(coef_zero, 3 * core)
-    rest, coef_outer = lax.optimization_barrier((coef_zero, coef_outer))
-    coef_outer = swapped(coef_outer, far)
-    coef_sibling = swapped(side_plane(rest, 3 - 3 * core), near)
+    coef_outer = swapped(side_plane(coef_zero, 3 * core), far)
+    coef_sibling = swapped(side_plane(coef_zero, 3 - 3 * core), near)
     first, partial = call(
         first_inner, [shape(2, n, n), shape(2, n, n)],
-        [tiled(4, n), vm(2, n, n), vm(2, n, n), vm(2, n, n)], 24, 40 * n * n, 12 * plane, 60,
+        [tiled(4, n), vm(2, n, n), vm(2, n, n), vm(2, n, n)], 24, 40 * n * n, 12 * plane, 32,
     )(scalars, coef_zero, rhs_fine)
     coefs_sibling = swapped(coef_one, near)
     beyond = lax.dynamic_slice_in_dim(coefs_sibling, core, 1, 0)
@@ -830,7 +828,7 @@
     partial, coefs_out = lax.optimization_barrier((partial, coefs_out))
     first_outer, first_sibling = call(
         first_rim, [shape(n, n), shape(n, n)],
-        [vm(2, n, n)] * 4, 16, 10 * n * n, 8 * plane, 60,
+        [vm(2, n, n)] * 4, 16, 10 * n * n, 8 * plane, 32,
     )(scalars, rhs_fine, partial, coef_outer, coef_sibling)
 
     halo_outer = swapped(first_outer, far)
@@ -838,13 +836,13 @@
     smooth, known, factor = call(
         smooth_inner, [shape(4, n, n), shape(2, n, n), shape(2, n, n)],
         [tiled(6, n), tiled(6, n), vm(4, n, n), vm(2, n, n), vm(2, n, n), vm(2, n, n)],
-        54, 160 * n * n, 20 * plane, 60,
+        54, 160 * n * n, 20 * plane, 62,
     )(scalars, coef_zero, rhs_fine, coef_outer, coef_sibling, first, first_outer, first_sibling)
     coefs_out, known = lax.optimization_barrier((coefs_out, known))
     coefs_outer = swapped(coefs_out, far)
     smooth_zero, smooth_outer, smooth_sibling = call(
         smooth_rim, [shape(4, n, n), shape(n, n), shape(n, n)],
-        [vm(2, n, n)] * 4, 20, 4 * n * n, 10 * plane, 60, {1: 0},
+        [vm(2, n, n)] * 4, 20, 4 * n * n, 10 * plane, 62, {1: 0},
     )(scalars, smooth, known, factor, halo_outer, halo_sibling)
 
     halo_outer = swapped(smooth_outer, far)
@@ -855,7 +853,7 @@
         residual_inner, [shape(2, n1, n1), shape(2, n, n), shape(2, n, n)],
         [tiled(6, n), tiled(6, n), vm(4, n, n), vm(2, n, n), vm(2, n, n),
          tiled(2, n), vm(2, n1, n1), pltpu.VMEM((n, n1), BF16)],
-        54, 160 * n * n, 20 * plane, 60,
+        54, 160 * n * n, 20 * plane, 62,
     )(scalars, coef_zero, rhs_fine, coef_outer, coef_sibling, smooth_zero, smooth_outer,
       smooth_sibling, matrix0)
     coefs_beyond = swapped(lax.dynamic_index_in_dim(coefs_outer, 1 - core, 0, False), near)
@@ -864,7 +862,7 @@
         residual_rim, [shape(3, n1, n1)],
         [vm(2, n, n), vm(2, n, n), vm(2, n, n), tiled(2, n), vm(4, n1, n1), vm(3, n1, n1),
          pltpu.VMEM((n, n1), BF16)],
-        15, 20 * n * n, 8 * plane, 60,
+        15, 20 * n * n, 8 * plane, 62,
     )(scalars, known, factor, halo_outer, halo_sibling, lowered, matrix0)
 
     packed_outer = swapped(packed, far)

time: 188 us -> 184 us (0.979)
  Pallas kernels: 78.6 us -> 73.7 us
  local copies, waits for them, and re-layouts: 7.05 us -> 10.7 us
  waiting for transfers between devices: 22 us -> 19.6 us
    pallas_call x9, Pallas kernels: 78.6 us -> 73.7 us  [run(): pl.pallas_call(body, out_shape=outs, in_specs=[pl.BlockSpec(memory_space=...]
    unnamed x21 -> x37, local copies, waits for them, and re-layouts: 3.09 us -> 7.23 us
    ppermute x20, waiting for transfers between devices: 22 us -> 19.6 us  [swapped(): return lax.ppermute(value, 'box', pairs)]
  transfers between devices with their start and end apart: 20 -> 20, of which waited for: 8 -> 8; matrix products, arithmetic and copies ran while one was open for 1% -> 1% of each run, Pallas kernels for 21% -> 20%
where the time goes in v4:
time: 184 us
  Pallas kernels  73.7 us (40%)
  blocking collectives  40.7 us (22%)
  starting transfers between devices  36.4 us (20%)
  waiting for transfers between devices  19.6 us (11%)
  local copies, waits for them, and re-layouts  10.7 us (6%)
    pallas_call x9, Pallas kernels, run(): pl.pallas_call(body, out_shape=outs, in_specs=[pl.BlockSpec(memory_space=...  73.7 us
    all_to_all x1, blocking collectives, local(): lax.all_to_all(copies, 'box', 0, 0, tiled=True, axis_index_groups=groups)  40.7 us
    ppermute x20, starting transfers between devices, swapped(): return lax.ppermute(value, 'box', pairs)  36.4 us
    ppermute x20, waiting for transfers between devices, swapped(): return lax.ppermute(value, 'box', pairs)  19.6 us
    unnamed x37, local copies, waits for them, and re-layouts  7.23 us
  transfers between devices with their start and end apart: 20, of which 8 were waited for; matrix products, arithmetic and copies ran while one was open for 1% of the time, Pallas kernels for 20%

profile of v4, /device:TPU:1, one launch (start us, length us, event | category | flops | bytes accessed | tf_op | source)
XLA Modules:
  0.0 183.8 jit_solution(4655255934846824121)
XLA Ops:
  0.7 3.1 %dynamic-slice_bitcast_fusion = (f32[512,512]{1,0:T(8,128)}, f32[512,512]{1,0:T(8,128)}) fusion(f32[4,512,512]{2,1,0:T(8,128)} %coef.6, s32[]{:T(128)S(6)} %select_n.23, s32[]{:T(128)S(6)} %select_n.22), kind=kLoop, calls=%fused_computation.1 | loop fusion | bytes 4194312 | tf_op jit(solution)/shard_map/jit(dynamic_index_in_dim)/squeeze | solution.py:817
  3.8 4.5 %collective-permute-start = (f32[512,512]{1,0:T(8,128)}, f32[512,512]{1,0:T(8,128)S(1)}, u32[]{:S(2)}, u32[]{:S(2)}) collective-permute-start(f32[512,512]{1,0:T(8,128)} %get-tuple-element.61), channel_id=1, source_target_pairs={{1,2},{3,4},{5,6},{7,8},{9,10},{11,12},{13,14},{15,16},{17,18},{19... | collective-permute-start | bytes 3145736 | tf_op jit(solution)/shard_map/ppermute | solution.py:795
  9.0 2.2 %copy-done = f32[4,512,512]{2,1,0:T(8,128)S(1)} copy-done((f32[4,512,512]{2,1,0:T(8,128)S(1)}, f32[4,512,512]{2,1,0:T(8,128)}, u32[]{:S(2)}) %copy-start) | copy-done | bytes 4194328
  11.2 2.2 %copy-done.2 = f32[4,512,512]{2,1,0:T(8,128)S(1)} copy-done((f32[4,512,512]{2,1,0:T(8,128)S(1)}, f32[4,512,512]{2,1,0:T(8,128)}, u32[]{:S(2)}) %copy-start.2) | copy-done | bytes 4194328
  13.3 5.2 %shard_map.111 = (f32[2,512,512]{2,1,0:T(8,128)S(1)}, f32[2,512,512]{2,1,0:T(8,128)S(1)}) custom-call(s32[3]{0:T(128)S(1)} %pad_add_fusion.scalars, f32[4,512,512]{2,1,0:T(8,128)S(1)} %copy-done.2, f32[4,512,512]{2,1,0:T(8,128)S(1)} %copy-done), custom_call_target="tpu_custom_call" | custom-call | flops 10485760 | bytes 12582912 | tf_op jit(solution)/shard_map/pallas_call | solution.py:39
  21.0 2.5 %shard_map.112 = (f32[512,512]{1,0:T(8,128)}, f32[512,512]{1,0:T(8,128)}) custom-call(s32[3]{0:T(128)S(1)} %pad_add_fusion.scalars, f32[4,512,512]{2,1,0:T(8,128)S(1)} %copy-done.1, f32[2,512,512]{2,1,0:T(8,128)S(1)} %get-tuple-element.34.partial, f32[512,512]{1,0:T(8,128)S(1)} %collective-permute-done.coef_outer, ...), custom_call_target="tpu_custom_call" | custom-call | flops 2621440 | bytes 8388608 | tf_op jit(solution)/shard_map/pallas_call | solution.py:39
  23.6 3.6 %collective-permute-start.3 = (f32[512,512]{1,0:T(8,128)}, f32[512,512]{1,0:T(8,128)}, u32[]{:S(2)}, u32[]{:S(2)}) collective-permute-start(f32[512,512]{1,0:T(8,128)} %get-tuple-element.35.first_outer), channel_id=1, source_target_pairs={{1,2},{3,4},{5,6},{7,8},{9,10},{11,12},{13,14},{15,16},{17,18},{19... | collective-permute-start | bytes 3145736 | tf_op jit(solution)/shard_map/ppermute | solution.py:795
  27.3 11.3 %shard_map.113 = (f32[4,512,512]{2,1,0:T(8,128)}, f32[2,512,512]{2,1,0:T(8,128)}, f32[2,512,512]{2,1,0:T(8,128)}) custom-call(s32[3]{0:T(128)} %copy-done.14, f32[4,512,512]{2,1,0:T(8,128)} %coef.6, f32[4,512,512]{2,1,0:T(8,128)} %rhs.7, f32[512,512]{1,0:T(8,128)} %copy-done.3, f32[512,512]{1,0:T(8,128)} %copy-done.4, f32[2,512,512]{2,1,0:T(8,128)} %copy-done.6, ...), custom_call_target="tpu_custom_call" | custom-call | flops 41943040 | bytes 20971520 | tf_op jit(solution)/shard_map/pallas_call | solution.py:39
  38.6 3.5 %collective-permute-start.5 = (f32[3,256,256]{2,1,0:T(8,128)}, f32[3,256,256]{2,1,0:T(8,128)S(1)}, u32[]{:S(2)}, u32[]{:S(2)}) collective-permute-start(f32[3,256,256]{2,1,0:T(8,128)} %pad_maximum_fusion.1), channel_id=1, source_target_pairs={{1,2},{3,4},{5,6},{7,8},{9,10},{11,12},{13,14},{15,16},{17,18},{19... | collective-permute-start | bytes 2359304 | tf_op jit(solution)/shard_map/ppermute | solution.py:795
  42.2 5.7 %shard_map.114 = (f32[4,512,512]{2,1,0:T(8,128)}, f32[512,512]{1,0:T(8,128)}, f32[512,512]{1,0:T(8,128)}) custom-call(s32[3]{0:T(128)} %copy-done.14, f32[4,512,512]{2,1,0:T(8,128)} %get-tuple-element.37.started, f32[2,512,512]{2,1,0:T(8,128)} %get-tuple-element.40.known, f32[2,512,512]{2,1,0:T(8,128)} %get-tuple-element.41.factor, ...), custom_call_target="tpu_custom_call", output_to_operand_aliasing={{0}: (1, {})} | custom-call | flops 1048576 | bytes 10485760 | tf_op jit(solution)/shard_map/pallas_call | solution.py:39
  50.0 2.1 %collective-permute-done.5.coef_outer = f32[3,256,256]{2,1,0:T(8,128)S(1)} collective-permute-done((f32[3,256,256]{2,1,0:T(8,128)}, f32[3,256,256]{2,1,0:T(8,128)S(1)}, u32[]{:S(2)}, u32[]{:S(2)}) %collective-permute-start.5) | collective-permute-done | bytes 786464 | tf_op jit(solution)/shard_map/ppermute | solution.py:795
  52.3 14.7 %shard_map.115 = (f32[2,256,256]{2,1,0:T(8,128)}, f32[2,512,512]{2,1,0:T(8,128)}, f32[2,512,512]{2,1,0:T(8,128)}) custom-call(s32[3]{0:T(128)} %copy-done.14, f32[4,512,512]{2,1,0:T(8,128)} %coef.6, f32[4,512,512]{2,1,0:T(8,128)} %rhs.7, f32[512,512]{1,0:T(8,128)} %copy-done.3, f32[512,512]{1,0:T(8,128)} %copy-done.4, ...), custom_call_target="tpu_custom_call" | custom-call | flops 41943040 | bytes 20971520 | tf_op jit(solution)/shard_map/pallas_call | solution.py:39
  67.8 5.5 %shard_map.116.own = f32[3,256,256]{2,1,0:T(8,128)} custom-call(s32[3]{0:T(128)} %copy-done.14, f32[2,512,512]{2,1,0:T(8,128)} %get-tuple-element.47.known, f32[2,512,512]{2,1,0:T(8,128)} %get-tuple-element.48.factor, f32[512,512]{1,0:T(8,128)} %collective-permute-done.6.halo_outer, f32[512,512]{1,0:T(8,128)} %collective-permute-done.7.halo_sibling, ...), custom_call_target="tpu_custom_call" | custom-call | flops 5242880 | bytes 8388608 | tf_op jit(solution)/shard_map/pallas_call | solution.py:39
  73.9 3.5 %collective-permute-start.10 = (f32[3,256,256]{2,1,0:T(8,128)}, f32[3,256,256]{2,1,0:T(8,128)S(1)}, u32[]{:S(2)}, u32[]{:S(2)}) collective-permute-start(f32[3,256,256]{2,1,0:T(8,128)} %shard_map.116.own), channel_id=1, source_target_pairs={{1,2},{3,4},{5,6},{7,8},{9,10},{11,12},{13,14},{15,16},{17,18},{19... | collective-permute-start | bytes 2359304 | tf_op jit(solution)/shard_map/ppermute | solution.py:795
  77.4 2.4 %collective-permute-start.11 = (f32[256,256]{1,0:T(8,128)S(1)}, f32[256,256]{1,0:T(8,128)S(1)}, u32[]{:S(2)}, u32[]{:S(2)}) collective-permute-start(f32[256,256]{1,0:T(8,128)S(1)} %slice_bitcast_fusion.1), channel_id=1, source_target_pairs={{1,2},{3,4},{5,6},{7,8},{9,10},{11,12},{13,14},{15,16},{17,18},{19... | collective-permute-start | bytes 786440 | tf_op jit(solution)/shard_map/ppermute | solution.py:795
  79.8 7.6 %collective-permute-done.10.outer = f32[3,256,256]{2,1,0:T(8,128)S(1)} collective-permute-done((f32[3,256,256]{2,1,0:T(8,128)}, f32[3,256,256]{2,1,0:T(8,128)S(1)}, u32[]{:S(2)}, u32[]{:S(2)}) %collective-permute-start.10) | collective-permute-done | bytes 786464 | tf_op jit(solution)/shard_map/ppermute | solution.py:795
  87.5 2.7 %collective-permute-done.11.rim_outer = f32[256,256]{1,0:T(8,128)S(1)} collective-permute-done((f32[256,256]{1,0:T(8,128)S(1)}, f32[256,256]{1,0:T(8,128)S(1)}, u32[]{:S(2)}, u32[]{:S(2)}) %collective-permute-start.11) | collective-permute-done | bytes 262176 | tf_op jit(solution)/shard_map/ppermute | solution.py:795
  92.3 6.8 %shard_map.117 = (f32[2,256,256]{2,1,0:T(8,128)}, f32[2,128,128]{2,1,0:T(8,128)S(1)}) custom-call(s32[3]{0:T(128)S(1)} %copy-done.15, f32[3,256,256]{2,1,0:T(8,128)S(1)} %copy-done.5, f32[3,256,256]{2,1,0:T(8,128)S(1)} %collective-permute-done.9.sibling, f32[3,256,256]{2,1,0:T(8,128)S(1)} %collective-permute-done.10.outer, ...), custom_call_target="tpu_custom_call" | custom-call | flops 26214400 | bytes 6291456 | tf_op jit(solution)/shard_map/pallas_call | solution.py:39
  99.1 2.7 %collective-permute-start.14 = (f32[3,128,128]{2,1,0:T(8,128)S(1)}, f32[3,128,128]{2,1,0:T(8,128)S(1)}, u32[]{:S(2)}, u32[]{:S(2)}) collective-permute-start(f32[3,128,128]{2,1,0:T(8,128)S(1)} %constant_dynamic-update-slice_fusion.own), channel_id=1, source_target_pairs={{0,2},{1,3},{2,0},{3,1},{4,6},{5,7},{6,4},{7,5},{8,10},{9,11},{10,... | collective-permute-start | bytes 589832 | tf_op jit(solution)/shard_map/ppermute | solution.py:795
  102.6 9.6 %collective-permute-start.16 = (f32[2,128,128]{2,1,0:T(8,128)S(1)}, f32[2,128,128]{2,1,0:T(8,128)S(1)}, u32[]{:S(2)}, u32[]{:S(2)}) collective-permute-start(f32[2,128,128]{2,1,0:T(8,128)S(1)} %slice.22), channel_id=1, source_target_pairs={{1,4},{3,6},{5,8},{7,10},{9,12},{11,14},{13,16},{15,18},{17,20},{1... | collective-permute-start | bytes 393224 | tf_op jit(solution)/shard_map/ppermute | solution.py:795
  112.3 3.0 %collective-permute-done.16.third = f32[2,128,128]{2,1,0:T(8,128)S(1)} collective-permute-done((f32[2,128,128]{2,1,0:T(8,128)S(1)}, f32[2,128,128]{2,1,0:T(8,128)S(1)}, u32[]{:S(2)}, u32[]{:S(2)}) %collective-permute-start.16) | collective-permute-done | bytes 131104 | tf_op jit(solution)/shard_map/ppermute | solution.py:795
  117.0 4.4 %shard_map.118 = (f32[1,128,128]{2,1,0:T(8,128)}, f32[64,32,128]{2,1,0:T(8,128)S(1)}) custom-call(s32[3]{0:T(128)S(1)} %copy-done.15, f32[3,128,128]{2,1,0:T(8,128)S(1)} %constant_dynamic-update-slice_fusion.own, f32[3,128,128]{2,1,0:T(8,128)S(1)} %collective-permute-done.13.sibling, f32[3,128,128]{2,1,0:T(8,128)S(1)} %collective-permute-done.14.even_chip, ...), custom_call_target="tpu_custom_call" | custom-call | flops 4915200 | bytes 2621440 | tf_op jit(solution)/shard_map/pallas_call | solution.py:39
  121.4 40.7 %all_to_all.5.own = f32[64,32,128]{2,1,0:T(8,128)S(1)} all-to-all(f32[64,32,128]{2,1,0:T(8,128)S(1)} %get-tuple-element.59), channel_id=1, replica_groups={{0,2,4,6,8,10,12,14,16,18,20,22,24,26,28,30,32,34,36,38,40,42,44,46,48,..., dimensions={0} | all-to-all | bytes 2097152 | tf_op jit(solution)/shard_map/all_to_all | solution.py:905
  166.1 17.6 %shard_map.119 = f32[64,64,64]{2,1,0:T(8,128)} custom-call(s32[3]{0:T(128)S(1)} %copy-done.15, f32[64,32,128]{2,1,0:T(8,128)S(1)} %all_to_all.5.own, f32[64,32,128]{2,1,0:T(8,128)S(1)} %collective-permute-done.19.sibling, f32[32,64,128]{2,1,0:T(8,128)S(1)} %pad_maximum_fusion.coef), custom_call_target="tpu_custom_call" | custom-call | flops 78643200 | bytes 5242880 | tf_op jit(solution)/shard_map/pallas_call | solution.py:39
  (74 shorter events, 15.4 us)
Async XLA Ops:
  3.8 17.2 %collective-permute-start = (f32[512,512]{1,0:T(8,128)}, f32[512,512]{1,0:T(8,128)S(1)}, u32[]{:S(2)}, u32[]{:S(2)}) collective-permute-start(f32[512,512]{1,0:T(8,128)} %get-tuple-element.61), channel_id=1, source_target_pairs={{1,2},{3,4},{5,6},{7,8},{9,10},{11,12},{13,14},{15,16},{17,18},{19... | collective-permute-start | bytes 3145736 | tf_op jit(solution)/shard_map/ppermute | solution.py:795
  8.3 12.7 %collective-permute-start.1 = (f32[512,512]{1,0:T(8,128)}, f32[512,512]{1,0:T(8,128)S(1)}, u32[]{:S(2)}, u32[]{:S(2)}) collective-permute-start(f32[512,512]{1,0:T(8,128)} %get-tuple-element.60), channel_id=1, source_target_pairs={{0,1},{1,0},{2,3},{3,2},{4,5},{5,4},{6,7},{7,6},{8,9},{9,8},{10,11... | collective-permute-start | bytes 3145736 | tf_op jit(solution)/shard_map/ppermute | solution.py:795
  8.4 10.2 %collective-permute-start.2 = (f32[2,256,256]{2,1,0:T(8,128)S(1)}, f32[2,256,256]{2,1,0:T(8,128)S(1)}, u32[]{:S(2)}, u32[]{:S(2)}) collective-permute-start(f32[2,256,256]{2,1,0:T(8,128)S(1)} %copy-done.7), channel_id=1, source_target_pairs={{0,1},{1,0},{2,3},{3,2},{4,5},{5,4},{6,7},{7,6},{8,9},{9,8},{10,11... | collective-permute-start | bytes 1572872 | tf_op jit(solution)/shard_map/ppermute | solution.py:795
  23.6 18.5 %collective-permute-start.3 = (f32[512,512]{1,0:T(8,128)}, f32[512,512]{1,0:T(8,128)}, u32[]{:S(2)}, u32[]{:S(2)}) collective-permute-start(f32[512,512]{1,0:T(8,128)} %get-tuple-element.35.first_outer), channel_id=1, source_target_pairs={{1,2},{3,4},{5,6},{7,8},{9,10},{11,12},{13,14},{15,16},{17,18},{19... | collective-permute-start | bytes 3145736 | tf_op jit(solution)/shard_map/ppermute | solution.py:795
  27.2 14.9 %collective-permute-start.4 = (f32[512,512]{1,0:T(8,128)}, f32[512,512]{1,0:T(8,128)}, u32[]{:S(2)}, u32[]{:S(2)}) collective-permute-start(f32[512,512]{1,0:T(8,128)} %get-tuple-element.36.first_sibling), channel_id=1, source_target_pairs={{0,1},{1,0},{2,3},{3,2},{4,5},{5,4},{6,7},{7,6},{8,9},{9,8},{10,11... | collective-permute-start | bytes 3145736 | tf_op jit(solution)/shard_map/ppermute | solution.py:795
  38.6 13.5 %collective-permute-start.5 = (f32[3,256,256]{2,1,0:T(8,128)}, f32[3,256,256]{2,1,0:T(8,128)S(1)}, u32[]{:S(2)}, u32[]{:S(2)}) collective-permute-start(f32[3,256,256]{2,1,0:T(8,128)} %pad_maximum_fusion.1), channel_id=1, source_target_pairs={{1,2},{3,4},{5,6},{7,8},{9,10},{11,12},{13,14},{15,16},{17,18},{19... | collective-permute-start | bytes 2359304 | tf_op jit(solution)/shard_map/ppermute | solution.py:795
  47.9 19.9 %collective-permute-start.6 = (f32[512,512]{1,0:T(8,128)}, f32[512,512]{1,0:T(8,128)}, u32[]{:S(2)}, u32[]{:S(2)}) collective-permute-start(f32[512,512]{1,0:T(8,128)} %get-tuple-element.45.smooth_outer), channel_id=1, source_target_pairs={{1,2},{3,4},{5,6},{7,8},{9,10},{11,12},{13,14},{15,16},{17,18},{19... | collective-permute-start | bytes 3145736 | tf_op jit(solution)/shard_map/ppermute | solution.py:795
  49.9 17.8 %collective-permute-start.7 = (f32[512,512]{1,0:T(8,128)}, f32[512,512]{1,0:T(8,128)}, u32[]{:S(2)}, u32[]{:S(2)}) collective-permute-start(f32[512,512]{1,0:T(8,128)} %get-tuple-element.46.smooth_sibling), channel_id=1, source_target_pairs={{0,1},{1,0},{2,3},{3,2},{4,5},{5,4},{6,7},{7,6},{8,9},{9,8},{10,11... | collective-permute-start | bytes 3145736 | tf_op jit(solution)/shard_map/ppermute | solution.py:795
  52.2 14.8 %collective-permute-start.8 = (f32[256,256]{1,0:T(8,128)S(1)}, f32[256,256]{1,0:T(8,128)S(1)}, u32[]{:S(2)}, u32[]{:S(2)}) collective-permute-start(f32[256,256]{1,0:T(8,128)S(1)} %dynamic-slice_bitcast_fusion.2), channel_id=1, source_target_pairs={{0,1},{1,0},{2,3},{3,2},{4,5},{5,4},{6,7},{7,6},{8,9},{9,8},{10,11... | collective-permute-start | bytes 786440 | tf_op jit(solution)/shard_map/ppermute | solution.py:795
  67.7 22.5 %copy-start.9 = (f32[2,256,256]{2,1,0:T(8,128)S(1)}, f32[2,256,256]{2,1,0:T(8,128)}, u32[]{:S(2)}) copy-start(f32[2,256,256]{2,1,0:T(8,128)} %copy-done.8) | copy-start | bytes 1572868
  67.7 22.5 %copy-start.13 = (bf16[256,128]{1,0:T(8,128)(2,1)S(1)}, bf16[256,128]{1,0:T(8,128)(2,1)}, u32[]{:S(2)}) copy-start(bf16[256,128]{1,0:T(8,128)(2,1)} %constant.44.clone.matrix) | copy-start | bytes 196612
  73.3 4.1 %collective-permute-start.9 = (f32[3,256,256]{2,1,0:T(8,128)}, f32[3,256,256]{2,1,0:T(8,128)S(1)}, u32[]{:S(2)}, u32[]{:S(2)}) collective-permute-start(f32[3,256,256]{2,1,0:T(8,128)} %shard_map.116.own), channel_id=1, source_target_pairs={{0,1},{1,0},{2,3},{3,2},{4,5},{5,4},{6,7},{7,6},{8,9},{9,8},{10,11... | collective-permute-start | bytes 2359304 | tf_op jit(solution)/shard_map/ppermute | solution.py:795
  73.9 13.5 %collective-permute-start.10 = (f32[3,256,256]{2,1,0:T(8,128)}, f32[3,256,256]{2,1,0:T(8,128)S(1)}, u32[]{:S(2)}, u32[]{:S(2)}) collective-permute-start(f32[3,256,256]{2,1,0:T(8,128)} %shard_map.116.own), channel_id=1, source_target_pairs={{1,2},{3,4},{5,6},{7,8},{9,10},{11,12},{13,14},{15,16},{17,18},{19... | collective-permute-start | bytes 2359304 | tf_op jit(solution)/shard_map/ppermute | solution.py:795
  77.4 12.8 %collective-permute-start.11 = (f32[256,256]{1,0:T(8,128)S(1)}, f32[256,256]{1,0:T(8,128)S(1)}, u32[]{:S(2)}, u32[]{:S(2)}) collective-permute-start(f32[256,256]{1,0:T(8,128)S(1)} %slice_bitcast_fusion.1), channel_id=1, source_target_pairs={{1,2},{3,4},{5,6},{7,8},{9,10},{11,12},{13,14},{15,16},{17,18},{19... | collective-permute-start | bytes 786440 | tf_op jit(solution)/shard_map/ppermute | solution.py:795
  87.4 29.6 %copy-start.12 = (bf16[2,128,128]{2,1,0:T(8,128)(2,1)S(1)}, bf16[2,128,128]{2,1,0:T(8,128)(2,1)}, u32[]{:S(2)}) copy-start(bf16[2,128,128]{2,1,0:T(8,128)(2,1)} %constant.45.clone.matrices) | copy-start | bytes 196612
  87.4 2.8 %collective-permute-start.12 = (f32[256,256]{1,0:T(8,128)S(1)}, f32[256,256]{1,0:T(8,128)S(1)}, u32[]{:S(2)}, u32[]{:S(2)}) collective-permute-start(f32[256,256]{1,0:T(8,128)S(1)} %slice_bitcast_fusion), channel_id=1, source_target_pairs={{0,1},{1,0},{2,3},{3,2},{4,5},{5,4},{6,7},{7,6},{8,9},{9,8},{10,11... | collective-permute-start | bytes 786440 | tf_op jit(solution)/shard_map/ppermute | solution.py:795
  99.1 64.7 %copy-start.16 = (f32[64,64,64]{2,1,0:T(8,128)S(1)}, f32[64,64,64]{2,1,0:T(8,128)}, u32[]{:S(2)}) copy-start(f32[64,64,64]{2,1,0:T(8,128)} %param.12) | copy-start | bytes 3145732
  99.1 16.2 %collective-permute-start.14 = (f32[3,128,128]{2,1,0:T(8,128)S(1)}, f32[3,128,128]{2,1,0:T(8,128)S(1)}, u32[]{:S(2)}, u32[]{:S(2)}) collective-permute-start(f32[3,128,128]{2,1,0:T(8,128)S(1)} %constant_dynamic-update-slice_fusion.own), channel_id=1, source_target_pairs={{0,2},{1,3},{2,0},{3,1},{4,6},{5,7},{6,4},{7,5},{8,10},{9,11},{10,... | collective-permute-start | bytes 589832 | tf_op jit(solution)/shard_map/ppermute | solution.py:795
  101.9 13.4 %collective-permute-start.15 = (f32[3,128,128]{2,1,0:T(8,128)S(1)}, f32[3,128,128]{2,1,0:T(8,128)S(1)}, u32[]{:S(2)}, u32[]{:S(2)}) collective-permute-start(f32[3,128,128]{2,1,0:T(8,128)S(1)} %constant_dynamic-update-slice_fusion.own), channel_id=1, source_target_pairs={{2,4},{3,5},{6,8},{7,9},{10,12},{11,13},{14,16},{15,17},{18,20},{1... | collective-permute-start | bytes 589832 | tf_op jit(solution)/shard_map/ppermute | solution.py:795
  102.6 12.7 %collective-permute-start.16 = (f32[2,128,128]{2,1,0:T(8,128)S(1)}, f32[2,128,128]{2,1,0:T(8,128)S(1)}, u32[]{:S(2)}, u32[]{:S(2)}) collective-permute-start(f32[2,128,128]{2,1,0:T(8,128)S(1)} %slice.22), channel_id=1, source_target_pairs={{1,4},{3,6},{5,8},{7,10},{9,12},{11,14},{13,16},{15,18},{17,20},{1... | collective-permute-start | bytes 393224 | tf_op jit(solution)/shard_map/ppermute | solution.py:795
  112.2 3.6 %collective-permute-start.13 = (f32[3,128,128]{2,1,0:T(8,128)S(1)}, f32[3,128,128]{2,1,0:T(8,128)S(1)}, u32[]{:S(2)}, u32[]{:S(2)}) collective-permute-start(f32[3,128,128]{2,1,0:T(8,128)S(1)} %constant_dynamic-update-slice_fusion.own), channel_id=1, source_target_pairs={{0,1},{1,0},{2,3},{3,2},{4,5},{5,4},{6,7},{7,6},{8,9},{9,8},{10,11... | collective-permute-start | bytes 589832 | tf_op jit(solution)/shard_map/ppermute | solution.py:795
  115.3 1.4 collective-permute-start.17
  115.3 1.7 collective-permute-start.18
  162.1 4.0 %collective-permute-start.19 = (f32[64,32,128]{2,1,0:T(8,128)S(1)}, f32[64,32,128]{2,1,0:T(8,128)S(1)}, u32[]{:S(2)}, u32[]{:S(2)}) collective-permute-start(f32[64,32,128]{2,1,0:T(8,128)S(1)} %all_to_all.5.own), channel_id=1, source_target_pairs={{0,1},{1,0},{2,3},{3,2},{4,5},{5,4},{6,7},{7,6},{8,9},{9,8},{10,11... | collective-permute-start | bytes 3145736 | tf_op jit(solution)/shard_map/ppermute | solution.py:795
  (14 other events, 79.5 us)
